TPU v7x, 32 devices: a whole 2x2x4 slice. The times are simulated.
32 devices in a mesh: gx: 4 (over x, core), gy: 8 (over z, y).
Axes of the slice: x: 2, y: 2, z: 4, core: 2. Of those that a mesh axis runs over, the one named last changes fastest.
Arguments:
- patches: bfloat16 [4096, 1664], P('gy', 'gx'), may hold values from -6 to 6
- segment_ids: int32 [4096], P('gy'), may hold values from 0 to 31, as said below
- image_requests: int32 [32], replicated, may hold values from 0 to 7
- merge_index: int32 [1024, 4], P('gy'), may hold values from 0 to 4095, as said below
- qkv_weight: bfloat16 [1664, 3, 1664], P('gy', None, 'gx'), may hold values from -128 to 128
- out_weight: bfloat16 [1664, 1664], P('gx', 'gy'), may hold values from -0.15625 to 0.15625
- up_weight: bfloat16 [1664, 8192], P('gy', 'gx'), may hold values from -0.15625 to 0.15625
- down_weight: bfloat16 [8192, 1664], P('gx', 'gy'), may hold values from -0.0625 to 0.0625
- merge_weight: bfloat16 [6656, 4096], P('gy', 'gx'), may hold values from -0.078125 to 0.078125
Outputs:
- merged: bfloat16 [1024, 4096], P('gy', 'gx')
- request_norms: float32 [8], replicated
- top_logit: float32 [], replicated
Inputs may be any that keep to these rules, and one draw needn't show every extreme that they name: `segment_ids`: segment ids never fall along the tokens; the 512 tokens of block b (tokens b * 512 onward) hold exactly the images b * 4 to (b + 1) * 4 - 1, each a multiple of 4 tokens long. `merge_index`: every token stands in exactly one merged row; the four tokens of merged row m belong to one image, in the block of 512 tokens that holds token 4 * m.
All inputs are finite; a program needn't handle non-finite values.
Results may differ from a plain program's by a relative error of at most 0.011.
Values may be sent and summed in bfloat16 or wider, within the bound.
A program may use at most 128 MiB of HBM per device.

v0:
```python
import math

import jax
import jax.numpy as jnp
from jax import lax
from jax.sharding import PartitionSpec as P

HEAD = 104
IMG_GRP = 4


def layer_norm(values):
    center = jnp.mean(values, axis=-1, keepdims=True)
    square = jnp.mean(values * values, axis=-1, keepdims=True)
    return (values - center) * lax.rsqrt(square - center * center + 1e-06)


def add_columns(left, piece):
    flat = piece.reshape(piece.shape[0], -1)
    return jnp.dot(left, flat, preferred_element_type=jnp.float32)


def finish_sum(head_partial, stream_full, feat_share):
    own_index = lax.axis_index("gx")
    summed = lax.psum(head_partial, "gx")
    new_full = (stream_full.astype(jnp.float32) + summed).astype(jnp.bfloat16)
    new_share = lax.dynamic_slice_in_dim(new_full, own_index * feat_share, feat_share, 1)
    return (new_full, new_share)


def per_device(
    patches,
    segment_ids,
    image_requests,
    merge_index,
    qkv_weight,
    out_weight,
    up_weight,
    down_weight,
    merge_weight,
):
    tok_rows = patches.shape[0]
    feat_share = patches.shape[1]
    group_index = lax.axis_index("gy")
    stream_full = lax.all_gather(patches, "gx", axis=1, tiled=True)
    normed = layer_norm(stream_full.astype(jnp.float32)).astype(jnp.bfloat16)
    head_share = qkv_weight.shape[2]
    local_heads = head_share // HEAD
    projected = add_columns(normed, lax.all_gather(qkv_weight, "gy", axis=0, tiled=True))
    projected = projected.astype(jnp.bfloat16).reshape(tok_rows, 3, local_heads, HEAD)
    scores = jnp.einsum(
        "qhe,khe->hqk", projected[:, 0], projected[:, 1], preferred_element_type=jnp.float32
    ) / math.sqrt(HEAD)
    allowed = segment_ids[:, None] == segment_ids[None, :]
    scores = jnp.where(allowed[None], scores, -1e30)
    probs = jax.nn.softmax(scores, axis=-1).astype(jnp.bfloat16)
    mixed = jnp.einsum("hqk,khe->qhe", probs, projected[:, 2], preferred_element_type=jnp.float32)
    mixed = mixed.astype(jnp.bfloat16).reshape(tok_rows, head_share)
    head_partial = jnp.dot(
        mixed,
        lax.all_gather(out_weight, "gy", axis=1, tiled=True),
        preferred_element_type=jnp.float32,
    )
    stream_full, stream_share = finish_sum(head_partial, stream_full, feat_share)
    normed_two = layer_norm(stream_full.astype(jnp.float32)).astype(jnp.bfloat16)
    hidden = add_columns(normed_two, lax.all_gather(up_weight, "gy", axis=0, tiled=True))
    hidden = jax.nn.gelu(hidden, approximate=False).astype(jnp.bfloat16)
    unit_partial = jnp.dot(
        hidden,
        lax.all_gather(down_weight, "gy", axis=1, tiled=True),
        preferred_element_type=jnp.float32,
    )
    final_full, final_share = finish_sum(unit_partial, stream_full, feat_share)
    row_squares = jnp.sum(jnp.square(final_share.astype(jnp.float32)), axis=1)
    image_ids = group_index * IMG_GRP + jnp.arange(IMG_GRP, dtype=jnp.int32)
    member = segment_ids[:, None] == image_ids[None, :]
    image_sq = jnp.sum(jnp.where(member, row_squares[:, None], 0.0), axis=0)
    local_requests = lax.dynamic_slice_in_dim(image_requests, group_index * IMG_GRP, IMG_GRP)
    request_count = image_requests.shape[0] // 4
    owner = local_requests[:, None] == jnp.arange(request_count, dtype=jnp.int32)[None, :]
    request_part = jnp.sum(jnp.where(owner, image_sq[:, None], 0.0), axis=0)
    local_index = (merge_index - group_index * tok_rows).reshape(-1)
    joined = jnp.take(final_full, local_index, axis=0).reshape(
        merge_index.shape[0], 4 * final_full.shape[1]
    )
    logits = add_columns(joined, lax.all_gather(merge_weight, "gy", axis=0, tiled=True))
    local_top = jnp.max(logits)
    request_sq = lax.psum(request_part, ("gx", "gy"))
    top_logit = lax.pmax(local_top, ("gx", "gy"))
    return (logits.astype(jnp.bfloat16), jnp.sqrt(request_sq), top_logit)


def solution(mesh):
    in_specs = (
        P("gy", "gx"),
        P("gy"),
        P(),
        P("gy", None),
        P("gy", None, "gx"),
        P("gx", "gy"),
        P("gy", "gx"),
        P("gx", "gy"),
        P("gy", "gx"),
    )
    out_specs = (P("gy", "gx"), P(), P())
    return jax.shard_map(
        per_device, mesh=mesh, in_specs=in_specs, out_specs=out_specs, check_vma=False
    )
```

profile of v0, /device:TPU:0, one launch (start us, length us, event | category | flops | bytes accessed | tf_op | source)
XLA Modules:
  0.0 815.3 jit_solution(6109742581719975203)
XLA Ops:
  7.2 0.0 all-gather.7.cloned.1.call-start
  7.2 0.7 all-gather.7.cloned.1.call-update
  7.9 0.0 all-gather.9.cloned.1.call-start
  7.9 2.6 copy.29
  10.5 0.0 all-gather.9.cloned.1.call-update
  10.6 0.0 all-gather.11.cloned.1.call-start
  10.6 1.7 copy.32
  12.4 0.0 all-gather.11.cloned.1.call-update
  12.4 0.0 all-reduce.3.cloned.1.call-start
  12.4 1.0 broadcast_compare_fusion
  13.4 19.3 %all-gather.7.cloned.1.call-done = bf16[512,1664]{0,1:T(8,128)(2,1)} async-done(((bf16[512,416]{0,1:T(8,128)(2,1)}), bf16[512,1664]{0,1:T(8,128)(2,1)}) %all-gather.7.cloned.1.call-update) | async-done | bytes 1703952 | tf_op jit(solution)/shard_map/all_gather | solution.py:45
  32.7 2.7 copy.28
  35.4 0.6 convert_reduce_fusion.1
  36.1 104.4 %all-gather.9.cloned.1.call-done = bf16[1664,3,416]{2,1,0:T(4,128)(2,1)} async-done(((bf16[208,3,416]{2,1,0:T(4,128)(2,1)}), bf16[1664,3,416]{2,1,0:T(4,128)(2,1)}) %all-gather.9.cloned.1.call-update) | async-done | bytes 4153360 | tf_op jit(solution)/shard_map/all_gather | solution.py:49
  140.5 11.3 %copy.30 = bf16[1664,3,416]{0,2,1:T(8,128)(2,1)} copy(bf16[1664,3,416]{2,1,0:T(4,128)(2,1)} %all-gather.9.cloned.1.call-done) | data formatting | bytes 8306688 | tf_op jit(solution)/shard_map/all_gather | solution.py:49
  151.7 4.8 convolution_convert_fusion
  156.6 0.7 fusion.73
  157.3 2.1 fusion.109
  159.5 0.5 fusion.71
  160.0 26.7 %all-gather.11.cloned.1.call-done = bf16[416,1664]{0,1:T(8,128)(2,1)} async-done(((bf16[416,208]{0,1:T(8,128)(2,1)}), bf16[416,1664]{0,1:T(8,128)(2,1)}) %all-gather.11.cloned.1.call-update) | async-done | bytes 1384464 | tf_op jit(solution)/shard_map/all_gather | solution.py:61
  186.7 4.4 fusion.110
  191.1 0.0 all-reduce.3.cloned.1.call-update
  191.1 0.0 all-gather.13.cloned.1.call-start
  191.1 0.5 all-gather.13.cloned.1.call-update
  191.7 0.0 all-gather.15.cloned.1.call-start
  191.7 0.5 all-gather.15.cloned.1.call-update
  192.3 0.2 all-reduce.5.cloned.1.call-start
  192.5 70.4 %all-reduce.3.cloned.1.call-done = f32[512,1664]{1,0:T(8,128)} async-done(((f32[512,1664]{1,0:T(8,128)}), f32[512,1664]{1,0:T(8,128)}) %all-reduce.3.cloned.1.call-update) | async-done | bytes 3407888 | tf_op jit(solution)/shard_map/psum | solution.py:25
  262.9 2.7 convert_reduce_fusion
  265.6 105.1 %all-gather.13.cloned.1.call-done = bf16[1664,2048]{1,0:T(8,128)(2,1)} async-done(((bf16[208,2048]{1,0:T(8,128)(2,1)}), bf16[1664,2048]{1,0:T(8,128)(2,1)}) %all-gather.13.cloned.1.call-update) | async-done | bytes 6815760 | tf_op jit(solution)/shard_map/all_gather | solution.py:66
  370.6 105.8 %all-gather.15.cloned.1.call-done = bf16[2048,1664]{0,1:T(8,128)(2,1)} async-done(((bf16[2048,208]{0,1:T(8,128)(2,1)}), bf16[2048,1664]{0,1:T(8,128)(2,1)}) %all-gather.15.cloned.1.call-update) | async-done | bytes 6815760 | tf_op jit(solution)/shard_map/all_gather | solution.py:70
  476.5 21.5 %fusion.20 = f32[512,1664]{1,0:T(8,128)} fusion(bf16[2048,1664]{0,1:T(8,128)(2,1)} %all-gather.15.cloned.1.call-done, bf16[1664,2048]{1,0:T(8,128)(2,1)} %all-gather.13.cloned.1.call-done, bf16[512,1664]{1,0:T(8,128)(2,1)S(1)} %get-tuple-element.7, f32[512]{0:T(512)S(1)} %get-tuple-element.13, f32[512]{0:T(512)S(1)} %get-tuple-element.12), kind=kOutput, calls=%fused_computation.42 | convolution fusion | flops 7050887168 | bytes 18747392 | tf_op jit(solution)/shard_map/dot_general | solution.py:68
  497.9 0.0 copy-start.1
  497.9 0.0 copy-start.2
  497.9 0.0 all-reduce.5.cloned.1.call-update
  498.0 0.0 all-gather.17.cloned.1.call-start
  498.0 0.7 all-gather.17.cloned.1.call-update
  498.7 0.0 copy-start
  498.7 0.0 copy-done.1
  498.8 0.1 copy.33
  498.9 0.1 reshape.131
  499.0 0.1 copy.27
  499.1 0.0 copy-done.2
  499.1 0.1 dynamic_slice.6
  499.2 69.8 %all-reduce.5.cloned.1.call-done = f32[512,1664]{1,0:T(8,128)} async-done(((f32[512,1664]{1,0:T(8,128)}), f32[512,1664]{1,0:T(8,128)}) %all-reduce.5.cloned.1.call-update) | async-done | bytes 3407888 | tf_op jit(solution)/shard_map/psum | solution.py:25
  569.0 2.2 fusion.18
  571.2 0.4 multiply_reduce_fusion
  571.6 0.0 copy-done
  571.6 0.2 select_reduce_fusion
  571.8 0.1 select_reduce_fusion.1
  571.9 0.5 broadcast_in_dim.63
  572.4 1.3 copy.35
  573.8 42.4 %psum.23 = f32[8]{0:T(128)S(1)} all-reduce(f32[8]{0:T(128)S(1)} %select_reduce_fusion.1), channel_id=1, replica_groups=mesh['gx'=4,'gy'=8] {'gx','gy'}, use_global_device_ids=true, to_apply=%region_11.12 | all-reduce | flops 8 | bytes 64 | tf_op jit(solution)/shard_map/psum | solution.py:88
  616.2 2.3 gather_fusion
  618.5 1.2 gather.7
  619.7 0.5 sqrt.3
  620.2 141.2 %all-gather.17.cloned.1.call-done = bf16[6656,1024]{1,0:T(8,128)(2,1)} async-done(((bf16[832,1024]{1,0:T(8,128)(2,1)}), bf16[6656,1024]{1,0:T(8,128)(2,1)}) %all-gather.17.cloned.1.call-update) | async-done | bytes 13631504 | tf_op jit(solution)/shard_map/all_gather | solution.py:86
  761.5 8.4 %fusion.108 = (f32[]{:T(128)}, bf16[128,1024]{1,0:T(8,128)(2,1)}) fusion(bf16[6656,1024]{1,0:T(8,128)(2,1)} %all-gather.17.cloned.1.call-done, pred[128,6656]{1,0:T(8,128)(4,1)} %bitcast.26, bf16[128,6656]{1,0:T(8,128)(2,1)S(1)} %gather.7), kind=kOutput, calls=%fused_computation.138 | convolution fusion | flops 1745944576 | bytes 16449540 | tf_op jit(solution)/shard_map/dot_general | solution.py:20
  769.9 38.6 %pmax.7 = f32[]{:T(128)} all-reduce(f32[]{:T(128)} %get-tuple-element.10), channel_id=1, replica_groups=mesh['gx'=4,'gy'=8] {'gx','gy'}, use_global_device_ids=true, to_apply=%region_13.14 | all-reduce | flops 1 | bytes 8 | tf_op jit(solution)/shard_map/pmax | solution.py:89
  (6 shorter events, 0.0 us)
Async XLA Ops:
  7.2 25.5 %all-gather.7.cloned.1.call-start = ((), (), s32[]{:S(2)}) async-start(), calls=%async_computation | async-start | bytes 2129920 | tf_op jit(solution)/shard_map/all_gather | solution.py:45
  7.9 132.6 %all-gather.9.cloned.1.call-start = ((), (), s32[]{:S(2)}) async-start(), calls=%async_computation.1 | async-start | bytes 7667712 | tf_op jit(solution)/shard_map/all_gather | solution.py:49
  10.6 176.1 %all-gather.11.cloned.1.call-start = ((), (), s32[]{:S(2)}) async-start(), calls=%async_computation.2 | async-start | bytes 1916928 | tf_op jit(solution)/shard_map/all_gather | solution.py:61
  12.4 250.5 %all-reduce.3.cloned.1.call-start = ((), (), s32[]{:S(2)}) async-start(), calls=%async_computation.3 | async-start | bytes 6815744 | tf_op jit(solution)/shard_map/psum | solution.py:25
  191.1 179.6 %all-gather.13.cloned.1.call-start = ((), (), s32[]{:S(2)}) async-start(), calls=%async_computation.4 | async-start | bytes 7667712 | tf_op jit(solution)/shard_map/all_gather | solution.py:66
  191.7 284.8 %all-gather.15.cloned.1.call-start = ((), (), s32[]{:S(2)}) async-start(), calls=%async_computation.5 | async-start | bytes 7667712 | tf_op jit(solution)/shard_map/all_gather | solution.py:70
  192.3 376.7 %all-reduce.5.cloned.1.call-start = ((), (), s32[]{:S(2)}) async-start(), calls=%async_computation.6 | async-start | bytes 6815744 | tf_op jit(solution)/shard_map/psum | solution.py:25
  497.9 0.8 copy-start.1
  497.9 1.2 copy-start.2
  498.0 263.5 %all-gather.17.cloned.1.call-start = ((), (), s32[]{:S(2)}) async-start(), calls=%async_computation.7 | async-start | bytes 15335424 | tf_op jit(solution)/shard_map/all_gather | solution.py:86
  498.7 72.9 %copy-start = (s32[512]{0:T(512)S(1)}, s32[512]{0:T(512)}, u32[]{:S(2)}) copy-start(s32[512]{0:T(512)} %param.10) | copy-start | bytes 6148
Sparse Core Ops, SparseCore 0:
  9.6 23.0 all-gather.6
  34.9 105.5 all-gather.8
  143.2 43.4 all-gather.10
  191.2 71.6 all-reduce.2
  264.9 105.6 all-gather.12
  372.7 103.7 all-gather.14
  498.1 70.8 all-reduce.4
  571.2 190.2 all-gather.16
where the time goes:
time: 816 us; the launch traced here: 815 us
  waiting for transfers between devices  645 us (79%)
  blocking collectives  81.1 us (10%)
  matrix products  40.3 us (5%)
  local copies, waits for them, and re-layouts  24.7 us (3%)
  between operations  14.3 us (2%)
  other arithmetic  9.36 us (1%)
    all_gather x1, waiting for transfers between devices, per_device(): lax.all_gather(merge_weight, 'gy', axis=0, tiled=True)  141 us
    psum x2, waiting for transfers between devices, finish_sum(): summed = lax.psum(head_partial, 'gx')  140 us
    all_gather x1, waiting for transfers between devices, per_device(): lax.all_gather(down_weight, 'gy', axis=1, tiled=True)  106 us
    all_gather x1, waiting for transfers between devices, per_device(): lax.all_gather(up_weight, 'gy', axis=0, tiled=True)  105 us
    all_gather x1, waiting for transfers between devices, per_device(): lax.all_gather(qkv_weight, 'gy', axis=0, tiled=True)  104 us
    psum x1, blocking collectives, per_device(): request_sq = lax.psum(request_part, ('gx', 'gy'))  42.4 us
    pmax x1, blocking collectives, per_device(): top_logit = lax.pmax(local_top, ('gx', 'gy'))  38.6 us
    all_gather x1, waiting for transfers between devices, per_device(): lax.all_gather(out_weight, 'gy', axis=1, tiled=True)  26.7 us
  transfers between devices with their start and end apart: 8, of which 8 were waited for; matrix products, arithmetic and copies ran while one was open for 5% of the time, Pallas kernels for 0%

commit v1 on v0

v1 whole, which is shorter than its diff:
```python
import math

import jax
import jax.numpy as jnp
import numpy as np
from jax import lax
from jax.experimental import pallas as pl
from jax.experimental.pallas import tpu as pltpu
from jax.sharding import PartitionSpec as P

HEAD = 104
IMG_GRP = 4
MESH = pl.DeviceIdType.MESH


def ring_order(count):
    ny = 2 if count <= 8 else 4
    nz = count // ny
    walk = [z * ny for z in range(nz)]
    for k, z in enumerate(range(nz - 1, -1, -1)):
        ys = range(1, ny) if k % 2 == 0 else range(ny - 1, 0, -1)
        walk += [z * ny + y for y in ys]
    return walk


def layer_norm(values):
    center = jnp.mean(values, axis=-1, keepdims=True)
    square = jnp.mean(values * values, axis=-1, keepdims=True)
    return (values - center) * lax.rsqrt(square - center * center + 1e-06)


def after(value, *others):
    return lax.optimization_barrier((value, *others))[0]


class Ring:
    def __init__(self, count):
        self.count = count
        self.walk = ring_order(count)
        where = np.argsort(np.array(self.walk))
        self.walk_arr = jnp.asarray(np.array(self.walk, np.int32))
        self.here = jnp.asarray(where.astype(np.int32))[lax.axis_index("gy")]
        n = count
        self.right = [(self.walk[i], self.walk[(i + 1) % n]) for i in range(n)]
        self.left = [(self.walk[i], self.walk[(i - 1) % n]) for i in range(n)]

    def origin(self, offset):
        return self.walk_arr[lax.rem(self.here + offset + self.count, self.count)]

    def gather(self, shard, split_axis):
        n = self.count
        found = [(self.origin(0), shard)]
        cw = ccw = shard
        for step in range(1, (n - 1) // 2 + 1):
            cw = lax.ppermute(cw, "gy", self.right)
            ccw = lax.ppermute(ccw, "gy", self.left)
            found.append((self.origin(-step), cw))
            found.append((self.origin(step), ccw))
        half = shard.shape[split_axis] // 2
        first = lax.slice_in_dim(cw, 0, half, axis=split_axis)
        second = lax.slice_in_dim(ccw, half, 2 * half, axis=split_axis)
        first = lax.ppermute(first, "gy", self.right)
        second = lax.ppermute(second, "gy", self.left)
        far = lax.concatenate([first, second], split_axis)
        found.append((self.origin(n // 2), far))
        return found


def pick(stacked, index):
    return lax.dynamic_index_in_dim(stacked, index, 0, keepdims=False)


def sum_chunks(left, found):
    total = None
    for index, shard in found:
        term = jnp.dot(pick(left, index), shard, preferred_element_type=jnp.float32)
        total = term if total is None else total + term
    return total


def chunked(values, count):
    rows, width = values.shape
    return values.reshape(rows, count, width // count).transpose(1, 0, 2)


def place_columns(left, found, count):
    width = found[0][1].shape[0]
    out = jnp.zeros((count, left.shape[0], width), jnp.float32)
    for index, shard in found:
        term = lax.dot_general(
            left, shard, (((1,), (1,)), ((), ())), preferred_element_type=jnp.float32
        )
        out = lax.dynamic_update_index_in_dim(out, term, index, 0)
    return out.transpose(1, 0, 2).reshape(left.shape[0], count * width)


def core_pairs(gx):
    return [(i, i ^ 1) for i in range(gx)]


def x_shift(gx, k):
    return [(i, (i + 2 * k) % gx) for i in range(gx)]


def gather_features(share, gx):
    me = lax.axis_index("gx")
    chip, core = me // 2, me % 2
    chips = gx // 2
    rows, feats = share.shape
    mine = jnp.zeros((chips, rows, feats), share.dtype)
    mine = lax.dynamic_update_index_in_dim(mine, share, chip, 0)
    for k in range(1, chips):
        got = lax.ppermute(share, "gx", x_shift(gx, k))
        mine = lax.dynamic_update_index_in_dim(mine, got, lax.rem(chip - k + chips, chips), 0)
    theirs = lax.ppermute(mine, "gx", core_pairs(gx))
    low = jnp.where(core == 0, mine, theirs)
    high = jnp.where(core == 0, theirs, mine)
    both = jnp.stack([low, high], axis=1)
    return both.transpose(2, 0, 1, 3).reshape(rows, gx * feats)


def add_sum(partial, stream, gx):
    core = lax.axis_index("gx") % 2
    rows = partial.shape[0] // 2
    keep = lax.dynamic_slice_in_dim(partial, core * rows, rows, 0)
    give = lax.dynamic_slice_in_dim(partial, (1 - core) * rows, rows, 0)
    chip_sum = keep + lax.ppermute(give, "gx", core_pairs(gx))
    sent = chip_sum.astype(jnp.bfloat16)
    total = sent.astype(jnp.float32)
    for k in range(1, gx // 2):
        total = total + lax.ppermute(sent, "gx", x_shift(gx, k)).astype(jnp.float32)
    base = lax.dynamic_slice_in_dim(stream, core * rows, rows, 0)
    mine = (base.astype(jnp.float32) + total).astype(jnp.bfloat16)
    theirs = lax.ppermute(mine, "gx", core_pairs(gx))
    low = jnp.where(core == 0, mine, theirs)
    high = jnp.where(core == 0, theirs, mine)
    return jnp.concatenate([low, high], axis=0)


def scalar_kernel(gx, gy, mine_ref, out_ref, slot_a, slot_b, send_a, recv_a, send_b, recv_b):
    mx, my = lax.axis_index("gx"), lax.axis_index("gy")
    barrier = pltpu.get_barrier_semaphore()
    for k in range(1, gx):
        pl.semaphore_signal(
            barrier, inc=1, device_id=(lax.rem(mx + k, gx), my), device_id_type=MESH
        )
    for k in range(1, gy):
        pl.semaphore_signal(
            barrier, inc=1, device_id=(mx, lax.rem(my + k, gy)), device_id_type=MESH
        )
    pl.semaphore_wait(barrier, gx + gy - 2)

    def combine(one, two):
        row = lax.broadcasted_iota(jnp.int32, one.shape, 0)
        return jnp.where(row == 0, jnp.maximum(one, two), one + two)

    copies = []
    for k in range(1, gx):
        copy = pltpu.make_async_remote_copy(
            src_ref=mine_ref,
            dst_ref=slot_a.at[k],
            send_sem=send_a.at[k],
            recv_sem=recv_a.at[k],
            device_id=(lax.rem(mx + k, gx), my),
            device_id_type=MESH,
        )
        copy.start()
        copies.append(copy)
    total = mine_ref[...]
    for k, copy in enumerate(copies):
        copy.wait()
        total = combine(total, slot_a[k + 1])
    slot_b[0] = total
    copies = []
    for k in range(1, gy):
        copy = pltpu.make_async_remote_copy(
            src_ref=slot_b.at[0],
            dst_ref=slot_b.at[k],
            send_sem=send_b.at[k],
            recv_sem=recv_b.at[k],
            device_id=(mx, lax.rem(my + k, gy)),
            device_id_type=MESH,
        )
        copy.start()
        copies.append(copy)
    for k, copy in enumerate(copies):
        copy.wait()
        total = combine(total, slot_b[k + 1])
    out_ref[...] = total


def reduce_scalars(requests, top, gx, gy):
    count = requests.shape[0]
    tile = jnp.zeros((8, 128), jnp.float32)
    tile = tile.at[0, :].set(top).at[1, :count].set(requests)
    out = pl.pallas_call(
        lambda *refs: scalar_kernel(gx, gy, *refs),
        out_shape=jax.ShapeDtypeStruct((8, 128), jnp.float32),
        in_specs=[pl.BlockSpec(memory_space=pltpu.VMEM)],
        out_specs=pl.BlockSpec(memory_space=pltpu.VMEM),
        scratch_shapes=[
            pltpu.VMEM((gx, 8, 128), jnp.float32),
            pltpu.VMEM((gy, 8, 128), jnp.float32),
            pltpu.SemaphoreType.DMA((gx,)),
            pltpu.SemaphoreType.DMA((gx,)),
            pltpu.SemaphoreType.DMA((gy,)),
            pltpu.SemaphoreType.DMA((gy,)),
        ],
        compiler_params=pltpu.CompilerParams(collective_id=0, has_side_effects=True),
        name="scalar_sums",
    )(tile)
    return out[1, :count], out[0, 0]


def attend(projected, segment_ids):
    scores = jnp.einsum(
        "qhe,khe->hqk", projected[:, 0], projected[:, 1], preferred_element_type=jnp.float32
    ) / math.sqrt(HEAD)
    allowed = segment_ids[:, None] == segment_ids[None, :]
    scores = jnp.where(allowed[None], scores, -1e30)
    probs = jax.nn.softmax(scores, axis=-1).astype(jnp.bfloat16)
    mixed = jnp.einsum("hqk,khe->qhe", probs, projected[:, 2], preferred_element_type=jnp.float32)
    return mixed.astype(jnp.bfloat16)


def per_device(
    gx,
    gy,
    patches,
    segment_ids,
    image_requests,
    merge_index,
    qkv_weight,
    out_weight,
    up_weight,
    down_weight,
    merge_weight,
):
    tok_rows, feat_share = patches.shape
    group_index = lax.axis_index("gy")
    own_index = lax.axis_index("gx")
    ring = Ring(gy)
    head_share = qkv_weight.shape[2]
    local_heads = head_share // HEAD

    qkv_found = ring.gather(qkv_weight.reshape(qkv_weight.shape[0], -1), 1)
    out_found = ring.gather(out_weight.T, 1)
    up_found = ring.gather(after(up_weight, qkv_found[-1][1]), 1)
    down_found = ring.gather(after(down_weight.T, out_found[-1][1]), 1)
    half = merge_weight.shape[1] // 2
    merge_a = ring.gather(after(merge_weight[:, :half], up_found[-1][1]), 1)
    merge_b = ring.gather(after(merge_weight[:, half:], down_found[-1][1]), 1)

    stream_full = gather_features(patches, gx)
    normed = layer_norm(stream_full.astype(jnp.float32)).astype(jnp.bfloat16)
    projected = sum_chunks(chunked(normed, gy), qkv_found)
    projected = projected.astype(jnp.bfloat16).reshape(tok_rows, 3, local_heads, HEAD)
    mixed = attend(projected, segment_ids).reshape(tok_rows, head_share)
    head_partial = place_columns(mixed, out_found, gy)
    stream_full = add_sum(head_partial, stream_full, gx)
    normed_two = layer_norm(stream_full.astype(jnp.float32)).astype(jnp.bfloat16)
    hidden = sum_chunks(chunked(normed_two, gy), up_found)
    hidden = jax.nn.gelu(hidden, approximate=False).astype(jnp.bfloat16)
    unit_partial = place_columns(hidden, down_found, gy)
    final_full = add_sum(unit_partial, stream_full, gx)
    final_share = lax.dynamic_slice_in_dim(final_full, own_index * feat_share, feat_share, 1)
    row_squares = jnp.sum(jnp.square(final_share.astype(jnp.float32)), axis=1)
    image_ids = group_index * IMG_GRP + jnp.arange(IMG_GRP, dtype=jnp.int32)
    member = segment_ids[:, None] == image_ids[None, :]
    image_sq = jnp.sum(jnp.where(member, row_squares[:, None], 0.0), axis=0)
    local_requests = lax.dynamic_slice_in_dim(image_requests, group_index * IMG_GRP, IMG_GRP)
    request_count = image_requests.shape[0] // 4
    owner = local_requests[:, None] == jnp.arange(request_count, dtype=jnp.int32)[None, :]
    request_part = jnp.sum(jnp.where(owner, image_sq[:, None], 0.0), axis=0)
    local_index = (merge_index - group_index * tok_rows).reshape(-1)
    joined = jnp.take(final_full, local_index, axis=0).reshape(
        merge_index.shape[0], 4 * final_full.shape[1]
    )
    chunks = chunked(joined, gy)
    logits = jnp.concatenate([sum_chunks(chunks, merge_a), sum_chunks(chunks, merge_b)], axis=1)
    local_top = jnp.max(logits)
    request_sq, top_logit = reduce_scalars(request_part, local_top, gx, gy)
    return (logits.astype(jnp.bfloat16), jnp.sqrt(request_sq), top_logit)


def solution(mesh):
    gx, gy = mesh.shape["gx"], mesh.shape["gy"]
    in_specs = (
        P("gy", "gx"),
        P("gy"),
        P(),
        P("gy", None),
        P("gy", None, "gx"),
        P("gx", "gy"),
        P("gy", "gx"),
        P("gx", "gy"),
        P("gy", "gx"),
    )
    out_specs = (P("gy", "gx"), P(), P())

    def body(*args):
        return per_device(gx, gy, *args)

    return jax.shard_map(
        body, mesh=mesh, in_specs=in_specs, out_specs=out_specs, check_vma=False
    )
```

time: 816 us -> 492 us (0.60)
  waiting for transfers between devices: 645 us -> 240 us
  blocking collectives: 81.1 us -> 0 us
  starting transfers between devices: 0.5 us -> 55.4 us
  matrix products: 40.3 us -> 83.1 us
  local copies, waits for them, and re-layouts: 24.7 us -> 55.4 us
  Pallas kernels: 0 us -> 10.2 us
  between operations: 14.3 us -> 23.6 us
    all_gather x6 -> x0, waiting for transfers between devices: 503 us -> none  [the longest x1 141 us: per_device(): lax.all_gather(merge_weight, 'gy', axis=0, tiled=True)]
    ppermute x0 -> x56, waiting for transfers between devices: none -> 240 us  [the longest x18 155 us: gather(): ccw = lax.ppermute(ccw, 'gy', self.left)]
    psum x2 -> x0, waiting for transfers between devices: 140 us -> none  [finish_sum(): summed = lax.psum(head_partial, 'gx')]
    ppermute x0 -> x56, starting transfers between devices: none -> 55.4 us  [the longest x18 28.5 us: gather(): cw = lax.ppermute(cw, 'gy', self.right)]
    dot_general x6 -> x50, matrix products: 40.3 us -> 83.1 us  [the longest x32 63.5 us: sum_chunks(): term = jnp.dot(pick(left, index), shard, preferred_element_type=jnp.float32)]
    psum x1 -> x0, blocking collectives: 42.4 us -> none  [per_device(): request_sq = lax.psum(request_part, ('gx', 'gy'))]
    pmax x1 -> x0, blocking collectives: 38.6 us -> none  [per_device(): top_logit = lax.pmax(local_top, ('gx', 'gy'))]
    another operation x0 -> x11, local copies, waits for them, and re-layouts: none -> 15.7 us
  transfers between devices with their start and end apart: 8 -> 56, of which waited for: 8 -> 22; matrix products, arithmetic and copies ran while one was open for 5% -> 18% of each run, Pallas kernels for 0% -> 0%
where the time goes in v1:
time: 492 us; the launch traced here: 485 us
  waiting for transfers between devices  240 us (49%)
  matrix products  83.1 us (17%)
  local copies, waits for them, and re-layouts  55.4 us (11%)
  starting transfers between devices  55.4 us (11%)
  between operations  23.6 us (5%)
  other arithmetic  17.2 us (3%)
  Pallas kernels  10.2 us (2%)
    ppermute x18, waiting for transfers between devices, gather(): ccw = lax.ppermute(ccw, 'gy', self.left)  155 us
    dot_general x32, matrix products, sum_chunks(): term = jnp.dot(pick(left, index), shard, preferred_element_type=jnp.float32)  63.5 us
    ppermute x18, waiting for transfers between devices, gather(): cw = lax.ppermute(cw, 'gy', self.right)  52.2 us
    ppermute x18, starting transfers between devices, gather(): cw = lax.ppermute(cw, 'gy', self.right)  28.5 us
    ppermute x6, waiting for transfers between devices, gather(): second = lax.ppermute(second, 'gy', self.left)  24.4 us
    dot_general x16, matrix products, place_columns(): lax.dot_general(left, shard, (((1,), (1,)), ((), ())), preferred_element_...  18.4 us
    another operation x11, local copies, waits for them, and re-layouts  15.7 us
    unnamed x85, local copies, waits for them, and re-layouts  13.5 us
  transfers between devices with their start and end apart: 56, of which 22 were waited for; matrix products, arithmetic and copies ran while one was open for 18% of the time, Pallas kernels for 0%

profile of v1, /device:TPU:0, one launch (start us, length us, event | category | flops | bytes accessed | tf_op | source)
XLA Modules:
  0.0 484.6 jit_solution(9263884764702533471)
XLA Ops:
  0.7 3.0 collective-permute-start
  5.3 1.6 collective-permute-start.2
  9.0 4.7 collective-permute-done
  13.8 1.8 collective-permute-start.11
  15.6 7.9 %collective-permute-done.10 = bf16[208,416]{0,1:T(8,128)(2,1)} collective-permute-done((bf16[208,416]{0,1:T(8,128)(2,1)}, bf16[208,416]{0,1:T(8,128)(2,1)}, u32[]{:S(2)}, u32[]{:S(2)}) %collective-permute-start.10) | collective-permute-done | bytes 173088 | tf_op jit(solution)/shard_map/ppermute | solution.py:55
  25.6 4.0 collective-permute-done.12
  33.7 4.1 collective-permute-done.14
  63.3 1.6 collective-permute-start.21
  66.3 5.4 %collective-permute-done.17 = bf16[208,208]{0,1:T(8,128)(2,1)S(1)} collective-permute-done((bf16[208,208]{0,1:T(8,128)(2,1)S(1)}, bf16[208,208]{0,1:T(8,128)(2,1)S(1)}, u32[]{:S(2)}, u32[]{:S(2)}) %collective-permute-start.17) | collective-permute-done | bytes 86560 | tf_op jit(solution)/shard_map/ppermute | solution.py:63
  77.6 1.6 convolution_add_fusion.2
  79.2 1.6 fusion.99
  81.5 10.9 %collective-permute-done.6 = bf16[208,1248]{1,0:T(8,128)(2,1)S(1)} collective-permute-done((bf16[208,1248]{1,0:T(8,128)(2,1)S(1)}, bf16[208,1248]{1,0:T(8,128)(2,1)S(1)}, u32[]{:S(2)}, u32[]{:S(2)}) %collective-permute-start.6) | collective-permute-done | bytes 519200 | tf_op jit(solution)/shard_map/ppermute | solution.py:55
  92.4 1.6 collective-permute-start.8
  95.4 3.5 collective-permute-done.8
  98.9 1.9 collective-permute-done.9
  103.1 2.1 fusion.146
  112.5 1.7 copy.99
  118.3 18.0 %collective-permute-done.22 = bf16[208,2048]{1,0:T(8,128)(2,1)} collective-permute-done((bf16[208,2048]{1,0:T(8,128)(2,1)}, bf16[208,2048]{1,0:T(8,128)(2,1)}, u32[]{:S(2)}, u32[]{:S(2)}) %collective-permute-start.22) | collective-permute-done | bytes 852000 | tf_op jit(solution)/shard_map/ppermute | solution.py:56
  138.3 16.2 %collective-permute-done.30 = bf16[208,2048]{1,0:T(8,128)(2,1)} collective-permute-done((bf16[208,2048]{1,0:T(8,128)(2,1)}, bf16[208,2048]{1,0:T(8,128)(2,1)}, u32[]{:S(2)}, u32[]{:S(2)}) %collective-permute-start.30) | collective-permute-done | bytes 852000 | tf_op jit(solution)/shard_map/ppermute | solution.py:56
  157.4 1.7 add_convert_fusion.3
  159.7 13.1 %collective-permute-done.24 = bf16[208,2048]{1,0:T(8,128)(2,1)} collective-permute-done((bf16[208,2048]{1,0:T(8,128)(2,1)}, bf16[208,2048]{1,0:T(8,128)(2,1)}, u32[]{:S(2)}, u32[]{:S(2)}) %collective-permute-start.24) | collective-permute-done | bytes 852000 | tf_op jit(solution)/shard_map/ppermute | solution.py:56
  175.6 15.4 %collective-permute-done.32 = bf16[208,2048]{1,0:T(8,128)(2,1)} collective-permute-done((bf16[208,2048]{1,0:T(8,128)(2,1)}, bf16[208,2048]{1,0:T(8,128)(2,1)}, u32[]{:S(2)}, u32[]{:S(2)}) %collective-permute-start.32) | collective-permute-done | bytes 852000 | tf_op jit(solution)/shard_map/ppermute | solution.py:56
  192.6 1.6 collective-permute-start.27
  194.6 14.7 %collective-permute-done.26 = bf16[208,2048]{1,0:T(8,128)(2,1)} collective-permute-done((bf16[208,2048]{1,0:T(8,128)(2,1)}, bf16[208,2048]{1,0:T(8,128)(2,1)}, u32[]{:S(2)}, u32[]{:S(2)}) %collective-permute-start.26) | collective-permute-done | bytes 852000 | tf_op jit(solution)/shard_map/ppermute | solution.py:56
  211.9 1.6 collective-permute-start.35
  213.5 13.9 %collective-permute-done.34 = bf16[208,2048]{1,0:T(8,128)(2,1)S(1)} collective-permute-done((bf16[208,2048]{1,0:T(8,128)(2,1)}, bf16[208,2048]{1,0:T(8,128)(2,1)S(1)}, u32[]{:S(2)}, u32[]{:S(2)}) %collective-permute-start.34) | collective-permute-done | bytes 852000 | tf_op jit(solution)/shard_map/ppermute | solution.py:56
  228.2 8.3 %collective-permute-done.28 = bf16[208,1024]{1,0:T(8,128)(2,1)S(1)} collective-permute-done((bf16[208,1024]{1,0:T(8,128)(2,1)S(1)}, bf16[208,1024]{1,0:T(8,128)(2,1)S(1)}, u32[]{:S(2)}, u32[]{:S(2)}) %collective-permute-start.28) | collective-permute-done | bytes 426016 | tf_op jit(solution)/shard_map/ppermute | solution.py:63
  236.7 8.7 %collective-permute-done.36 = bf16[208,1024]{1,0:T(8,128)(2,1)S(1)} collective-permute-done((bf16[208,1024]{1,0:T(8,128)(2,1)S(1)}, bf16[208,1024]{1,0:T(8,128)(2,1)S(1)}, u32[]{:S(2)}, u32[]{:S(2)}) %collective-permute-start.36) | collective-permute-done | bytes 426016 | tf_op jit(solution)/shard_map/ppermute | solution.py:63
  249.7 1.8 multiply_convert_fusion
  251.5 2.0 fusion.92
  254.3 1.9 fusion.84
  256.2 1.9 fusion.86
  258.1 3.9 fusion.88
  262.0 3.9 fusion.90
  265.9 4.0 fusion.82
  269.9 14.4 %fusion.3 = bf16[512,2048]{1,0:T(8,128)(2,1)} fusion(f32[512,2048]{1,0:T(8,128)S(1)} %fusion.78, f32[512,2048]{1,0:T(8,128)} %fusion.82, f32[512,2048]{1,0:T(8,128)S(1)} %fusion.84, f32[512,2048]{1,0:T(8,128)S(1)} %fusion.86, f32[512,2048]{1,0:T(8,128)} %fusion.88, f32[512,2048]{1,0:T(8,128)S(1)} %fusion.92, f32[512,2048]{1,0:T(8,128)} %fusion.90, ...), kind=kOutput, calls=%fused_computation.7 | convolution fusion | flops 511705088 | bytes 32522244 | tf_op jit(solution)/shard_map/dot_general | solution.py:76
  287.0 2.1 fusion.37
  289.1 2.1 fusion.36
  291.2 2.1 fusion.35
  293.3 2.1 fusion.34
  295.3 2.1 fusion.33
  299.6 1.6 constant_dynamic-slice_fusion.8
  301.2 2.7 copy.101
  305.4 1.6 collective-permute-start.40
  309.5 19.4 %collective-permute-done.41 = bf16[832,512]{1,0:T(8,128)(2,1)} collective-permute-done((bf16[832,512]{1,0:T(8,128)(2,1)S(1)}, bf16[832,512]{1,0:T(8,128)(2,1)}, u32[]{:S(2)}, u32[]{:S(2)}) %collective-permute-start.41) | collective-permute-done | bytes 852000 | tf_op jit(solution)/shard_map/ppermute | solution.py:56
  330.9 16.2 %collective-permute-done.49 = bf16[832,512]{1,0:T(8,128)(2,1)} collective-permute-done((bf16[832,512]{1,0:T(8,128)(2,1)S(1)}, bf16[832,512]{1,0:T(8,128)(2,1)}, u32[]{:S(2)}, u32[]{:S(2)}) %collective-permute-start.49) | collective-permute-done | bytes 852000 | tf_op jit(solution)/shard_map/ppermute | solution.py:56
  349.2 1.7 copy.100
  350.9 2.1 add_convert_fusion.1
  353.6 11.8 %collective-permute-done.43 = bf16[832,512]{1,0:T(8,128)(2,1)} collective-permute-done((bf16[832,512]{1,0:T(8,128)(2,1)}, bf16[832,512]{1,0:T(8,128)(2,1)}, u32[]{:S(2)}, u32[]{:S(2)}) %collective-permute-start.43) | collective-permute-done | bytes 852000 | tf_op jit(solution)/shard_map/ppermute | solution.py:56
  367.4 16.2 %collective-permute-done.51 = bf16[832,512]{1,0:T(8,128)(2,1)} collective-permute-done((bf16[832,512]{1,0:T(8,128)(2,1)}, bf16[832,512]{1,0:T(8,128)(2,1)}, u32[]{:S(2)}, u32[]{:S(2)}) %collective-permute-start.51) | collective-permute-done | bytes 852000 | tf_op jit(solution)/shard_map/ppermute | solution.py:56
  388.8 11.4 %collective-permute-done.44 = bf16[832,512]{1,0:T(8,128)(2,1)S(1)} collective-permute-done((bf16[832,512]{1,0:T(8,128)(2,1)}, bf16[832,512]{1,0:T(8,128)(2,1)S(1)}, u32[]{:S(2)}, u32[]{:S(2)}) %collective-permute-start.44) | collective-permute-done | bytes 852000 | tf_op jit(solution)/shard_map/ppermute | solution.py:55
  402.6 1.8 slice.122
  404.9 13.7 %collective-permute-done.52 = bf16[832,512]{1,0:T(8,128)(2,1)} collective-permute-done((bf16[832,512]{1,0:T(8,128)(2,1)}, bf16[832,512]{1,0:T(8,128)(2,1)}, u32[]{:S(2)}, u32[]{:S(2)}) %collective-permute-start.52) | collective-permute-done | bytes 852000 | tf_op jit(solution)/shard_map/ppermute | solution.py:55
  418.6 1.8 slice.123
  421.9 1.8 slice.124
  425.6 2.5 gather_fusion
  429.5 4.7 constant_dynamic-slice_fusion.2
  437.2 1.6 copy.92
  441.9 1.9 copy.95
  448.9 2.2 fusion.64
  451.1 2.2 fusion.60
  456.4 2.2 fusion.58
  466.9 2.1 fusion.143
  471.1 10.2 %scalar_sums.1 = f32[8,128]{1,0:T(8,128)} custom-call(f32[8,128]{1,0:T(8,128)} %copy-done.28), custom_call_target="tpu_custom_call" | custom-call | tf_op jit(solution)/shard_map/scalar_sums/pallas_call | solution.py:196
  (261 shorter events, 110.9 us)
Async XLA Ops:
  0.6 41.0 %copy-start.35 = (s32[8]{0:T(128)S(1)}, s32[8]{0:T(128)}, u32[]{:S(2)}) copy-start(s32[8]{0:T(128)} %constant.361.clone) | copy-start | bytes 100
  0.6 46.8 %copy-start.25 = (s32[8]{0:T(128)S(1)}, s32[8]{0:T(128)}, u32[]{:S(2)}) copy-start(s32[8]{0:T(128)} %constant.360.clone) | copy-start | bytes 100
  0.7 40.0 %copy-start.26 = (s32[512]{0:T(512)S(1)}, s32[512]{0:T(512)}, u32[]{:S(2)}) copy-start(s32[512]{0:T(512)} %param.16) | copy-start | bytes 6148
  0.7 13.0 %collective-permute-start = (bf16[512,416]{0,1:T(8,128)(2,1)}, bf16[512,416]{0,1:T(8,128)(2,1)S(1)}, u32[]{:S(2)}, u32[]{:S(2)}) collective-permute-start(bf16[512,416]{0,1:T(8,128)(2,1)} %param.15), channel_id=1, source_target_pairs={{0,16},{8,24},{16,0},{24,8},{1,17},{9,25},{17,1},{25,9},{2,18},{10... | collective-permute-start | bytes 1277960 | tf_op jit(solution)/shard_map/ppermute | solution.py:113
  5.3 26.4 %collective-permute-start.2 = (bf16[208,1248]{1,0:T(8,128)(2,1)S(1)}, bf16[208,1248]{1,0:T(8,128)(2,1)S(1)}, u32[]{:S(2)}, u32[]{:S(2)}) collective-permute-start(bf16[208,1248]{1,0:T(8,128)(2,1)S(1)} %copy.78), channel_id=1, source_target_pairs={{0,2},{2,4},{4,6},{6,7},{7,5},{5,3},{3,1},{1,0},{8,10},{10,12},{12... | collective-permute-start | bytes 1557512 | tf_op jit(solution)/shard_map/ppermute | solution.py:55
  6.9 24.3 %collective-permute-start.3 = (bf16[208,1248]{1,0:T(8,128)(2,1)S(1)}, bf16[208,1248]{1,0:T(8,128)(2,1)}, u32[]{:S(2)}, u32[]{:S(2)}) collective-permute-start(bf16[208,1248]{1,0:T(8,128)(2,1)S(1)} %copy.78), channel_id=1, source_target_pairs={{0,1},{2,0},{4,2},{6,4},{7,6},{5,7},{3,5},{1,3},{8,9},{10,8},{12,1... | collective-permute-start | bytes 1557512 | tf_op jit(solution)/shard_map/ppermute | solution.py:56
  7.3 16.2 %collective-permute-start.10 = (bf16[208,416]{0,1:T(8,128)(2,1)}, bf16[208,416]{0,1:T(8,128)(2,1)}, u32[]{:S(2)}, u32[]{:S(2)}) collective-permute-start(bf16[208,416]{0,1:T(8,128)(2,1)} %bitcast.302), channel_id=1, source_target_pairs={{0,2},{2,4},{4,6},{6,7},{7,5},{5,3},{3,1},{1,0},{8,10},{10,12},{12... | collective-permute-start | bytes 519176 | tf_op jit(solution)/shard_map/ppermute | solution.py:55
  13.7 60.1 %collective-permute-start.1 = (bf16[2,512,416]{1,2,0:T(8,128)(2,1)S(1)}, bf16[2,512,416]{1,2,0:T(8,128)(2,1)S(1)}, u32[]{:S(2)}, u32[]{:S(2)}) collective-permute-start(bf16[2,512,416]{1,2,0:T(8,128)(2,1)S(1)} %bitcast_dynamic-update-slice_fusion), channel_id=1, source_target_pairs={{0,8},{8,0},{16,24},{24,16},{1,9},{9,1},{17,25},{25,17},{2,10},{10... | collective-permute-start | bytes 2555912 | tf_op jit(solution)/shard_map/ppermute | solution.py:115
  13.8 11.3 %collective-permute-start.11 = (bf16[208,416]{0,1:T(8,128)(2,1)}, bf16[208,416]{0,1:T(8,128)(2,1)S(1)}, u32[]{:S(2)}, u32[]{:S(2)}) collective-permute-start(bf16[208,416]{0,1:T(8,128)(2,1)} %bitcast.303), channel_id=1, source_target_pairs={{0,1},{2,0},{4,2},{6,4},{7,6},{5,7},{3,5},{1,3},{8,9},{10,8},{12,1... | collective-permute-start | bytes 519176 | tf_op jit(solution)/shard_map/ppermute | solution.py:56
  23.5 6.1 %collective-permute-start.12 = (bf16[208,416]{0,1:T(8,128)(2,1)}, bf16[208,416]{0,1:T(8,128)(2,1)S(1)}, u32[]{:S(2)}, u32[]{:S(2)}) collective-permute-start(bf16[208,416]{0,1:T(8,128)(2,1)} %collective-permute-done.10), channel_id=1, source_target_pairs={{0,2},{2,4},{4,6},{6,7},{7,5},{5,3},{3,1},{1,0},{8,10},{10,12},{12... | collective-permute-start | bytes 519176 | tf_op jit(solution)/shard_map/ppermute | solution.py:55
  25.1 8.1 %collective-permute-start.13 = (bf16[208,416]{0,1:T(8,128)(2,1)S(1)}, bf16[208,416]{0,1:T(8,128)(2,1)}, u32[]{:S(2)}, u32[]{:S(2)}) collective-permute-start(bf16[208,416]{0,1:T(8,128)(2,1)S(1)} %collective-permute-done.11), channel_id=1, source_target_pairs={{0,1},{2,0},{4,2},{6,4},{7,6},{5,7},{3,5},{1,3},{8,9},{10,8},{12,1... | collective-permute-start | bytes 519176 | tf_op jit(solution)/shard_map/ppermute | solution.py:56
  29.6 8.2 %collective-permute-start.14 = (bf16[208,416]{0,1:T(8,128)(2,1)S(1)}, bf16[208,416]{0,1:T(8,128)(2,1)S(1)}, u32[]{:S(2)}, u32[]{:S(2)}) collective-permute-start(bf16[208,416]{0,1:T(8,128)(2,1)S(1)} %collective-permute-done.12), channel_id=1, source_target_pairs={{0,2},{2,4},{4,6},{6,7},{7,5},{5,3},{3,1},{1,0},{8,10},{10,12},{12... | collective-permute-start | bytes 519176 | tf_op jit(solution)/shard_map/ppermute | solution.py:55
  31.2 40.6 %collective-permute-start.5 = (bf16[208,1248]{1,0:T(8,128)(2,1)}, bf16[208,1248]{1,0:T(8,128)(2,1)}, u32[]{:S(2)}, u32[]{:S(2)}) collective-permute-start(bf16[208,1248]{1,0:T(8,128)(2,1)} %collective-permute-done.3), channel_id=1, source_target_pairs={{0,1},{2,0},{4,2},{6,4},{7,6},{5,7},{3,5},{1,3},{8,9},{10,8},{12,1... | collective-permute-start | bytes 1557512 | tf_op jit(solution)/shard_map/ppermute | solution.py:56
  31.6 40.6 %collective-permute-start.4 = (bf16[208,1248]{1,0:T(8,128)(2,1)S(1)}, bf16[208,1248]{1,0:T(8,128)(2,1)S(1)}, u32[]{:S(2)}, u32[]{:S(2)}) collective-permute-start(bf16[208,1248]{1,0:T(8,128)(2,1)S(1)} %collective-permute-done.2), channel_id=1, source_target_pairs={{0,2},{2,4},{4,6},{6,7},{7,5},{5,3},{3,1},{1,0},{8,10},{10,12},{12... | collective-permute-start | bytes 1557512 | tf_op jit(solution)/shard_map/ppermute | solution.py:55
  33.2 30.0 %collective-permute-start.15 = (bf16[208,416]{0,1:T(8,128)(2,1)}, bf16[208,416]{0,1:T(8,128)(2,1)}, u32[]{:S(2)}, u32[]{:S(2)}) collective-permute-start(bf16[208,416]{0,1:T(8,128)(2,1)} %collective-permute-done.13), channel_id=1, source_target_pairs={{0,1},{2,0},{4,2},{6,4},{7,6},{5,7},{3,5},{1,3},{8,9},{10,8},{12,1... | collective-permute-start | bytes 519176 | tf_op jit(solution)/shard_map/ppermute | solution.py:56
  39.1 26.7 %collective-permute-start.16 = (bf16[208,208]{0,1:T(8,128)(2,1)}, bf16[208,208]{0,1:T(8,128)(2,1)S(1)}, u32[]{:S(2)}, u32[]{:S(2)}) collective-permute-start(bf16[208,208]{0,1:T(8,128)(2,1)} %slice.115), channel_id=1, source_target_pairs={{0,2},{2,4},{4,6},{6,7},{7,5},{5,3},{3,1},{1,0},{8,10},{10,12},{12... | collective-permute-start | bytes 259592 | tf_op jit(solution)/shard_map/ppermute | solution.py:62
  63.3 53.4 %collective-permute-start.21 = (bf16[208,2048]{1,0:T(8,128)(2,1)}, bf16[208,2048]{1,0:T(8,128)(2,1)}, u32[]{:S(2)}, u32[]{:S(2)}) collective-permute-start(bf16[208,2048]{1,0:T(8,128)(2,1)} %param.21), channel_id=1, source_target_pairs={{0,2},{2,4},{4,6},{6,7},{7,5},{5,3},{3,1},{1,0},{8,10},{10,12},{12... | collective-permute-start | bytes 2555912 | tf_op jit(solution)/shard_map/ppermute | solution.py:55
  65.8 6.0 %collective-permute-start.17 = (bf16[208,208]{0,1:T(8,128)(2,1)S(1)}, bf16[208,208]{0,1:T(8,128)(2,1)S(1)}, u32[]{:S(2)}, u32[]{:S(2)}) collective-permute-start(bf16[208,208]{0,1:T(8,128)(2,1)S(1)} %slice.116), channel_id=1, source_target_pairs={{0,1},{2,0},{4,2},{6,4},{7,6},{5,7},{3,5},{1,3},{8,9},{10,8},{12,1... | collective-permute-start | bytes 259592 | tf_op jit(solution)/shard_map/ppermute | solution.py:63
  71.8 22.2 %collective-permute-start.7 = (bf16[208,1248]{1,0:T(8,128)(2,1)}, bf16[208,1248]{1,0:T(8,128)(2,1)S(1)}, u32[]{:S(2)}, u32[]{:S(2)}) collective-permute-start(bf16[208,1248]{1,0:T(8,128)(2,1)} %collective-permute-done.5), channel_id=1, source_target_pairs={{0,1},{2,0},{4,2},{6,4},{7,6},{5,7},{3,5},{1,3},{8,9},{10,8},{12,1... | collective-permute-start | bytes 1557512 | tf_op jit(solution)/shard_map/ppermute | solution.py:56
  72.3 20.1 %collective-permute-start.6 = (bf16[208,1248]{1,0:T(8,128)(2,1)S(1)}, bf16[208,1248]{1,0:T(8,128)(2,1)S(1)}, u32[]{:S(2)}, u32[]{:S(2)}) collective-permute-start(bf16[208,1248]{1,0:T(8,128)(2,1)S(1)} %collective-permute-done.4), channel_id=1, source_target_pairs={{0,2},{2,4},{4,6},{6,7},{7,5},{5,3},{3,1},{1,0},{8,10},{10,12},{12... | collective-permute-start | bytes 1557512 | tf_op jit(solution)/shard_map/ppermute | solution.py:55
  92.4 6.5 %collective-permute-start.8 = (bf16[208,624]{1,0:T(8,128)(2,1)S(1)}, bf16[208,624]{1,0:T(8,128)(2,1)S(1)}, u32[]{:S(2)}, u32[]{:S(2)}) collective-permute-start(bf16[208,624]{1,0:T(8,128)(2,1)S(1)} %slice.110), channel_id=1, source_target_pairs={{0,2},{2,4},{4,6},{6,7},{7,5},{5,3},{3,1},{1,0},{8,10},{10,12},{12... | collective-permute-start | bytes 778760 | tf_op jit(solution)/shard_map/ppermute | solution.py:62
  94.2 6.6 %collective-permute-start.9 = (bf16[208,624]{1,0:T(8,128)(2,1)S(1)}, bf16[208,624]{1,0:T(8,128)(2,1)S(1)}, u32[]{:S(2)}, u32[]{:S(2)}) collective-permute-start(bf16[208,624]{1,0:T(8,128)(2,1)S(1)} %slice.111), channel_id=1, source_target_pairs={{0,1},{2,0},{4,2},{6,4},{7,6},{5,7},{3,5},{1,3},{8,9},{10,8},{12,1... | collective-permute-start | bytes 778760 | tf_op jit(solution)/shard_map/ppermute | solution.py:63
  114.2 43.1 %collective-permute-start.18 = (f32[256,1664]{1,0:T(8,128)}, f32[256,1664]{1,0:T(8,128)}, u32[]{:S(2)}, u32[]{:S(2)}) collective-permute-start(f32[256,1664]{1,0:T(8,128)} %copy.99), channel_id=1, source_target_pairs={{0,8},{8,0},{16,24},{24,16},{1,9},{9,1},{17,25},{25,17},{2,10},{10... | collective-permute-start | bytes 5111816 | tf_op jit(solution)/shard_map/ppermute | solution.py:127
  114.2 22.1 %collective-permute-start.22 = (bf16[208,2048]{1,0:T(8,128)(2,1)}, bf16[208,2048]{1,0:T(8,128)(2,1)}, u32[]{:S(2)}, u32[]{:S(2)}) collective-permute-start(bf16[208,2048]{1,0:T(8,128)(2,1)} %param.21), channel_id=1, source_target_pairs={{0,1},{2,0},{4,2},{6,4},{7,6},{5,7},{3,5},{1,3},{8,9},{10,8},{12,1... | collective-permute-start | bytes 2555912 | tf_op jit(solution)/shard_map/ppermute | solution.py:56
  114.6 22.1 %collective-permute-start.29 = (bf16[208,2048]{1,0:T(8,128)(2,1)}, bf16[208,2048]{1,0:T(8,128)(2,1)}, u32[]{:S(2)}, u32[]{:S(2)}) collective-permute-start(bf16[208,2048]{1,0:T(8,128)(2,1)} %bitcast.306), channel_id=1, source_target_pairs={{0,2},{2,4},{4,6},{6,7},{7,5},{5,3},{3,1},{1,0},{8,10},{10,12},{12... | collective-permute-start | bytes 2555912 | tf_op jit(solution)/shard_map/ppermute | solution.py:55
  116.2 38.3 %collective-permute-start.30 = (bf16[208,2048]{1,0:T(8,128)(2,1)}, bf16[208,2048]{1,0:T(8,128)(2,1)}, u32[]{:S(2)}, u32[]{:S(2)}) collective-permute-start(bf16[208,2048]{1,0:T(8,128)(2,1)} %bitcast.307), channel_id=1, source_target_pairs={{0,1},{2,0},{4,2},{6,4},{7,6},{5,7},{3,5},{1,3},{8,9},{10,8},{12,1... | collective-permute-start | bytes 2555912 | tf_op jit(solution)/shard_map/ppermute | solution.py:56
  116.7 38.3 %collective-permute-start.23 = (bf16[208,2048]{1,0:T(8,128)(2,1)}, bf16[208,2048]{1,0:T(8,128)(2,1)}, u32[]{:S(2)}, u32[]{:S(2)}) collective-permute-start(bf16[208,2048]{1,0:T(8,128)(2,1)} %collective-permute-done.21), channel_id=1, source_target_pairs={{0,2},{2,4},{4,6},{6,7},{7,5},{5,3},{3,1},{1,0},{8,10},{10,12},{12... | collective-permute-start | bytes 2555912 | tf_op jit(solution)/shard_map/ppermute | solution.py:55
  136.3 36.5 %collective-permute-start.24 = (bf16[208,2048]{1,0:T(8,128)(2,1)}, bf16[208,2048]{1,0:T(8,128)(2,1)}, u32[]{:S(2)}, u32[]{:S(2)}) collective-permute-start(bf16[208,2048]{1,0:T(8,128)(2,1)} %collective-permute-done.22), channel_id=1, source_target_pairs={{0,1},{2,0},{4,2},{6,4},{7,6},{5,7},{3,5},{1,3},{8,9},{10,8},{12,1... | collective-permute-start | bytes 2555912 | tf_op jit(solution)/shard_map/ppermute | solution.py:56
  136.7 36.5 %collective-permute-start.31 = (bf16[208,2048]{1,0:T(8,128)(2,1)}, bf16[208,2048]{1,0:T(8,128)(2,1)}, u32[]{:S(2)}, u32[]{:S(2)}) collective-permute-start(bf16[208,2048]{1,0:T(8,128)(2,1)} %collective-permute-done.29), channel_id=1, source_target_pairs={{0,2},{2,4},{4,6},{6,7},{7,5},{5,3},{3,1},{1,0},{8,10},{10,12},{12... | collective-permute-start | bytes 2555912 | tf_op jit(solution)/shard_map/ppermute | solution.py:55
  154.5 36.5 %collective-permute-start.32 = (bf16[208,2048]{1,0:T(8,128)(2,1)}, bf16[208,2048]{1,0:T(8,128)(2,1)}, u32[]{:S(2)}, u32[]{:S(2)}) collective-permute-start(bf16[208,2048]{1,0:T(8,128)(2,1)} %collective-permute-done.30), channel_id=1, source_target_pairs={{0,1},{2,0},{4,2},{6,4},{7,6},{5,7},{3,5},{1,3},{8,9},{10,8},{12,1... | collective-permute-start | bytes 2555912 | tf_op jit(solution)/shard_map/ppermute | solution.py:56
  155.0 36.5 %collective-permute-start.25 = (bf16[208,2048]{1,0:T(8,128)(2,1)}, bf16[208,2048]{1,0:T(8,128)(2,1)}, u32[]{:S(2)}, u32[]{:S(2)}) collective-permute-start(bf16[208,2048]{1,0:T(8,128)(2,1)} %collective-permute-done.23), channel_id=1, source_target_pairs={{0,2},{2,4},{4,6},{6,7},{7,5},{5,3},{3,1},{1,0},{8,10},{10,12},{12... | collective-permute-start | bytes 2555912 | tf_op jit(solution)/shard_map/ppermute | solution.py:55
  159.1 35.1 %collective-permute-start.19 = (bf16[256,1664]{1,0:T(8,128)(2,1)S(1)}, bf16[256,1664]{1,0:T(8,128)(2,1)S(1)}, u32[]{:S(2)}, u32[]{:S(2)}) collective-permute-start(bf16[256,1664]{1,0:T(8,128)(2,1)S(1)} %add_convert_fusion.3), channel_id=1, source_target_pairs={{0,16},{8,24},{16,0},{24,8},{1,17},{9,25},{17,1},{25,9},{2,18},{10... | collective-permute-start | bytes 2555912 | tf_op jit(solution)/shard_map/ppermute | solution.py:131
  172.8 36.5 %collective-permute-start.26 = (bf16[208,2048]{1,0:T(8,128)(2,1)}, bf16[208,2048]{1,0:T(8,128)(2,1)}, u32[]{:S(2)}, u32[]{:S(2)}) collective-permute-start(bf16[208,2048]{1,0:T(8,128)(2,1)} %collective-permute-done.24), channel_id=1, source_target_pairs={{0,1},{2,0},{4,2},{6,4},{7,6},{5,7},{3,5},{1,3},{8,9},{10,8},{12,1... | collective-permute-start | bytes 2555912 | tf_op jit(solution)/shard_map/ppermute | solution.py:56
  173.3 37.6 %collective-permute-start.33 = (bf16[208,2048]{1,0:T(8,128)(2,1)}, bf16[208,2048]{1,0:T(8,128)(2,1)}, u32[]{:S(2)}, u32[]{:S(2)}) collective-permute-start(bf16[208,2048]{1,0:T(8,128)(2,1)} %collective-permute-done.31), channel_id=1, source_target_pairs={{0,2},{2,4},{4,6},{6,7},{7,5},{5,3},{3,1},{1,0},{8,10},{10,12},{12... | collective-permute-start | bytes 2555912 | tf_op jit(solution)/shard_map/ppermute | solution.py:55
  191.0 36.4 %collective-permute-start.34 = (bf16[208,2048]{1,0:T(8,128)(2,1)}, bf16[208,2048]{1,0:T(8,128)(2,1)S(1)}, u32[]{:S(2)}, u32[]{:S(2)}) collective-permute-start(bf16[208,2048]{1,0:T(8,128)(2,1)} %collective-permute-done.32), channel_id=1, source_target_pairs={{0,1},{2,0},{4,2},{6,4},{7,6},{5,7},{3,5},{1,3},{8,9},{10,8},{12,1... | collective-permute-start | bytes 2555912 | tf_op jit(solution)/shard_map/ppermute | solution.py:56
  192.6 35.6 %collective-permute-start.27 = (bf16[208,1024]{1,0:T(8,128)(2,1)S(1)}, bf16[208,1024]{1,0:T(8,128)(2,1)S(1)}, u32[]{:S(2)}, u32[]{:S(2)}) collective-permute-start(bf16[208,1024]{1,0:T(8,128)(2,1)S(1)} %slice.117), channel_id=1, source_target_pairs={{0,2},{2,4},{4,6},{6,7},{7,5},{5,3},{3,1},{1,0},{8,10},{10,12},{12... | collective-permute-start | bytes 1277960 | tf_op jit(solution)/shard_map/ppermute | solution.py:62
  194.5 51.8 %collective-permute-start.20 = (bf16[256,1664]{1,0:T(8,128)(2,1)S(1)}, bf16[256,1664]{1,0:T(8,128)(2,1)S(1)}, u32[]{:S(2)}, u32[]{:S(2)}) collective-permute-start(bf16[256,1664]{1,0:T(8,128)(2,1)S(1)} %add_convert_fusion.2), channel_id=1, source_target_pairs={{0,8},{8,0},{16,24},{24,16},{1,9},{9,1},{17,25},{25,17},{2,10},{10... | collective-permute-start | bytes 2555912 | tf_op jit(solution)/shard_map/ppermute | solution.py:134
  210.3 26.2 %collective-permute-start.28 = (bf16[208,1024]{1,0:T(8,128)(2,1)S(1)}, bf16[208,1024]{1,0:T(8,128)(2,1)S(1)}, u32[]{:S(2)}, u32[]{:S(2)}) collective-permute-start(bf16[208,1024]{1,0:T(8,128)(2,1)S(1)} %slice.118), channel_id=1, source_target_pairs={{0,1},{2,0},{4,2},{6,4},{7,6},{5,7},{3,5},{1,3},{8,9},{10,8},{12,1... | collective-permute-start | bytes 1277960 | tf_op jit(solution)/shard_map/ppermute | solution.py:63
  211.9 24.7 %collective-permute-start.35 = (bf16[208,1024]{1,0:T(8,128)(2,1)S(1)}, bf16[208,1024]{1,0:T(8,128)(2,1)S(1)}, u32[]{:S(2)}, u32[]{:S(2)}) collective-permute-start(bf16[208,1024]{1,0:T(8,128)(2,1)S(1)} %slice.119), channel_id=1, source_target_pairs={{0,2},{2,4},{4,6},{6,7},{7,5},{5,3},{3,1},{1,0},{8,10},{10,12},{12... | collective-permute-start | bytes 1277960 | tf_op jit(solution)/shard_map/ppermute | solution.py:62
  227.4 19.0 %copy-start.15 = (bf16[208,2048]{1,0:T(8,128)(2,1)}, bf16[208,2048]{1,0:T(8,128)(2,1)S(1)}, u32[]{:S(2)}) copy-start(bf16[208,2048]{1,0:T(8,128)(2,1)S(1)} %collective-permute-done.34) | copy-start | bytes 2555908
  227.5 17.8 %collective-permute-start.36 = (bf16[208,1024]{1,0:T(8,128)(2,1)S(1)}, bf16[208,1024]{1,0:T(8,128)(2,1)S(1)}, u32[]{:S(2)}, u32[]{:S(2)}) collective-permute-start(bf16[208,1024]{1,0:T(8,128)(2,1)S(1)} %slice.120), channel_id=1, source_target_pairs={{0,1},{2,0},{4,2},{6,4},{7,6},{5,7},{3,5},{1,3},{8,9},{10,8},{12,1... | collective-permute-start | bytes 1277960 | tf_op jit(solution)/shard_map/ppermute | solution.py:63
  303.8 47.0 %collective-permute-start.37 = (f32[256,1664]{1,0:T(8,128)}, f32[256,1664]{1,0:T(8,128)}, u32[]{:S(2)}, u32[]{:S(2)}) collective-permute-start(f32[256,1664]{1,0:T(8,128)} %copy.101), channel_id=1, source_target_pairs={{0,8},{8,0},{16,24},{24,16},{1,9},{9,1},{17,25},{25,17},{2,10},{10... | collective-permute-start | bytes 5111816 | tf_op jit(solution)/shard_map/ppermute | solution.py:127
  305.4 42.2 %copy-start.3 = (bf16[832,512]{1,0:T(8,128)(2,1)}, bf16[832,512]{1,0:T(8,128)(2,1)S(1)}, u32[]{:S(2)}) copy-start(bf16[832,512]{1,0:T(8,128)(2,1)S(1)} %get-tuple-element.33) | copy-start | bytes 2555908
  305.4 24.0 %collective-permute-start.40 = (bf16[832,512]{1,0:T(8,128)(2,1)S(1)}, bf16[832,512]{1,0:T(8,128)(2,1)}, u32[]{:S(2)}, u32[]{:S(2)}) collective-permute-start(bf16[832,512]{1,0:T(8,128)(2,1)S(1)} %get-tuple-element.33), channel_id=1, source_target_pairs={{0,2},{2,4},{4,6},{6,7},{7,5},{5,3},{3,1},{1,0},{8,10},{10,12},{12... | collective-permute-start | bytes 2555912 | tf_op jit(solution)/shard_map/ppermute | solution.py:55
  307.0 21.9 %collective-permute-start.41 = (bf16[832,512]{1,0:T(8,128)(2,1)S(1)}, bf16[832,512]{1,0:T(8,128)(2,1)}, u32[]{:S(2)}, u32[]{:S(2)}) collective-permute-start(bf16[832,512]{1,0:T(8,128)(2,1)S(1)} %get-tuple-element.33), channel_id=1, source_target_pairs={{0,1},{2,0},{4,2},{6,4},{7,6},{5,7},{3,5},{1,3},{8,9},{10,8},{12,1... | collective-permute-start | bytes 2555912 | tf_op jit(solution)/shard_map/ppermute | solution.py:56
  307.5 39.7 %collective-permute-start.49 = (bf16[832,512]{1,0:T(8,128)(2,1)S(1)}, bf16[832,512]{1,0:T(8,128)(2,1)}, u32[]{:S(2)}, u32[]{:S(2)}) collective-permute-start(bf16[832,512]{1,0:T(8,128)(2,1)S(1)} %get-tuple-element.34), channel_id=1, source_target_pairs={{0,1},{2,0},{4,2},{6,4},{7,6},{5,7},{3,5},{1,3},{8,9},{10,8},{12,1... | collective-permute-start | bytes 2555912 | tf_op jit(solution)/shard_map/ppermute | solution.py:56
  307.9 39.7 %collective-permute-start.48 = (bf16[832,512]{1,0:T(8,128)(2,1)S(1)}, bf16[832,512]{1,0:T(8,128)(2,1)}, u32[]{:S(2)}, u32[]{:S(2)}) collective-permute-start(bf16[832,512]{1,0:T(8,128)(2,1)S(1)} %get-tuple-element.34), channel_id=1, source_target_pairs={{0,2},{2,4},{4,6},{6,7},{7,5},{5,3},{3,1},{1,0},{8,10},{10,12},{12... | collective-permute-start | bytes 2555912 | tf_op jit(solution)/shard_map/ppermute | solution.py:55
  328.9 36.5 %collective-permute-start.43 = (bf16[832,512]{1,0:T(8,128)(2,1)}, bf16[832,512]{1,0:T(8,128)(2,1)}, u32[]{:S(2)}, u32[]{:S(2)}) collective-permute-start(bf16[832,512]{1,0:T(8,128)(2,1)} %collective-permute-done.41), channel_id=1, source_target_pairs={{0,1},{2,0},{4,2},{6,4},{7,6},{5,7},{3,5},{1,3},{8,9},{10,8},{12,1... | collective-permute-start | bytes 2555912 | tf_op jit(solution)/shard_map/ppermute | solution.py:56
  329.3 36.5 %collective-permute-start.42 = (bf16[832,512]{1,0:T(8,128)(2,1)}, bf16[832,512]{1,0:T(8,128)(2,1)}, u32[]{:S(2)}, u32[]{:S(2)}) collective-permute-start(bf16[832,512]{1,0:T(8,128)(2,1)} %collective-permute-done.40), channel_id=1, source_target_pairs={{0,2},{2,4},{4,6},{6,7},{7,5},{5,3},{3,1},{1,0},{8,10},{10,12},{12... | collective-permute-start | bytes 2555912 | tf_op jit(solution)/shard_map/ppermute | solution.py:55
  347.2 36.5 %collective-permute-start.51 = (bf16[832,512]{1,0:T(8,128)(2,1)}, bf16[832,512]{1,0:T(8,128)(2,1)}, u32[]{:S(2)}, u32[]{:S(2)}) collective-permute-start(bf16[832,512]{1,0:T(8,128)(2,1)} %collective-permute-done.49), channel_id=1, source_target_pairs={{0,1},{2,0},{4,2},{6,4},{7,6},{5,7},{3,5},{1,3},{8,9},{10,8},{12,1... | collective-permute-start | bytes 2555912 | tf_op jit(solution)/shard_map/ppermute | solution.py:56
  347.6 36.5 %collective-permute-start.50 = (bf16[832,512]{1,0:T(8,128)(2,1)}, bf16[832,512]{1,0:T(8,128)(2,1)}, u32[]{:S(2)}, u32[]{:S(2)}) collective-permute-start(bf16[832,512]{1,0:T(8,128)(2,1)} %collective-permute-done.48), channel_id=1, source_target_pairs={{0,2},{2,4},{4,6},{6,7},{7,5},{5,3},{3,1},{1,0},{8,10},{10,12},{12... | collective-permute-start | bytes 2555912 | tf_op jit(solution)/shard_map/ppermute | solution.py:55
  350.9 35.8 %copy-start.31 = (s32[128,4]{0,1:T(4,128)S(1)}, s32[128,4]{0,1:T(4,128)}, u32[]{:S(2)}) copy-start(s32[128,4]{0,1:T(4,128)} %param.18) | copy-start | bytes 6148
  350.9 36.2 %copy-start.34 = (s32[32]{0:T(128)S(1)}, s32[32]{0:T(128)}, u32[]{:S(2)}) copy-start(s32[32]{0:T(128)} %param.17) | copy-start | bytes 388
  353.0 32.7 %collective-permute-start.38 = (bf16[256,1664]{1,0:T(8,128)(2,1)S(1)}, bf16[256,1664]{1,0:T(8,128)(2,1)S(1)}, u32[]{:S(2)}, u32[]{:S(2)}) collective-permute-start(bf16[256,1664]{1,0:T(8,128)(2,1)S(1)} %add_convert_fusion.1), channel_id=1, source_target_pairs={{0,16},{8,24},{16,0},{24,8},{1,17},{9,25},{17,1},{25,9},{2,18},{10... | collective-permute-start | bytes 2555912 | tf_op jit(solution)/shard_map/ppermute | solution.py:131
  365.4 37.2 %collective-permute-start.45 = (bf16[832,512]{1,0:T(8,128)(2,1)}, bf16[832,512]{1,0:T(8,128)(2,1)}, u32[]{:S(2)}, u32[]{:S(2)}) collective-permute-start(bf16[832,512]{1,0:T(8,128)(2,1)} %collective-permute-done.43), channel_id=1, source_target_pairs={{0,1},{2,0},{4,2},{6,4},{7,6},{5,7},{3,5},{1,3},{8,9},{10,8},{12,1... | collective-permute-start | bytes 2555912 | tf_op jit(solution)/shard_map/ppermute | solution.py:56
  365.9 34.3 %collective-permute-start.44 = (bf16[832,512]{1,0:T(8,128)(2,1)}, bf16[832,512]{1,0:T(8,128)(2,1)S(1)}, u32[]{:S(2)}, u32[]{:S(2)}) collective-permute-start(bf16[832,512]{1,0:T(8,128)(2,1)} %collective-permute-done.42), channel_id=1, source_target_pairs={{0,2},{2,4},{4,6},{6,7},{7,5},{5,3},{3,1},{1,0},{8,10},{10,12},{12... | collective-permute-start | bytes 2555912 | tf_op jit(solution)/shard_map/ppermute | solution.py:55
  383.7 38.3 %collective-permute-start.53 = (bf16[832,512]{1,0:T(8,128)(2,1)}, bf16[832,512]{1,0:T(8,128)(2,1)}, u32[]{:S(2)}, u32[]{:S(2)}) collective-permute-start(bf16[832,512]{1,0:T(8,128)(2,1)} %collective-permute-done.51), channel_id=1, source_target_pairs={{0,1},{2,0},{4,2},{6,4},{7,6},{5,7},{3,5},{1,3},{8,9},{10,8},{12,1... | collective-permute-start | bytes 2555912 | tf_op jit(solution)/shard_map/ppermute | solution.py:56
  384.1 34.4 %collective-permute-start.52 = (bf16[832,512]{1,0:T(8,128)(2,1)}, bf16[832,512]{1,0:T(8,128)(2,1)}, u32[]{:S(2)}, u32[]{:S(2)}) collective-permute-start(bf16[832,512]{1,0:T(8,128)(2,1)} %collective-permute-done.50), channel_id=1, source_target_pairs={{0,2},{2,4},{4,6},{6,7},{7,5},{5,3},{3,1},{1,0},{8,10},{10,12},{12... | collective-permute-start | bytes 2555912 | tf_op jit(solution)/shard_map/ppermute | solution.py:55
  386.6 37.6 %collective-permute-start.39 = (bf16[256,1664]{1,0:T(8,128)(2,1)S(1)}, bf16[256,1664]{1,0:T(8,128)(2,1)S(1)}, u32[]{:S(2)}, u32[]{:S(2)}) collective-permute-start(bf16[256,1664]{1,0:T(8,128)(2,1)S(1)} %add_convert_fusion), channel_id=1, source_target_pairs={{0,8},{8,0},{16,24},{24,16},{1,9},{9,1},{17,25},{25,17},{2,10},{10... | collective-permute-start | bytes 2555912 | tf_op jit(solution)/shard_map/ppermute | solution.py:134
  400.2 24.1 %copy-start.5 = (bf16[832,512]{1,0:T(8,128)(2,1)}, bf16[832,512]{1,0:T(8,128)(2,1)S(1)}, u32[]{:S(2)}) copy-start(bf16[832,512]{1,0:T(8,128)(2,1)S(1)} %collective-permute-done.44) | copy-start | bytes 2555908
  401.1 59.1 %collective-permute-start.46 = (bf16[832,256]{1,0:T(8,128)(2,1)}, bf16[832,256]{1,0:T(8,128)(2,1)}, u32[]{:S(2)}, u32[]{:S(2)}) collective-permute-start(bf16[832,256]{1,0:T(8,128)(2,1)} %slice.121), channel_id=1, source_target_pairs={{0,2},{2,4},{4,6},{6,7},{7,5},{5,3},{3,1},{1,0},{8,10},{10,12},{12... | collective-permute-start | bytes 1277960 | tf_op jit(solution)/shard_map/ppermute | solution.py:62
  404.4 55.7 %collective-permute-start.47 = (bf16[832,256]{1,0:T(8,128)(2,1)}, bf16[832,256]{1,0:T(8,128)(2,1)}, u32[]{:S(2)}, u32[]{:S(2)}) collective-permute-start(bf16[832,256]{1,0:T(8,128)(2,1)} %slice.122), channel_id=1, source_target_pairs={{0,1},{2,0},{4,2},{6,4},{7,6},{5,7},{3,5},{1,3},{8,9},{10,8},{12,1... | collective-permute-start | bytes 1277960 | tf_op jit(solution)/shard_map/ppermute | solution.py:63
  420.4 44.0 %collective-permute-start.54 = (bf16[832,256]{1,0:T(8,128)(2,1)}, bf16[832,256]{1,0:T(8,128)(2,1)}, u32[]{:S(2)}, u32[]{:S(2)}) collective-permute-start(bf16[832,256]{1,0:T(8,128)(2,1)} %slice.123), channel_id=1, source_target_pairs={{0,2},{2,4},{4,6},{6,7},{7,5},{5,3},{3,1},{1,0},{8,10},{10,12},{12... | collective-permute-start | bytes 1277960 | tf_op jit(solution)/shard_map/ppermute | solution.py:62
  423.7 40.6 %collective-permute-start.55 = (bf16[832,256]{1,0:T(8,128)(2,1)}, bf16[832,256]{1,0:T(8,128)(2,1)}, u32[]{:S(2)}, u32[]{:S(2)}) collective-permute-start(bf16[832,256]{1,0:T(8,128)(2,1)} %slice.124), channel_id=1, source_target_pairs={{0,1},{2,0},{4,2},{6,4},{7,6},{5,7},{3,5},{1,3},{8,9},{10,8},{12,1... | collective-permute-start | bytes 1277960 | tf_op jit(solution)/shard_map/ppermute | solution.py:63
  (30 other events, 149.4 us)

commit v2 on v1

--- a/solution.py
+++ b/solution.py
@@ -47,11 +47,16 @@
     def origin(self, offset):
         return self.walk_arr[lax.rem(self.here + offset + self.count, self.count)]
 
-    def gather(self, shard, split_axis):
+    def gather(self, shard, split_axis, use=None):
         n = self.count
         found = [(self.origin(0), shard)]
         cw = ccw = shard
+        total = None
         for step in range(1, (n - 1) // 2 + 1):
+            if use is not None and step > 1:
+                for index, block in found[max(0, 2 * step - 5) : 2 * step - 3]:
+                    total = use(total, index, block)
+                cw, ccw, total = lax.optimization_barrier((cw, ccw, total))
             cw = lax.ppermute(cw, "gy", self.right)
             ccw = lax.ppermute(ccw, "gy", self.left)
             found.append((self.origin(-step), cw))
@@ -63,7 +68,11 @@
         second = lax.ppermute(second, "gy", self.left)
         far = lax.concatenate([first, second], split_axis)
         found.append((self.origin(n // 2), far))
-        return found
+        if use is None:
+            return found
+        for index, block in found[max(0, 2 * ((n - 1) // 2) - 3) :]:
+            total = use(total, index, block)
+        return total
 
 
 def pick(stacked, index):
@@ -73,9 +82,13 @@
 def sum_chunks(left, found):
     total = None
     for index, shard in found:
-        term = jnp.dot(pick(left, index), shard, preferred_element_type=jnp.float32)
-        total = term if total is None else total + term
+        total = add_chunk(left, total, index, shard)
     return total
+
+
+def add_chunk(left, total, index, shard):
+    term = jnp.dot(pick(left, index), shard, preferred_element_type=jnp.float32)
+    return term if total is None else total + term
 
 
 def chunked(values, count):
@@ -245,11 +258,8 @@
 
     qkv_found = ring.gather(qkv_weight.reshape(qkv_weight.shape[0], -1), 1)
     out_found = ring.gather(out_weight.T, 1)
-    up_found = ring.gather(after(up_weight, qkv_found[-1][1]), 1)
     down_found = ring.gather(after(down_weight.T, out_found[-1][1]), 1)
-    half = merge_weight.shape[1] // 2
-    merge_a = ring.gather(after(merge_weight[:, :half], up_found[-1][1]), 1)
-    merge_b = ring.gather(after(merge_weight[:, half:], down_found[-1][1]), 1)
+    merge_full = lax.all_gather(merge_weight, "gy", axis=0, tiled=True)
 
     stream_full = gather_features(patches, gx)
     normed = layer_norm(stream_full.astype(jnp.float32)).astype(jnp.bfloat16)
@@ -259,7 +269,12 @@
     head_partial = place_columns(mixed, out_found, gy)
     stream_full = add_sum(head_partial, stream_full, gx)
     normed_two = layer_norm(stream_full.astype(jnp.float32)).astype(jnp.bfloat16)
-    hidden = sum_chunks(chunked(normed_two, gy), up_found)
+    left = chunked(normed_two, gy)
+
+    def use(total, index, block):
+        return add_chunk(left, total, index, block)
+
+    hidden = ring.gather(after(up_weight, qkv_found[-1][1]), 1, use)
     hidden = jax.nn.gelu(hidden, approximate=False).astype(jnp.bfloat16)
     unit_partial = place_columns(hidden, down_found, gy)
     final_full = add_sum(unit_partial, stream_full, gx)
@@ -276,8 +291,7 @@
     joined = jnp.take(final_full, local_index, axis=0).reshape(
         merge_index.shape[0], 4 * final_full.shape[1]
     )
-    chunks = chunked(joined, gy)
-    logits = jnp.concatenate([sum_chunks(chunks, merge_a), sum_chunks(chunks, merge_b)], axis=1)
+    logits = jnp.dot(joined, merge_full, preferred_element_type=jnp.float32)
     local_top = jnp.max(logits)
     request_sq, top_logit = reduce_scalars(request_part, local_top, gx, gy)
     return (logits.astype(jnp.bfloat16), jnp.sqrt(request_sq), top_logit)

time: 492 us -> 481 us (0.978)
  starting transfers between devices: 55.4 us -> 83.6 us
  matrix products: 83.1 us -> 59.4 us
  local copies, waits for them, and re-layouts: 55.4 us -> 33.2 us
  between operations: 23.6 us -> 35.8 us
    ppermute x18 -> x12, waiting for transfers between devices: 155 us -> 39.4 us  [gather(): ccw = lax.ppermute(ccw, 'gy', self.left)]
    ppermute x18 -> x12, waiting for transfers between devices: 52.2 us -> 141 us  [gather(): cw = lax.ppermute(cw, 'gy', self.right)]
    dot_general x32 -> x17, matrix products: 63.5 us -> 35.1 us  [the longest x16 26.7 us: add_chunk(): term = jnp.dot(pick(left, index), shard, preferred_element_type=jnp.float32)]
    ppermute x18 -> x12, starting transfers between devices: 28.5 us -> 49 us  [gather(): cw = lax.ppermute(cw, 'gy', self.right)]
    ppermute x2, waiting for transfers between devices: 0.01 us -> 19.9 us  [add_sum(): total = total + lax.ppermute(sent, 'gx', x_shift(gx, k)).astype(jnp.float32)]
    another operation x11 -> x2, local copies, waits for them, and re-layouts: 15.7 us -> 0.84 us
    ppermute x6 -> x4, waiting for transfers between devices: 3.49 us -> 17.6 us  [gather(): first = lax.ppermute(first, 'gy', self.right)]
    ppermute x6 -> x4, waiting for transfers between devices: 24.4 us -> 12.4 us  [gather(): second = lax.ppermute(second, 'gy', self.left)]
  transfers between devices with their start and end apart: 56 -> 41, of which waited for: 22 -> 22; matrix products, arithmetic and copies ran while one was open for 18% -> 19% of each run, Pallas kernels for 0% -> 0%
where the time goes in v2:
time: 481 us; the launch traced here: 474 us
  waiting for transfers between devices  238 us (49%)
  starting transfers between devices  83.6 us (17%)
  matrix products  59.4 us (12%)
  between operations  35.8 us (7%)
  local copies, waits for them, and re-layouts  33.2 us (7%)
  other arithmetic  12.9 us (3%)
  Pallas kernels  10.5 us (2%)
    ppermute x12, waiting for transfers between devices, gather(): cw = lax.ppermute(cw, 'gy', self.right)  141 us
    ppermute x12, starting transfers between devices, gather(): cw = lax.ppermute(cw, 'gy', self.right)  49 us
    ppermute x12, waiting for transfers between devices, gather(): ccw = lax.ppermute(ccw, 'gy', self.left)  39.4 us
    dot_general x16, matrix products, add_chunk(): term = jnp.dot(pick(left, index), shard, preferred_element_type=jnp.float32)  26.7 us
    dot_general x16, matrix products, place_columns(): lax.dot_general(left, shard, (((1,), (1,)), ((), ())), preferred_element_...  23 us
    ppermute x2, waiting for transfers between devices, add_sum(): total = total + lax.ppermute(sent, 'gx', x_shift(gx, k)).astype(jnp.float32)  19.9 us
    ppermute x4, starting transfers between devices, gather(): first = lax.ppermute(first, 'gy', self.right)  19.5 us
    ppermute x4, waiting for transfers between devices, gather(): first = lax.ppermute(first, 'gy', self.right)  17.6 us
  transfers between devices with their start and end apart: 41, of which 22 were waited for; matrix products, arithmetic and copies ran while one was open for 19% of the time, Pallas kernels for 0%

profile of v2, /device:TPU:0, one launch (start us, length us, event | category | flops | bytes accessed | tf_op | source)
XLA Modules:
  0.0 473.8 jit_solution(460547348702832150)
XLA Ops:
  7.3 3.0 collective-permute-start
  11.8 1.6 collective-permute-start.2
  13.9 1.6 collective-permute-start.10
  15.6 4.7 collective-permute-done
  20.4 1.8 collective-permute-start.11
  22.2 7.9 %collective-permute-done.10 = bf16[208,416]{0,1:T(8,128)(2,1)} collective-permute-done((bf16[208,416]{0,1:T(8,128)(2,1)}, bf16[208,416]{0,1:T(8,128)(2,1)}, u32[]{:S(2)}, u32[]{:S(2)}) %collective-permute-start.10) | collective-permute-done | bytes 173088 | tf_op jit(solution)/shard_map/ppermute | solution.py:60
  30.1 1.6 collective-permute-start.12
  32.2 4.1 collective-permute-done.12
  36.3 1.6 collective-permute-start.14
  38.3 1.6 collective-permute-start.4
  40.4 4.4 collective-permute-done.14
  44.8 1.5 slice.91
  46.3 1.6 collective-permute-start.16
  72.2 8.8 %collective-permute-done.17 = bf16[208,208]{0,1:T(8,128)(2,1)S(1)} collective-permute-done((bf16[208,208]{0,1:T(8,128)(2,1)S(1)}, bf16[208,208]{0,1:T(8,128)(2,1)S(1)}, u32[]{:S(2)}, u32[]{:S(2)}) %collective-permute-start.17) | collective-permute-done | bytes 86560 | tf_op jit(solution)/shard_map/ppermute | solution.py:68
  81.1 2.0 collective-permute-start.6
  86.8 1.6 convolution_add_fusion.2
  88.4 1.6 fusion.76
  90.7 13.9 %collective-permute-done.6 = bf16[208,1248]{1,0:T(8,128)(2,1)S(1)} collective-permute-done((bf16[208,1248]{1,0:T(8,128)(2,1)S(1)}, bf16[208,1248]{1,0:T(8,128)(2,1)S(1)}, u32[]{:S(2)}, u32[]{:S(2)}) %collective-permute-start.6) | collective-permute-done | bytes 519200 | tf_op jit(solution)/shard_map/ppermute | solution.py:60
  104.6 14.5 %collective-permute-start.8 = (bf16[208,624]{1,0:T(8,128)(2,1)S(1)}, bf16[208,624]{1,0:T(8,128)(2,1)S(1)}, u32[]{:S(2)}, u32[]{:S(2)}) collective-permute-start(bf16[208,624]{1,0:T(8,128)(2,1)S(1)} %slice.86), channel_id=1, source_target_pairs={{0,2},{2,4},{4,6},{6,7},{7,5},{5,3},{3,1},{1,0},{8,10},{10,12},{12... | collective-permute-start | bytes 778760 | tf_op jit(solution)/shard_map/ppermute | solution.py:67
  119.2 2.1 collective-permute-start.9
  121.8 4.2 collective-permute-done.8
  126.0 2.0 collective-permute-done.9
  130.3 2.1 fusion.122
  142.6 1.7 copy.75
  144.3 1.7 collective-permute-start.29
  148.2 1.6 add_convert_fusion.3
  151.3 33.2 %collective-permute-done.29 = bf16[208,2048]{1,0:T(8,128)(2,1)} collective-permute-done((bf16[208,2048]{1,0:T(8,128)(2,1)}, bf16[208,2048]{1,0:T(8,128)(2,1)}, u32[]{:S(2)}, u32[]{:S(2)}) %collective-permute-start.29) | collective-permute-done | bytes 852000 | tf_op jit(solution)/shard_map/ppermute | solution.py:60
  184.5 19.2 %collective-permute-start.31 = (bf16[208,2048]{1,0:T(8,128)(2,1)}, bf16[208,2048]{1,0:T(8,128)(2,1)}, u32[]{:S(2)}, u32[]{:S(2)}) collective-permute-start(bf16[208,2048]{1,0:T(8,128)(2,1)} %collective-permute-done.29), channel_id=1, source_target_pairs={{0,2},{2,4},{4,6},{6,7},{7,5},{5,3},{3,1},{1,0},{8,10},{10,12},{12... | collective-permute-start | bytes 2555912 | tf_op jit(solution)/shard_map/ppermute | solution.py:60
  203.7 1.8 collective-permute-done.30
  205.8 2.1 collective-permute-start.21
  207.9 33.9 %collective-permute-done.31 = bf16[208,2048]{1,0:T(8,128)(2,1)} collective-permute-done((bf16[208,2048]{1,0:T(8,128)(2,1)}, bf16[208,2048]{1,0:T(8,128)(2,1)}, u32[]{:S(2)}, u32[]{:S(2)}) %collective-permute-start.31) | collective-permute-done | bytes 852000 | tf_op jit(solution)/shard_map/ppermute | solution.py:60
  241.8 14.5 %collective-permute-start.33 = (bf16[208,2048]{1,0:T(8,128)(2,1)}, bf16[208,2048]{1,0:T(8,128)(2,1)}, u32[]{:S(2)}, u32[]{:S(2)}) collective-permute-start(bf16[208,2048]{1,0:T(8,128)(2,1)} %collective-permute-done.31), channel_id=1, source_target_pairs={{0,2},{2,4},{4,6},{6,7},{7,5},{5,3},{3,1},{1,0},{8,10},{10,12},{12... | collective-permute-start | bytes 2555912 | tf_op jit(solution)/shard_map/ppermute | solution.py:60
  256.3 11.6 %collective-permute-done.32 = bf16[208,2048]{1,0:T(8,128)(2,1)} collective-permute-done((bf16[208,2048]{1,0:T(8,128)(2,1)}, bf16[208,2048]{1,0:T(8,128)(2,1)}, u32[]{:S(2)}, u32[]{:S(2)}) %collective-permute-start.32) | collective-permute-done | bytes 852000 | tf_op jit(solution)/shard_map/ppermute | solution.py:61
  270.4 1.9 fusion.69
  273.7 24.2 %collective-permute-done.22 = bf16[208,2048]{1,0:T(8,128)(2,1)} collective-permute-done((bf16[208,2048]{1,0:T(8,128)(2,1)}, bf16[208,2048]{1,0:T(8,128)(2,1)}, u32[]{:S(2)}, u32[]{:S(2)}) %collective-permute-start.22) | collective-permute-done | bytes 852000 | tf_op jit(solution)/shard_map/ppermute | solution.py:61
  297.9 2.0 collective-permute-start.24
  299.9 1.9 fusion.67
  301.8 2.0 add_add_fusion.1
  303.8 28.3 %collective-permute-done.23 = bf16[208,2048]{1,0:T(8,128)(2,1)S(1)} collective-permute-done((bf16[208,2048]{1,0:T(8,128)(2,1)}, bf16[208,2048]{1,0:T(8,128)(2,1)S(1)}, u32[]{:S(2)}, u32[]{:S(2)}) %collective-permute-start.23) | collective-permute-done | bytes 852000 | tf_op jit(solution)/shard_map/ppermute | solution.py:60
  332.1 1.9 collective-permute-done.24
  334.0 1.6 collective-permute-start.25
  337.1 1.8 collective-permute-start.35
  342.0 13.9 %collective-permute-done.25 = bf16[208,2048]{1,0:T(8,128)(2,1)S(1)} collective-permute-done((bf16[208,2048]{1,0:T(8,128)(2,1)S(1)}, bf16[208,2048]{1,0:T(8,128)(2,1)S(1)}, u32[]{:S(2)}, u32[]{:S(2)}) %collective-permute-start.25) | collective-permute-done | bytes 852000 | tf_op jit(solution)/shard_map/ppermute | solution.py:60
  355.9 1.6 collective-permute-start.27
  359.6 13.4 %collective-permute-done.27 = bf16[208,1024]{1,0:T(8,128)(2,1)S(1)} collective-permute-done((bf16[208,1024]{1,0:T(8,128)(2,1)S(1)}, bf16[208,1024]{1,0:T(8,128)(2,1)S(1)}, u32[]{:S(2)}, u32[]{:S(2)}) %collective-permute-start.27) | collective-permute-done | bytes 426016 | tf_op jit(solution)/shard_map/ppermute | solution.py:67
  372.9 1.5 collective-permute-done.28
  374.4 11.2 %fusion.3 = bf16[512,2048]{1,0:T(8,128)(2,1)S(1)} fusion(f32[512,2048]{1,0:T(8,128)S(1)} %fusion.55, f32[512,2048]{1,0:T(8,128)S(1)} %fusion.57, f32[512,2048]{1,0:T(8,128)S(1)} %fusion.59, f32[512,2048]{1,0:T(8,128)S(1)} %add_add_fusion.1, f32[512,2048]{1,0:T(8,128)S(1)} %fusion.61, bf16[208,1024]{1,0:T(8,128)(2,1)S(1)} %collective-permute-done.28, ...), kind=kOutput, calls=%fused_computation.7 | convolution fusion | flops 511311872 | bytes 24133636 | tf_op jit(solution)/shard_map/dot_general | solution.py:90
  387.6 2.0 fusion.39
  389.6 2.0 fusion.38
  391.7 2.0 fusion.37
  393.7 2.0 fusion.36
  395.7 2.0 fusion.35
  397.7 2.0 fusion.34
  399.7 2.0 fusion.33
  401.7 1.6 constant_dynamic-slice_fusion
  403.3 2.7 copy.77
  406.0 1.7 copy.76
  407.6 2.3 collective-permute-done.37
  409.9 2.1 add_convert_fusion.1
  413.1 19.9 %collective-permute-done.38 = bf16[256,1664]{1,0:T(8,128)(2,1)S(1)} collective-permute-done((bf16[256,1664]{1,0:T(8,128)(2,1)S(1)}, bf16[256,1664]{1,0:T(8,128)(2,1)S(1)}, u32[]{:S(2)}, u32[]{:S(2)}) %collective-permute-start.38) | collective-permute-done | bytes 852000 | tf_op jit(solution)/shard_map/ppermute | solution.py:144
  436.7 3.1 gather_fusion
  439.8 3.2 gather.7
  443.8 8.4 %fusion.120 = (f32[]{:T(128)}, bf16[128,1024]{1,0:T(8,128)(2,1)}) fusion(bf16[6656,1024]{1,0:T(8,128)(2,1)} %all-gather.2.cloned.1.call-done, pred[128,6656]{1,0:T(8,128)(4,1)} %bitcast.244, bf16[128,6656]{1,0:T(8,128)(2,1)S(1)} %gather.7), kind=kOutput, calls=%fused_computation.203 | convolution fusion | flops 1745944576 | bytes 16449540 | tf_op jit(solution)/shard_map/dot_general | solution.py:294
  453.7 10.5 %scalar_sums.1 = f32[8,128]{1,0:T(8,128)} custom-call(f32[8,128]{1,0:T(8,128)} %copy-done.6), custom_call_target="tpu_custom_call" | custom-call | tf_op jit(solution)/shard_map/scalar_sums/pallas_call | solution.py:209
  (143 shorter events, 50.6 us)
Async XLA Ops:
  7.2 8.4 %copy-start.1 = (bf16[512,416]{0,1:T(8,128)(2,1)S(1)}, bf16[512,416]{0,1:T(8,128)(2,1)}, u32[]{:S(2)}) copy-start(bf16[512,416]{0,1:T(8,128)(2,1)} %param.15) | copy-start | bytes 1277956
  7.2 41.7 %copy-start.10 = (s32[8]{0:T(128)S(1)}, s32[8]{0:T(128)}, u32[]{:S(2)}) copy-start(s32[8]{0:T(128)} %constant.327.clone) | copy-start | bytes 100
  7.2 47.5 %copy-start.4 = (s32[8]{0:T(128)S(1)}, s32[8]{0:T(128)}, u32[]{:S(2)}) copy-start(s32[8]{0:T(128)} %constant.326.clone) | copy-start | bytes 100
  7.2 40.7 %copy-start.5 = (s32[512]{0:T(512)S(1)}, s32[512]{0:T(512)}, u32[]{:S(2)}) copy-start(s32[512]{0:T(512)} %param.16) | copy-start | bytes 6148
  7.2 436.6 %all-gather.2.cloned.1.call-start = ((), (), s32[]{:S(2)}) async-start(), calls=%async_computation | async-start | bytes 15335424 | tf_op jit(solution)/shard_map/all_gather | solution.py:262
  7.3 13.0 %collective-permute-start = (bf16[512,416]{0,1:T(8,128)(2,1)}, bf16[512,416]{0,1:T(8,128)(2,1)S(1)}, u32[]{:S(2)}, u32[]{:S(2)}) collective-permute-start(bf16[512,416]{0,1:T(8,128)(2,1)} %param.15), channel_id=1, source_target_pairs={{0,16},{8,24},{16,0},{24,8},{1,17},{9,25},{17,1},{25,9},{2,18},{10... | collective-permute-start | bytes 1277960 | tf_op jit(solution)/shard_map/ppermute | solution.py:126
  11.8 26.5 %collective-permute-start.2 = (bf16[208,1248]{1,0:T(8,128)(2,1)S(1)}, bf16[208,1248]{1,0:T(8,128)(2,1)S(1)}, u32[]{:S(2)}, u32[]{:S(2)}) collective-permute-start(bf16[208,1248]{1,0:T(8,128)(2,1)S(1)} %copy.62), channel_id=1, source_target_pairs={{0,2},{2,4},{4,6},{6,7},{7,5},{5,3},{3,1},{1,0},{8,10},{10,12},{12... | collective-permute-start | bytes 1557512 | tf_op jit(solution)/shard_map/ppermute | solution.py:60
  13.5 24.4 %collective-permute-start.3 = (bf16[208,1248]{1,0:T(8,128)(2,1)S(1)}, bf16[208,1248]{1,0:T(8,128)(2,1)}, u32[]{:S(2)}, u32[]{:S(2)}) collective-permute-start(bf16[208,1248]{1,0:T(8,128)(2,1)S(1)} %copy.62), channel_id=1, source_target_pairs={{0,1},{2,0},{4,2},{6,4},{7,6},{5,7},{3,5},{1,3},{8,9},{10,8},{12,1... | collective-permute-start | bytes 1557512 | tf_op jit(solution)/shard_map/ppermute | solution.py:61
  13.9 16.2 %collective-permute-start.10 = (bf16[208,416]{0,1:T(8,128)(2,1)}, bf16[208,416]{0,1:T(8,128)(2,1)}, u32[]{:S(2)}, u32[]{:S(2)}) collective-permute-start(bf16[208,416]{0,1:T(8,128)(2,1)} %bitcast.245), channel_id=1, source_target_pairs={{0,2},{2,4},{4,6},{6,7},{7,5},{5,3},{3,1},{1,0},{8,10},{10,12},{12... | collective-permute-start | bytes 519176 | tf_op jit(solution)/shard_map/ppermute | solution.py:60
  20.3 62.8 %collective-permute-start.1 = (bf16[2,512,416]{1,2,0:T(8,128)(2,1)S(1)}, bf16[2,512,416]{1,2,0:T(8,128)(2,1)S(1)}, u32[]{:S(2)}, u32[]{:S(2)}) collective-permute-start(bf16[2,512,416]{1,2,0:T(8,128)(2,1)S(1)} %bitcast_dynamic-update-slice_fusion), channel_id=1, source_target_pairs={{0,8},{8,0},{16,24},{24,16},{1,9},{9,1},{17,25},{25,17},{2,10},{10... | collective-permute-start | bytes 2555912 | tf_op jit(solution)/shard_map/ppermute | solution.py:128
  20.4 11.3 %collective-permute-start.11 = (bf16[208,416]{0,1:T(8,128)(2,1)}, bf16[208,416]{0,1:T(8,128)(2,1)}, u32[]{:S(2)}, u32[]{:S(2)}) collective-permute-start(bf16[208,416]{0,1:T(8,128)(2,1)} %bitcast.246), channel_id=1, source_target_pairs={{0,1},{2,0},{4,2},{6,4},{7,6},{5,7},{3,5},{1,3},{8,9},{10,8},{12,1... | collective-permute-start | bytes 519176 | tf_op jit(solution)/shard_map/ppermute | solution.py:61
  30.1 6.2 %collective-permute-start.12 = (bf16[208,416]{0,1:T(8,128)(2,1)}, bf16[208,416]{0,1:T(8,128)(2,1)}, u32[]{:S(2)}, u32[]{:S(2)}) collective-permute-start(bf16[208,416]{0,1:T(8,128)(2,1)} %collective-permute-done.10), channel_id=1, source_target_pairs={{0,2},{2,4},{4,6},{6,7},{7,5},{5,3},{3,1},{1,0},{8,10},{10,12},{12... | collective-permute-start | bytes 519176 | tf_op jit(solution)/shard_map/ppermute | solution.py:60
  31.7 8.2 %collective-permute-start.13 = (bf16[208,416]{0,1:T(8,128)(2,1)}, bf16[208,416]{0,1:T(8,128)(2,1)}, u32[]{:S(2)}, u32[]{:S(2)}) collective-permute-start(bf16[208,416]{0,1:T(8,128)(2,1)} %collective-permute-done.11), channel_id=1, source_target_pairs={{0,1},{2,0},{4,2},{6,4},{7,6},{5,7},{3,5},{1,3},{8,9},{10,8},{12,1... | collective-permute-start | bytes 519176 | tf_op jit(solution)/shard_map/ppermute | solution.py:61
  36.3 8.5 %collective-permute-start.14 = (bf16[208,416]{0,1:T(8,128)(2,1)}, bf16[208,416]{0,1:T(8,128)(2,1)}, u32[]{:S(2)}, u32[]{:S(2)}) collective-permute-start(bf16[208,416]{0,1:T(8,128)(2,1)} %collective-permute-done.12), channel_id=1, source_target_pairs={{0,2},{2,4},{4,6},{6,7},{7,5},{5,3},{3,1},{1,0},{8,10},{10,12},{12... | collective-permute-start | bytes 519176 | tf_op jit(solution)/shard_map/ppermute | solution.py:60
  37.9 43.1 %collective-permute-start.5 = (bf16[208,1248]{1,0:T(8,128)(2,1)}, bf16[208,1248]{1,0:T(8,128)(2,1)}, u32[]{:S(2)}, u32[]{:S(2)}) collective-permute-start(bf16[208,1248]{1,0:T(8,128)(2,1)} %collective-permute-done.3), channel_id=1, source_target_pairs={{0,1},{2,0},{4,2},{6,4},{7,6},{5,7},{3,5},{1,3},{8,9},{10,8},{12,1... | collective-permute-start | bytes 1557512 | tf_op jit(solution)/shard_map/ppermute | solution.py:61
  38.3 42.7 %collective-permute-start.4 = (bf16[208,1248]{1,0:T(8,128)(2,1)S(1)}, bf16[208,1248]{1,0:T(8,128)(2,1)S(1)}, u32[]{:S(2)}, u32[]{:S(2)}) collective-permute-start(bf16[208,1248]{1,0:T(8,128)(2,1)S(1)} %collective-permute-done.2), channel_id=1, source_target_pairs={{0,2},{2,4},{4,6},{6,7},{7,5},{5,3},{3,1},{1,0},{8,10},{10,12},{12... | collective-permute-start | bytes 1557512 | tf_op jit(solution)/shard_map/ppermute | solution.py:60
  39.9 30.8 %collective-permute-start.15 = (bf16[208,416]{0,1:T(8,128)(2,1)}, bf16[208,416]{0,1:T(8,128)(2,1)}, u32[]{:S(2)}, u32[]{:S(2)}) collective-permute-start(bf16[208,416]{0,1:T(8,128)(2,1)} %collective-permute-done.13), channel_id=1, source_target_pairs={{0,1},{2,0},{4,2},{6,4},{7,6},{5,7},{3,5},{1,3},{8,9},{10,8},{12,1... | collective-permute-start | bytes 519176 | tf_op jit(solution)/shard_map/ppermute | solution.py:61
  46.3 25.8 %collective-permute-start.16 = (bf16[208,208]{0,1:T(8,128)(2,1)}, bf16[208,208]{0,1:T(8,128)(2,1)S(1)}, u32[]{:S(2)}, u32[]{:S(2)}) collective-permute-start(bf16[208,208]{0,1:T(8,128)(2,1)} %slice.91), channel_id=1, source_target_pairs={{0,2},{2,4},{4,6},{6,7},{7,5},{5,3},{3,1},{1,0},{8,10},{10,12},{12... | collective-permute-start | bytes 259592 | tf_op jit(solution)/shard_map/ppermute | solution.py:67
  71.7 9.3 %collective-permute-start.17 = (bf16[208,208]{0,1:T(8,128)(2,1)S(1)}, bf16[208,208]{0,1:T(8,128)(2,1)S(1)}, u32[]{:S(2)}, u32[]{:S(2)}) collective-permute-start(bf16[208,208]{0,1:T(8,128)(2,1)S(1)} %slice.92), channel_id=1, source_target_pairs={{0,1},{2,0},{4,2},{6,4},{7,6},{5,7},{3,5},{1,3},{8,9},{10,8},{12,1... | collective-permute-start | bytes 259592 | tf_op jit(solution)/shard_map/ppermute | solution.py:68
  81.0 38.1 %collective-permute-start.7 = (bf16[208,1248]{1,0:T(8,128)(2,1)}, bf16[208,1248]{1,0:T(8,128)(2,1)S(1)}, u32[]{:S(2)}, u32[]{:S(2)}) collective-permute-start(bf16[208,1248]{1,0:T(8,128)(2,1)} %collective-permute-done.5), channel_id=1, source_target_pairs={{0,1},{2,0},{4,2},{6,4},{7,6},{5,7},{3,5},{1,3},{8,9},{10,8},{12,1... | collective-permute-start | bytes 1557512 | tf_op jit(solution)/shard_map/ppermute | solution.py:61
  81.1 23.5 %collective-permute-start.6 = (bf16[208,1248]{1,0:T(8,128)(2,1)S(1)}, bf16[208,1248]{1,0:T(8,128)(2,1)S(1)}, u32[]{:S(2)}, u32[]{:S(2)}) collective-permute-start(bf16[208,1248]{1,0:T(8,128)(2,1)S(1)} %collective-permute-done.4), channel_id=1, source_target_pairs={{0,2},{2,4},{4,6},{6,7},{7,5},{5,3},{3,1},{1,0},{8,10},{10,12},{12... | collective-permute-start | bytes 1557512 | tf_op jit(solution)/shard_map/ppermute | solution.py:60
  104.6 21.5 %collective-permute-start.8 = (bf16[208,624]{1,0:T(8,128)(2,1)S(1)}, bf16[208,624]{1,0:T(8,128)(2,1)S(1)}, u32[]{:S(2)}, u32[]{:S(2)}) collective-permute-start(bf16[208,624]{1,0:T(8,128)(2,1)S(1)} %slice.86), channel_id=1, source_target_pairs={{0,2},{2,4},{4,6},{6,7},{7,5},{5,3},{3,1},{1,0},{8,10},{10,12},{12... | collective-permute-start | bytes 778760 | tf_op jit(solution)/shard_map/ppermute | solution.py:67
  119.2 8.8 %collective-permute-start.9 = (bf16[208,624]{1,0:T(8,128)(2,1)S(1)}, bf16[208,624]{1,0:T(8,128)(2,1)S(1)}, u32[]{:S(2)}, u32[]{:S(2)}) collective-permute-start(bf16[208,624]{1,0:T(8,128)(2,1)S(1)} %slice.87), channel_id=1, source_target_pairs={{0,1},{2,0},{4,2},{6,4},{7,6},{5,7},{3,5},{1,3},{8,9},{10,8},{12,1... | collective-permute-start | bytes 778760 | tf_op jit(solution)/shard_map/ppermute | solution.py:68
  129.4 1.0 copy-start.2
  132.9 1.0 copy-start.3
  144.3 3.9 collective-permute-start.18
  144.3 40.2 %collective-permute-start.29 = (bf16[208,2048]{1,0:T(8,128)(2,1)}, bf16[208,2048]{1,0:T(8,128)(2,1)}, u32[]{:S(2)}, u32[]{:S(2)}) collective-permute-start(bf16[208,2048]{1,0:T(8,128)(2,1)} %bitcast.249), channel_id=1, source_target_pairs={{0,2},{2,4},{4,6},{6,7},{7,5},{5,3},{3,1},{1,0},{8,10},{10,12},{12... | collective-permute-start | bytes 2555912 | tf_op jit(solution)/shard_map/ppermute | solution.py:60
  146.0 59.5 %collective-permute-start.30 = (bf16[208,2048]{1,0:T(8,128)(2,1)}, bf16[208,2048]{1,0:T(8,128)(2,1)}, u32[]{:S(2)}, u32[]{:S(2)}) collective-permute-start(bf16[208,2048]{1,0:T(8,128)(2,1)} %bitcast.250), channel_id=1, source_target_pairs={{0,1},{2,0},{4,2},{6,4},{7,6},{5,7},{3,5},{1,3},{8,9},{10,8},{12,1... | collective-permute-start | bytes 2555912 | tf_op jit(solution)/shard_map/ppermute | solution.py:61
  147.1 3.5 copy-start
  149.8 55.6 %collective-permute-start.19 = (bf16[256,1664]{1,0:T(8,128)(2,1)S(1)}, bf16[256,1664]{1,0:T(8,128)(2,1)S(1)}, u32[]{:S(2)}, u32[]{:S(2)}) collective-permute-start(bf16[256,1664]{1,0:T(8,128)(2,1)S(1)} %add_convert_fusion.3), channel_id=1, source_target_pairs={{0,16},{8,24},{16,0},{24,8},{1,17},{9,25},{17,1},{25,9},{2,18},{10... | collective-permute-start | bytes 2555912 | tf_op jit(solution)/shard_map/ppermute | solution.py:144
  184.5 57.3 %collective-permute-start.31 = (bf16[208,2048]{1,0:T(8,128)(2,1)}, bf16[208,2048]{1,0:T(8,128)(2,1)}, u32[]{:S(2)}, u32[]{:S(2)}) collective-permute-start(bf16[208,2048]{1,0:T(8,128)(2,1)} %collective-permute-done.29), channel_id=1, source_target_pairs={{0,2},{2,4},{4,6},{6,7},{7,5},{5,3},{3,1},{1,0},{8,10},{10,12},{12... | collective-permute-start | bytes 2555912 | tf_op jit(solution)/shard_map/ppermute | solution.py:60
  205.4 62.5 %collective-permute-start.32 = (bf16[208,2048]{1,0:T(8,128)(2,1)}, bf16[208,2048]{1,0:T(8,128)(2,1)}, u32[]{:S(2)}, u32[]{:S(2)}) collective-permute-start(bf16[208,2048]{1,0:T(8,128)(2,1)} %collective-permute-done.30), channel_id=1, source_target_pairs={{0,1},{2,0},{4,2},{6,4},{7,6},{5,7},{3,5},{1,3},{8,9},{10,8},{12,1... | collective-permute-start | bytes 2555912 | tf_op jit(solution)/shard_map/ppermute | solution.py:61
  205.7 62.2 %collective-permute-start.20 = (bf16[256,1664]{1,0:T(8,128)(2,1)S(1)}, bf16[256,1664]{1,0:T(8,128)(2,1)S(1)}, u32[]{:S(2)}, u32[]{:S(2)}) collective-permute-start(bf16[256,1664]{1,0:T(8,128)(2,1)S(1)} %add_convert_fusion.2), channel_id=1, source_target_pairs={{0,8},{8,0},{16,24},{24,16},{1,9},{9,1},{17,25},{25,17},{2,10},{10... | collective-permute-start | bytes 2555912 | tf_op jit(solution)/shard_map/ppermute | solution.py:147
  205.8 67.9 %collective-permute-start.21 = (bf16[208,2048]{1,0:T(8,128)(2,1)}, bf16[208,2048]{1,0:T(8,128)(2,1)}, u32[]{:S(2)}, u32[]{:S(2)}) collective-permute-start(bf16[208,2048]{1,0:T(8,128)(2,1)} %param.21), channel_id=1, source_target_pairs={{0,2},{2,4},{4,6},{6,7},{7,5},{5,3},{3,1},{1,0},{8,10},{10,12},{12... | collective-permute-start | bytes 2555912 | tf_op jit(solution)/shard_map/ppermute | solution.py:60
  207.9 90.0 %collective-permute-start.22 = (bf16[208,2048]{1,0:T(8,128)(2,1)}, bf16[208,2048]{1,0:T(8,128)(2,1)}, u32[]{:S(2)}, u32[]{:S(2)}) collective-permute-start(bf16[208,2048]{1,0:T(8,128)(2,1)} %param.21), channel_id=1, source_target_pairs={{0,1},{2,0},{4,2},{6,4},{7,6},{5,7},{3,5},{1,3},{8,9},{10,8},{12,1... | collective-permute-start | bytes 2555912 | tf_op jit(solution)/shard_map/ppermute | solution.py:61
  241.8 94.2 %collective-permute-start.33 = (bf16[208,2048]{1,0:T(8,128)(2,1)}, bf16[208,2048]{1,0:T(8,128)(2,1)}, u32[]{:S(2)}, u32[]{:S(2)}) collective-permute-start(bf16[208,2048]{1,0:T(8,128)(2,1)} %collective-permute-done.31), channel_id=1, source_target_pairs={{0,2},{2,4},{4,6},{6,7},{7,5},{5,3},{3,1},{1,0},{8,10},{10,12},{12... | collective-permute-start | bytes 2555912 | tf_op jit(solution)/shard_map/ppermute | solution.py:60
  267.9 71.0 %collective-permute-start.34 = (bf16[208,2048]{1,0:T(8,128)(2,1)}, bf16[208,2048]{1,0:T(8,128)(2,1)}, u32[]{:S(2)}, u32[]{:S(2)}) collective-permute-start(bf16[208,2048]{1,0:T(8,128)(2,1)} %collective-permute-done.32), channel_id=1, source_target_pairs={{0,1},{2,0},{4,2},{6,4},{7,6},{5,7},{3,5},{1,3},{8,9},{10,8},{12,1... | collective-permute-start | bytes 2555912 | tf_op jit(solution)/shard_map/ppermute | solution.py:61
  297.9 34.2 %collective-permute-start.23 = (bf16[208,2048]{1,0:T(8,128)(2,1)}, bf16[208,2048]{1,0:T(8,128)(2,1)S(1)}, u32[]{:S(2)}, u32[]{:S(2)}) collective-permute-start(bf16[208,2048]{1,0:T(8,128)(2,1)} %collective-permute-done.21), channel_id=1, source_target_pairs={{0,2},{2,4},{4,6},{6,7},{7,5},{5,3},{3,1},{1,0},{8,10},{10,12},{12... | collective-permute-start | bytes 2555912 | tf_op jit(solution)/shard_map/ppermute | solution.py:60
  297.9 36.1 %collective-permute-start.24 = (bf16[208,2048]{1,0:T(8,128)(2,1)}, bf16[208,2048]{1,0:T(8,128)(2,1)S(1)}, u32[]{:S(2)}, u32[]{:S(2)}) collective-permute-start(bf16[208,2048]{1,0:T(8,128)(2,1)} %collective-permute-done.22), channel_id=1, source_target_pairs={{0,1},{2,0},{4,2},{6,4},{7,6},{5,7},{3,5},{1,3},{8,9},{10,8},{12,1... | collective-permute-start | bytes 2555912 | tf_op jit(solution)/shard_map/ppermute | solution.py:61
  334.0 21.8 %collective-permute-start.25 = (bf16[208,2048]{1,0:T(8,128)(2,1)S(1)}, bf16[208,2048]{1,0:T(8,128)(2,1)S(1)}, u32[]{:S(2)}, u32[]{:S(2)}) collective-permute-start(bf16[208,2048]{1,0:T(8,128)(2,1)S(1)} %collective-permute-done.23), channel_id=1, source_target_pairs={{0,2},{2,4},{4,6},{6,7},{7,5},{5,3},{3,1},{1,0},{8,10},{10,12},{12... | collective-permute-start | bytes 2555912 | tf_op jit(solution)/shard_map/ppermute | solution.py:60
  335.6 21.9 %collective-permute-start.26 = (bf16[208,2048]{1,0:T(8,128)(2,1)S(1)}, bf16[208,2048]{1,0:T(8,128)(2,1)S(1)}, u32[]{:S(2)}, u32[]{:S(2)}) collective-permute-start(bf16[208,2048]{1,0:T(8,128)(2,1)S(1)} %collective-permute-done.24), channel_id=1, source_target_pairs={{0,1},{2,0},{4,2},{6,4},{7,6},{5,7},{3,5},{1,3},{8,9},{10,8},{12,1... | collective-permute-start | bytes 2555912 | tf_op jit(solution)/shard_map/ppermute | solution.py:61
  337.1 62.6 %collective-permute-start.35 = (bf16[208,1024]{1,0:T(8,128)(2,1)S(1)}, bf16[208,1024]{1,0:T(8,128)(2,1)}, u32[]{:S(2)}, u32[]{:S(2)}) collective-permute-start(bf16[208,1024]{1,0:T(8,128)(2,1)S(1)} %slice.95), channel_id=1, source_target_pairs={{0,2},{2,4},{4,6},{6,7},{7,5},{5,3},{3,1},{1,0},{8,10},{10,12},{12... | collective-permute-start | bytes 1277960 | tf_op jit(solution)/shard_map/ppermute | solution.py:67
  340.0 59.7 %collective-permute-start.36 = (bf16[208,1024]{1,0:T(8,128)(2,1)S(1)}, bf16[208,1024]{1,0:T(8,128)(2,1)}, u32[]{:S(2)}, u32[]{:S(2)}) collective-permute-start(bf16[208,1024]{1,0:T(8,128)(2,1)S(1)} %slice.96), channel_id=1, source_target_pairs={{0,1},{2,0},{4,2},{6,4},{7,6},{5,7},{3,5},{1,3},{8,9},{10,8},{12,1... | collective-permute-start | bytes 1277960 | tf_op jit(solution)/shard_map/ppermute | solution.py:68
  355.9 17.0 %collective-permute-start.27 = (bf16[208,1024]{1,0:T(8,128)(2,1)S(1)}, bf16[208,1024]{1,0:T(8,128)(2,1)S(1)}, u32[]{:S(2)}, u32[]{:S(2)}) collective-permute-start(bf16[208,1024]{1,0:T(8,128)(2,1)S(1)} %slice.93), channel_id=1, source_target_pairs={{0,2},{2,4},{4,6},{6,7},{7,5},{5,3},{3,1},{1,0},{8,10},{10,12},{12... | collective-permute-start | bytes 1277960 | tf_op jit(solution)/shard_map/ppermute | solution.py:67
  357.5 16.9 %collective-permute-start.28 = (bf16[208,1024]{1,0:T(8,128)(2,1)S(1)}, bf16[208,1024]{1,0:T(8,128)(2,1)S(1)}, u32[]{:S(2)}, u32[]{:S(2)}) collective-permute-start(bf16[208,1024]{1,0:T(8,128)(2,1)S(1)} %slice.94), channel_id=1, source_target_pairs={{0,1},{2,0},{4,2},{6,4},{7,6},{5,7},{3,5},{1,3},{8,9},{10,8},{12,1... | collective-permute-start | bytes 1277960 | tf_op jit(solution)/shard_map/ppermute | solution.py:68
  385.6 1.2 copy-start.8
  406.0 3.9 collective-permute-start.37
  407.6 26.4 %copy-start.7 = (s32[128,4]{0,1:T(4,128)S(1)}, s32[128,4]{0,1:T(4,128)}, u32[]{:S(2)}) copy-start(s32[128,4]{0,1:T(4,128)} %param.18) | copy-start | bytes 6148
  412.0 24.3 %copy-start.9 = (s32[32]{0:T(128)S(1)}, s32[32]{0:T(128)}, u32[]{:S(2)}) copy-start(s32[32]{0:T(128)} %param.17) | copy-start | bytes 388
  412.0 21.1 %collective-permute-start.38 = (bf16[256,1664]{1,0:T(8,128)(2,1)S(1)}, bf16[256,1664]{1,0:T(8,128)(2,1)S(1)}, u32[]{:S(2)}, u32[]{:S(2)}) collective-permute-start(bf16[256,1664]{1,0:T(8,128)(2,1)S(1)} %add_convert_fusion.1), channel_id=1, source_target_pairs={{0,16},{8,24},{16,0},{24,8},{1,17},{9,25},{17,1},{25,9},{2,18},{10... | collective-permute-start | bytes 2555912 | tf_op jit(solution)/shard_map/ppermute | solution.py:144
  434.0 2.4 collective-permute-start.39
  453.1 0.6 copy-start.6
Sparse Core Ops, SparseCore 0:
  40.0 278.5 all-gather.1

commit v3 on v1

--- a/solution.py
+++ b/solution.py
@@ -35,17 +35,20 @@
 
 class Ring:
     def __init__(self, count):
-        self.count = count
-        self.walk = ring_order(count)
-        where = np.argsort(np.array(self.walk))
-        self.walk_arr = jnp.asarray(np.array(self.walk, np.int32))
-        self.here = jnp.asarray(where.astype(np.int32))[lax.axis_index("gy")]
-        n = count
-        self.right = [(self.walk[i], self.walk[(i + 1) % n]) for i in range(n)]
-        self.left = [(self.walk[i], self.walk[(i - 1) % n]) for i in range(n)]
+        self.count = n = count
+        walk = ring_order(count)
+        where = np.argsort(np.array(walk))
+        table = np.array([[walk[(where[g] + k) % n] for k in range(n)] for g in range(n)])
+        row = lax.axis_index("gy").astype(jnp.uint32)
+        row = lax.dynamic_slice(
+            jnp.asarray(table.astype(np.uint32)), (row, jnp.uint32(0)), (1, n)
+        )
+        self.origins = [lax.reshape(lax.slice(row, (0, k), (1, k + 1)), ()) for k in range(n)]
+        self.right = [(walk[i], walk[(i + 1) % n]) for i in range(n)]
+        self.left = [(walk[i], walk[(i - 1) % n]) for i in range(n)]
 
     def origin(self, offset):
-        return self.walk_arr[lax.rem(self.here + offset + self.count, self.count)]
+        return self.origins[offset % self.count]
 
     def gather(self, shard, split_axis):
         n = self.count
@@ -66,16 +69,25 @@
         return found
 
 
+def step_of(found, step):
+    return [found[2 * step - 1][1], found[2 * step][1]]
+
+
 def pick(stacked, index):
-    return lax.dynamic_index_in_dim(stacked, index, 0, keepdims=False)
+    zero = jnp.uint32(0)
+    return lax.dynamic_slice(stacked, (index, zero, zero), (1,) + stacked.shape[1:])[0]
 
 
 def sum_chunks(left, found):
     total = None
     for index, shard in found:
-        term = jnp.dot(pick(left, index), shard, preferred_element_type=jnp.float32)
-        total = term if total is None else total + term
+        total = add_chunk(left, total, index, shard)
     return total
+
+
+def add_chunk(left, total, index, shard):
+    term = jnp.dot(pick(left, index), shard, preferred_element_type=jnp.float32)
+    return term if total is None else total + term
 
 
 def chunked(values, count):
@@ -90,7 +102,7 @@
         term = lax.dot_general(
             left, shard, (((1,), (1,)), ((), ())), preferred_element_type=jnp.float32
         )
-        out = lax.dynamic_update_index_in_dim(out, term, index, 0)
+        out = lax.dynamic_update_slice(out, term[None], (index, jnp.uint32(0), jnp.uint32(0)))
     return out.transpose(1, 0, 2).reshape(left.shape[0], count * width)
 
 
@@ -245,19 +257,20 @@
 
     qkv_found = ring.gather(qkv_weight.reshape(qkv_weight.shape[0], -1), 1)
     out_found = ring.gather(out_weight.T, 1)
-    up_found = ring.gather(after(up_weight, qkv_found[-1][1]), 1)
-    down_found = ring.gather(after(down_weight.T, out_found[-1][1]), 1)
-    half = merge_weight.shape[1] // 2
-    merge_a = ring.gather(after(merge_weight[:, :half], up_found[-1][1]), 1)
-    merge_b = ring.gather(after(merge_weight[:, half:], down_found[-1][1]), 1)
+    up_found = ring.gather(up_weight, 1)
+    down_found = ring.gather(down_weight.T, 1)
+    first_steps = step_of(up_found, 1) + step_of(down_found, 1)
+    second_steps = step_of(up_found, 2) + step_of(down_found, 2)
+    merge_full = lax.all_gather(after(merge_weight, *second_steps), "gy", axis=0, tiled=True)
 
     stream_full = gather_features(patches, gx)
     normed = layer_norm(stream_full.astype(jnp.float32)).astype(jnp.bfloat16)
     projected = sum_chunks(chunked(normed, gy), qkv_found)
-    projected = projected.astype(jnp.bfloat16).reshape(tok_rows, 3, local_heads, HEAD)
+    projected = after(projected.astype(jnp.bfloat16), *first_steps).reshape(tok_rows, 3, local_heads, HEAD)
     mixed = attend(projected, segment_ids).reshape(tok_rows, head_share)
     head_partial = place_columns(mixed, out_found, gy)
     stream_full = add_sum(head_partial, stream_full, gx)
+    stream_full = after(stream_full, *second_steps)
     normed_two = layer_norm(stream_full.astype(jnp.float32)).astype(jnp.bfloat16)
     hidden = sum_chunks(chunked(normed_two, gy), up_found)
     hidden = jax.nn.gelu(hidden, approximate=False).astype(jnp.bfloat16)
@@ -276,8 +289,7 @@
     joined = jnp.take(final_full, local_index, axis=0).reshape(
         merge_index.shape[0], 4 * final_full.shape[1]
     )
-    chunks = chunked(joined, gy)
-    logits = jnp.concatenate([sum_chunks(chunks, merge_a), sum_chunks(chunks, merge_b)], axis=1)
+    logits = jnp.dot(joined, merge_full, preferred_element_type=jnp.float32)
     local_top = jnp.max(logits)
     request_sq, top_logit = reduce_scalars(request_part, local_top, gx, gy)
     return (logits.astype(jnp.bfloat16), jnp.sqrt(request_sq), top_logit)

time: 492 us -> 435 us (0.88)
  waiting for transfers between devices: 240 us -> 214 us
  local copies, waits for them, and re-layouts: 55.4 us -> 36.7 us
  between operations: 23.6 us -> 15.2 us
    ppermute x18 -> x12, waiting for transfers between devices: 155 us -> 39 us  [gather(): ccw = lax.ppermute(ccw, 'gy', self.left)]
    ppermute x18 -> x12, waiting for transfers between devices: 52.2 us -> 95 us  [gather(): cw = lax.ppermute(cw, 'gy', self.right)]
    ppermute x2, waiting for transfers between devices: 0.01 us -> 34 us  [add_sum(): total = total + lax.ppermute(sent, 'gx', x_shift(gx, k)).astype(jnp.float32)]
    all_gather x0 -> x1, waiting for transfers between devices: none -> 26.1 us  [per_device(): lax.all_gather(after(merge_weight, *second_steps), 'gy', axis=0, tiled=True)]
    ppermute x6 -> x4, waiting for transfers between devices: 24.4 us -> 3.52 us  [gather(): second = lax.ppermute(second, 'gy', self.left)]
    another operation x11 -> x2, local copies, waits for them, and re-layouts: 15.7 us -> 0.84 us
    ppermute x18 -> x12, starting transfers between devices: 28.5 us -> 20.7 us  [gather(): cw = lax.ppermute(cw, 'gy', self.right)]
    dot_general x16, matrix products: 18.4 us -> 25.5 us  [place_columns(): lax.dot_general(left, shard, (((1,), (1,)), ((), ())), preferred_element_...]
  transfers between devices with their start and end apart: 56 -> 41, of which waited for: 22 -> 20; matrix products, arithmetic and copies ran while one was open for 18% -> 28% of each run, Pallas kernels for 0% -> 0%
where the time goes in v3:
time: 435 us; the launch traced here: 428 us
  waiting for transfers between devices  214 us (49%)
  matrix products  83.9 us (19%)
  starting transfers between devices  54.4 us (13%)
  local copies, waits for them, and re-layouts  36.7 us (8%)
  between operations  15.2 us (3%)
  other arithmetic  12.6 us (3%)
  Pallas kernels  10.9 us (3%)
    ppermute x12, waiting for transfers between devices, gather(): cw = lax.ppermute(cw, 'gy', self.right)  95 us
    dot_general x16, matrix products, add_chunk(): term = jnp.dot(pick(left, index), shard, preferred_element_type=jnp.float32)  48.7 us
    ppermute x12, waiting for transfers between devices, gather(): ccw = lax.ppermute(ccw, 'gy', self.left)  39 us
    ppermute x2, waiting for transfers between devices, add_sum(): total = total + lax.ppermute(sent, 'gx', x_shift(gx, k)).astype(jnp.float32)  34 us
    all_gather x1, waiting for transfers between devices, per_device(): lax.all_gather(after(merge_weight, *second_steps), 'gy', axis=0, tiled=True)  26.1 us
    dot_general x16, matrix products, place_columns(): lax.dot_general(left, shard, (((1,), (1,)), ((), ())), preferred_element_...  25.5 us
    ppermute x12, starting transfers between devices, gather(): cw = lax.ppermute(cw, 'gy', self.right)  20.7 us
    ppermute x4, starting transfers between devices, gather(): first = lax.ppermute(first, 'gy', self.right)  15.3 us
  transfers between devices with their start and end apart: 41, of which 20 were waited for; matrix products, arithmetic and copies ran while one was open for 28% of the time, Pallas kernels for 0%

profile of v3, /device:TPU:0, one launch (start us, length us, event | category | flops | bytes accessed | tf_op | source)
XLA Modules:
  0.0 427.6 jit_solution(2149098743095380364)
XLA Ops:
  7.2 3.0 collective-permute-start
  11.3 8.9 %collective-permute-done = bf16[512,416]{0,1:T(8,128)(2,1)S(1)} collective-permute-done((bf16[512,416]{0,1:T(8,128)(2,1)}, bf16[512,416]{0,1:T(8,128)(2,1)S(1)}, u32[]{:S(2)}, u32[]{:S(2)}) %collective-permute-start) | collective-permute-done | bytes 426016 | tf_op jit(solution)/shard_map/ppermute | solution.py:125
  20.4 1.9 collective-permute-start.14
  24.0 1.9 collective-permute-start.2
  26.1 2.7 collective-permute-done.14
  28.8 1.8 collective-permute-start.16
  32.2 12.0 %collective-permute-done.16 = bf16[208,416]{0,1:T(8,128)(2,1)S(1)} collective-permute-done((bf16[208,416]{0,1:T(8,128)(2,1)}, bf16[208,416]{0,1:T(8,128)(2,1)S(1)}, u32[]{:S(2)}, u32[]{:S(2)}) %collective-permute-start.16) | collective-permute-done | bytes 173088 | tf_op jit(solution)/shard_map/ppermute | solution.py:58
  44.2 1.8 collective-permute-start.18
  47.2 3.9 collective-permute-done.18
  51.1 1.8 collective-permute-start.12
  53.8 1.8 collective-permute-start.10
  55.7 1.6 collective-permute-start.4
  61.6 11.6 %collective-permute-done.12 = bf16[208,2048]{1,0:T(8,128)(2,1)S(1)} collective-permute-done((bf16[208,2048]{1,0:T(8,128)(2,1)}, bf16[208,2048]{1,0:T(8,128)(2,1)S(1)}, u32[]{:S(2)}, u32[]{:S(2)}) %collective-permute-start.12) | collective-permute-done | bytes 852000 | tf_op jit(solution)/shard_map/ppermute | solution.py:58
  73.2 1.7 collective-permute-start.5
  74.9 25.7 %collective-permute-done.4 = bf16[208,1248]{1,0:T(8,128)(2,1)S(1)} collective-permute-done((bf16[208,1248]{1,0:T(8,128)(2,1)S(1)}, bf16[208,1248]{1,0:T(8,128)(2,1)S(1)}, u32[]{:S(2)}, u32[]{:S(2)}) %collective-permute-start.4) | collective-permute-done | bytes 519200 | tf_op jit(solution)/shard_map/ppermute | solution.py:58
  100.6 1.8 collective-permute-start.6
  103.6 1.6 collective-permute-start.27
  105.2 2.2 convolution_add_fusion.2
  109.9 5.7 %collective-permute-done.6 = bf16[208,1248]{1,0:T(8,128)(2,1)S(1)} collective-permute-done((bf16[208,1248]{1,0:T(8,128)(2,1)S(1)}, bf16[208,1248]{1,0:T(8,128)(2,1)S(1)}, u32[]{:S(2)}, u32[]{:S(2)}) %collective-permute-start.6) | collective-permute-done | bytes 519200 | tf_op jit(solution)/shard_map/ppermute | solution.py:58
  115.6 1.7 collective-permute-start.7
  119.8 35.4 %collective-permute-done.7 = bf16[208,1248]{1,0:T(8,128)(2,1)S(1)} collective-permute-done((bf16[208,1248]{1,0:T(8,128)(2,1)S(1)}, bf16[208,1248]{1,0:T(8,128)(2,1)S(1)}, u32[]{:S(2)}, u32[]{:S(2)}) %collective-permute-start.7) | collective-permute-done | bytes 519200 | tf_op jit(solution)/shard_map/ppermute | solution.py:59
  158.1 2.6 fusion.76
  165.5 2.6 fusion.51
  168.1 2.4 fusion.18
  171.5 2.1 fusion.127
  176.0 1.9 fusion.33
  177.9 1.8 fusion.32
  183.6 1.9 fusion.27
  186.0 1.7 copy.71
  188.4 3.2 collective-permute-done.22
  191.6 1.6 add_convert_fusion.3
  199.6 14.7 %collective-permute-done.23 = bf16[256,1664]{1,0:T(8,128)(2,1)S(1)} collective-permute-done((bf16[256,1664]{1,0:T(8,128)(2,1)S(1)}, bf16[256,1664]{1,0:T(8,128)(2,1)S(1)}, u32[]{:S(2)}, u32[]{:S(2)}) %collective-permute-start.23) | collective-permute-done | bytes 852000 | tf_op jit(solution)/shard_map/ppermute | solution.py:143
  214.7 20.3 %collective-permute-done.29 = bf16[208,2048]{1,0:T(8,128)(2,1)S(1)} collective-permute-done((bf16[208,2048]{1,0:T(8,128)(2,1)}, bf16[208,2048]{1,0:T(8,128)(2,1)S(1)}, u32[]{:S(2)}, u32[]{:S(2)}) %collective-permute-start.29) | collective-permute-done | bytes 852000 | tf_op jit(solution)/shard_map/ppermute | solution.py:58
  235.8 9.8 %collective-permute-start.31 = (bf16[208,1024]{1,0:T(8,128)(2,1)}, bf16[208,1024]{1,0:T(8,128)(2,1)}, u32[]{:S(2)}, u32[]{:S(2)}) collective-permute-start(bf16[208,1024]{1,0:T(8,128)(2,1)} %slice.125), channel_id=1, source_target_pairs={{0,2},{2,4},{4,6},{6,7},{7,5},{5,3},{3,1},{1,0},{8,10},{10,12},{12... | collective-permute-start | bytes 1277960 | tf_op jit(solution)/shard_map/ppermute | solution.py:65
  245.6 3.5 collective-permute-done.30
  250.0 2.5 collective-permute-start.32
  252.4 13.2 %collective-permute-done.33 = bf16[208,2048]{1,0:T(8,128)(2,1)S(1)} collective-permute-done((bf16[208,2048]{1,0:T(8,128)(2,1)}, bf16[208,2048]{1,0:T(8,128)(2,1)S(1)}, u32[]{:S(2)}, u32[]{:S(2)}) %collective-permute-start.33) | collective-permute-done | bytes 852000 | tf_op jit(solution)/shard_map/ppermute | solution.py:58
  266.5 2.4 collective-permute-start.35
  272.3 2.3 copy.64
  274.6 1.8 collective-permute-done.31
  276.4 2.2 collective-permute-done.32
  278.5 2.8 fusion.43
  281.3 2.5 fusion.73
  285.3 2.7 fusion.65
  288.0 3.4 fusion.67
  291.4 3.4 fusion.69
  294.8 3.4 fusion.71
  298.2 14.9 %fusion.3 = bf16[512,2048]{1,0:T(8,128)(2,1)} fusion(f32[512,2048]{1,0:T(8,128)S(1)} %fusion.43, f32[512,2048]{1,0:T(8,128)S(1)} %fusion.63, f32[512,2048]{1,0:T(8,128)S(1)} %fusion.65, f32[512,2048]{1,0:T(8,128)} %fusion.67, f32[512,2048]{1,0:T(8,128)} %fusion.69, f32[512,2048]{1,0:T(8,128)S(1)} %fusion.73, f32[512,2048]{1,0:T(8,128)} %fusion.71, ...), kind=kOutput, calls=%fused_computation.8 | convolution fusion | flops 511705088 | bytes 32522244 | tf_op jit(solution)/shard_map/dot_general | solution.py:89
  314.2 3.0 fusion.42
  322.1 1.7 fusion.38
  323.8 1.6 fusion.37
  326.9 2.7 fusion.35
  329.6 1.6 constant_dynamic-slice_fusion.1
  331.2 2.7 copy.73
  334.0 1.6 copy.72
  335.6 2.3 collective-permute-done.37
  337.9 2.1 add_convert_fusion.1
  340.0 1.7 collective-permute-start.38
  341.7 19.4 %collective-permute-done.38 = bf16[256,1664]{1,0:T(8,128)(2,1)S(1)} collective-permute-done((bf16[256,1664]{1,0:T(8,128)(2,1)S(1)}, bf16[256,1664]{1,0:T(8,128)(2,1)S(1)}, u32[]{:S(2)}, u32[]{:S(2)}) %collective-permute-start.38) | collective-permute-done | bytes 852000 | tf_op jit(solution)/shard_map/ppermute | solution.py:143
  364.2 3.2 gather_fusion
  367.3 3.2 gather.7
  371.3 26.1 %all-gather.2.cloned.1.call-done = bf16[6656,1024]{1,0:T(8,128)(2,1)} async-done(((bf16[832,1024]{1,0:T(8,128)(2,1)}), bf16[6656,1024]{1,0:T(8,128)(2,1)}) %all-gather.2.cloned.1.call-update) | async-done | bytes 13631504 | tf_op jit(solution)/shard_map/all_gather | solution.py:264
  397.4 8.4 %fusion.125 = (f32[]{:T(128)}, bf16[128,1024]{1,0:T(8,128)(2,1)}) fusion(bf16[6656,1024]{1,0:T(8,128)(2,1)} %all-gather.2.cloned.1.call-done, pred[128,6656]{1,0:T(8,128)(4,1)} %bitcast.240, bf16[128,6656]{1,0:T(8,128)(2,1)S(1)} %gather.7), kind=kOutput, calls=%fused_computation.207 | convolution fusion | flops 1745944576 | bytes 16449540 | tf_op jit(solution)/shard_map/dot_general | solution.py:292
  407.3 10.9 %scalar_sums.1 = f32[8,128]{1,0:T(8,128)} custom-call(f32[8,128]{1,0:T(8,128)} %copy-done.30), custom_call_target="tpu_custom_call" | custom-call | tf_op jit(solution)/shard_map/scalar_sums/pallas_call | solution.py:208
  (205 shorter events, 62.4 us)
Async XLA Ops:
  7.2 39.1 %copy-start.29 = (s32[512]{0:T(512)S(1)}, s32[512]{0:T(512)}, u32[]{:S(2)}) copy-start(s32[512]{0:T(512)} %param.15) | copy-start | bytes 6148
  7.2 390.2 %all-gather.2.cloned.1.call-start = ((), (), s32[]{:S(2)}) async-start(), calls=%async_computation | async-start | bytes 15335424 | tf_op jit(solution)/shard_map/all_gather | solution.py:264
  7.2 13.0 %collective-permute-start = (bf16[512,416]{0,1:T(8,128)(2,1)}, bf16[512,416]{0,1:T(8,128)(2,1)S(1)}, u32[]{:S(2)}, u32[]{:S(2)}) collective-permute-start(bf16[512,416]{0,1:T(8,128)(2,1)} %param.14), channel_id=1, source_target_pairs={{0,16},{8,24},{16,0},{24,8},{1,17},{9,25},{17,1},{25,9},{2,18},{10... | collective-permute-start | bytes 1277960 | tf_op jit(solution)/shard_map/ppermute | solution.py:125
  20.3 35.3 %collective-permute-start.1 = (bf16[2,512,416]{1,2,0:T(8,128)(2,1)S(1)}, bf16[2,512,416]{1,2,0:T(8,128)(2,1)S(1)}, u32[]{:S(2)}, u32[]{:S(2)}) collective-permute-start(bf16[2,512,416]{1,2,0:T(8,128)(2,1)S(1)} %bitcast_dynamic-update-slice_fusion), channel_id=1, source_target_pairs={{0,8},{8,0},{16,24},{24,16},{1,9},{9,1},{17,25},{25,17},{2,10},{10... | collective-permute-start | bytes 2555912 | tf_op jit(solution)/shard_map/ppermute | solution.py:127
  20.4 8.4 %collective-permute-start.14 = (bf16[208,416]{0,1:T(8,128)(2,1)}, bf16[208,416]{0,1:T(8,128)(2,1)}, u32[]{:S(2)}, u32[]{:S(2)}) collective-permute-start(bf16[208,416]{0,1:T(8,128)(2,1)} %bitcast.241), channel_id=1, source_target_pairs={{0,2},{2,4},{4,6},{6,7},{7,5},{5,3},{3,1},{1,0},{8,10},{10,12},{12... | collective-permute-start | bytes 519176 | tf_op jit(solution)/shard_map/ppermute | solution.py:58
  22.2 8.4 %collective-permute-start.15 = (bf16[208,416]{0,1:T(8,128)(2,1)}, bf16[208,416]{0,1:T(8,128)(2,1)}, u32[]{:S(2)}, u32[]{:S(2)}) collective-permute-start(bf16[208,416]{0,1:T(8,128)(2,1)} %bitcast.242), channel_id=1, source_target_pairs={{0,1},{2,0},{4,2},{6,4},{7,6},{5,7},{3,5},{1,3},{8,9},{10,8},{12,1... | collective-permute-start | bytes 519176 | tf_op jit(solution)/shard_map/ppermute | solution.py:59
  24.0 29.8 %collective-permute-start.2 = (bf16[208,1248]{1,0:T(8,128)(2,1)S(1)}, bf16[208,1248]{1,0:T(8,128)(2,1)S(1)}, u32[]{:S(2)}, u32[]{:S(2)}) collective-permute-start(bf16[208,1248]{1,0:T(8,128)(2,1)S(1)} %copy.59), channel_id=1, source_target_pairs={{0,2},{2,4},{4,6},{6,7},{7,5},{5,3},{3,1},{1,0},{8,10},{10,12},{12... | collective-permute-start | bytes 1557512 | tf_op jit(solution)/shard_map/ppermute | solution.py:58
  25.9 34.1 %collective-permute-start.3 = (bf16[208,1248]{1,0:T(8,128)(2,1)S(1)}, bf16[208,1248]{1,0:T(8,128)(2,1)}, u32[]{:S(2)}, u32[]{:S(2)}) collective-permute-start(bf16[208,1248]{1,0:T(8,128)(2,1)S(1)} %copy.59), channel_id=1, source_target_pairs={{0,1},{2,0},{4,2},{6,4},{7,6},{5,7},{3,5},{1,3},{8,9},{10,8},{12,1... | collective-permute-start | bytes 1557512 | tf_op jit(solution)/shard_map/ppermute | solution.py:59
  28.8 15.4 %collective-permute-start.16 = (bf16[208,416]{0,1:T(8,128)(2,1)}, bf16[208,416]{0,1:T(8,128)(2,1)S(1)}, u32[]{:S(2)}, u32[]{:S(2)}) collective-permute-start(bf16[208,416]{0,1:T(8,128)(2,1)} %collective-permute-done.14), channel_id=1, source_target_pairs={{0,2},{2,4},{4,6},{6,7},{7,5},{5,3},{3,1},{1,0},{8,10},{10,12},{12... | collective-permute-start | bytes 519176 | tf_op jit(solution)/shard_map/ppermute | solution.py:58
  30.7 15.4 %collective-permute-start.17 = (bf16[208,416]{0,1:T(8,128)(2,1)}, bf16[208,416]{0,1:T(8,128)(2,1)S(1)}, u32[]{:S(2)}, u32[]{:S(2)}) collective-permute-start(bf16[208,416]{0,1:T(8,128)(2,1)} %collective-permute-done.15), channel_id=1, source_target_pairs={{0,1},{2,0},{4,2},{6,4},{7,6},{5,7},{3,5},{1,3},{8,9},{10,8},{12,1... | collective-permute-start | bytes 519176 | tf_op jit(solution)/shard_map/ppermute | solution.py:59
  44.2 11.4 %copy-start.25 = (bf16[208,416]{0,1:T(8,128)(2,1)}, bf16[208,416]{0,1:T(8,128)(2,1)S(1)}, u32[]{:S(2)}) copy-start(bf16[208,416]{0,1:T(8,128)(2,1)S(1)} %collective-permute-done.16) | copy-start | bytes 519172
  44.2 6.8 %collective-permute-start.18 = (bf16[208,416]{0,1:T(8,128)(2,1)S(1)}, bf16[208,416]{0,1:T(8,128)(2,1)S(1)}, u32[]{:S(2)}, u32[]{:S(2)}) collective-permute-start(bf16[208,416]{0,1:T(8,128)(2,1)S(1)} %collective-permute-done.16), channel_id=1, source_target_pairs={{0,2},{2,4},{4,6},{6,7},{7,5},{5,3},{3,1},{1,0},{8,10},{10,12},{12... | collective-permute-start | bytes 519176 | tf_op jit(solution)/shard_map/ppermute | solution.py:58
  46.0 9.6 %copy-start.27 = (bf16[208,416]{0,1:T(8,128)(2,1)}, bf16[208,416]{0,1:T(8,128)(2,1)S(1)}, u32[]{:S(2)}) copy-start(bf16[208,416]{0,1:T(8,128)(2,1)S(1)} %collective-permute-done.17) | copy-start | bytes 519172
  46.0 6.8 %collective-permute-start.19 = (bf16[208,416]{0,1:T(8,128)(2,1)S(1)}, bf16[208,416]{0,1:T(8,128)(2,1)S(1)}, u32[]{:S(2)}, u32[]{:S(2)}) collective-permute-start(bf16[208,416]{0,1:T(8,128)(2,1)S(1)} %collective-permute-done.17), channel_id=1, source_target_pairs={{0,1},{2,0},{4,2},{6,4},{7,6},{5,7},{3,5},{1,3},{8,9},{10,8},{12,1... | collective-permute-start | bytes 519176 | tf_op jit(solution)/shard_map/ppermute | solution.py:59
  51.1 4.6 %copy-start.14 = (bf16[208,416]{0,1:T(8,128)(2,1)}, bf16[208,416]{0,1:T(8,128)(2,1)S(1)}, u32[]{:S(2)}) copy-start(bf16[208,416]{0,1:T(8,128)(2,1)S(1)} %collective-permute-done.18) | copy-start | bytes 519172
  51.1 22.1 %collective-permute-start.12 = (bf16[208,2048]{1,0:T(8,128)(2,1)}, bf16[208,2048]{1,0:T(8,128)(2,1)S(1)}, u32[]{:S(2)}, u32[]{:S(2)}) collective-permute-start(bf16[208,2048]{1,0:T(8,128)(2,1)} %bitcast.245), channel_id=1, source_target_pairs={{0,2},{2,4},{4,6},{6,7},{7,5},{5,3},{3,1},{1,0},{8,10},{10,12},{12... | collective-permute-start | bytes 2555912 | tf_op jit(solution)/shard_map/ppermute | solution.py:58
  52.9 50.7 %collective-permute-start.13 = (bf16[208,2048]{1,0:T(8,128)(2,1)}, bf16[208,2048]{1,0:T(8,128)(2,1)S(1)}, u32[]{:S(2)}, u32[]{:S(2)}) collective-permute-start(bf16[208,2048]{1,0:T(8,128)(2,1)} %bitcast.246), channel_id=1, source_target_pairs={{0,1},{2,0},{4,2},{6,4},{7,6},{5,7},{3,5},{1,3},{8,9},{10,8},{12,1... | collective-permute-start | bytes 2555912 | tf_op jit(solution)/shard_map/ppermute | solution.py:59
  53.8 5.6 %copy-start.12 = (bf16[208,1248]{1,0:T(8,128)(2,1)}, bf16[208,1248]{1,0:T(8,128)(2,1)S(1)}, u32[]{:S(2)}) copy-start(bf16[208,1248]{1,0:T(8,128)(2,1)S(1)} %collective-permute-done.2) | copy-start | bytes 1557508
  53.8 53.6 %collective-permute-start.10 = (bf16[208,2048]{1,0:T(8,128)(2,1)}, bf16[208,2048]{1,0:T(8,128)(2,1)S(1)}, u32[]{:S(2)}, u32[]{:S(2)}) collective-permute-start(bf16[208,2048]{1,0:T(8,128)(2,1)} %param.20), channel_id=1, source_target_pairs={{0,2},{2,4},{4,6},{6,7},{7,5},{5,3},{3,1},{1,0},{8,10},{10,12},{12... | collective-permute-start | bytes 2555912 | tf_op jit(solution)/shard_map/ppermute | solution.py:58
  55.7 44.9 %collective-permute-start.4 = (bf16[208,1248]{1,0:T(8,128)(2,1)S(1)}, bf16[208,1248]{1,0:T(8,128)(2,1)S(1)}, u32[]{:S(2)}, u32[]{:S(2)}) collective-permute-start(bf16[208,1248]{1,0:T(8,128)(2,1)S(1)} %collective-permute-done.2), channel_id=1, source_target_pairs={{0,2},{2,4},{4,6},{6,7},{7,5},{5,3},{3,1},{1,0},{8,10},{10,12},{12... | collective-permute-start | bytes 1557512 | tf_op jit(solution)/shard_map/ppermute | solution.py:58
  59.5 42.9 %copy-start.13 = (bf16[208,1248]{1,0:T(8,128)(2,1)S(1)}, bf16[208,1248]{1,0:T(8,128)(2,1)}, u32[]{:S(2)}) copy-start(bf16[208,1248]{1,0:T(8,128)(2,1)} %copy-done.12) | copy-start | bytes 1557508
  60.0 98.1 %copy-start.1 = (bf16[512,8,208]{0,2,1:T(8,128)(2,1)}, bf16[512,8,208]{0,2,1:T(8,128)(2,1)S(1)}, u32[]{:S(2)}) copy-start(bf16[512,8,208]{0,2,1:T(8,128)(2,1)S(1)} %multiply_convert_fusion) | copy-start | bytes 5111812
  60.0 47.9 %collective-permute-start.11 = (bf16[208,2048]{1,0:T(8,128)(2,1)}, bf16[208,2048]{1,0:T(8,128)(2,1)S(1)}, u32[]{:S(2)}, u32[]{:S(2)}) collective-permute-start(bf16[208,2048]{1,0:T(8,128)(2,1)} %param.20), channel_id=1, source_target_pairs={{0,1},{2,0},{4,2},{6,4},{7,6},{5,7},{3,5},{1,3},{8,9},{10,8},{12,1... | collective-permute-start | bytes 2555912 | tf_op jit(solution)/shard_map/ppermute | solution.py:59
  73.2 34.2 %copy-start.33 = (bf16[208,2048]{1,0:T(8,128)(2,1)}, bf16[208,2048]{1,0:T(8,128)(2,1)S(1)}, u32[]{:S(2)}) copy-start(bf16[208,2048]{1,0:T(8,128)(2,1)S(1)} %collective-permute-done.12) | copy-start | bytes 2555908
  73.2 36.3 %collective-permute-start.5 = (bf16[208,1248]{1,0:T(8,128)(2,1)}, bf16[208,1248]{1,0:T(8,128)(2,1)S(1)}, u32[]{:S(2)}, u32[]{:S(2)}) collective-permute-start(bf16[208,1248]{1,0:T(8,128)(2,1)} %collective-permute-done.3), channel_id=1, source_target_pairs={{0,1},{2,0},{4,2},{6,4},{7,6},{5,7},{3,5},{1,3},{8,9},{10,8},{12,1... | collective-permute-start | bytes 1557512 | tf_op jit(solution)/shard_map/ppermute | solution.py:59
  100.6 15.0 %collective-permute-start.6 = (bf16[208,1248]{1,0:T(8,128)(2,1)S(1)}, bf16[208,1248]{1,0:T(8,128)(2,1)S(1)}, u32[]{:S(2)}, u32[]{:S(2)}) collective-permute-start(bf16[208,1248]{1,0:T(8,128)(2,1)S(1)} %collective-permute-done.4), channel_id=1, source_target_pairs={{0,2},{2,4},{4,6},{6,7},{7,5},{5,3},{3,1},{1,0},{8,10},{10,12},{12... | collective-permute-start | bytes 1557512 | tf_op jit(solution)/shard_map/ppermute | solution.py:58
  103.6 15.0 %copy-start.35 = (bf16[208,2048]{1,0:T(8,128)(2,1)}, bf16[208,2048]{1,0:T(8,128)(2,1)S(1)}, u32[]{:S(2)}) copy-start(bf16[208,2048]{1,0:T(8,128)(2,1)S(1)} %collective-permute-done.13) | copy-start | bytes 2555908
  103.6 54.1 %collective-permute-start.27 = (bf16[208,2048]{1,0:T(8,128)(2,1)S(1)}, bf16[208,2048]{1,0:T(8,128)(2,1)S(1)}, u32[]{:S(2)}, u32[]{:S(2)}) collective-permute-start(bf16[208,2048]{1,0:T(8,128)(2,1)S(1)} %collective-permute-done.12), channel_id=1, source_target_pairs={{0,2},{2,4},{4,6},{6,7},{7,5},{5,3},{3,1},{1,0},{8,10},{10,12},{12... | collective-permute-start | bytes 2555912 | tf_op jit(solution)/shard_map/ppermute | solution.py:58
  107.4 12.4 %copy-start.6 = (bf16[208,2048]{1,0:T(8,128)(2,1)}, bf16[208,2048]{1,0:T(8,128)(2,1)S(1)}, u32[]{:S(2)}) copy-start(bf16[208,2048]{1,0:T(8,128)(2,1)S(1)} %collective-permute-done.10) | copy-start | bytes 2555908
  107.4 53.3 %collective-permute-start.28 = (bf16[208,2048]{1,0:T(8,128)(2,1)S(1)}, bf16[208,2048]{1,0:T(8,128)(2,1)S(1)}, u32[]{:S(2)}, u32[]{:S(2)}) collective-permute-start(bf16[208,2048]{1,0:T(8,128)(2,1)S(1)} %collective-permute-done.13), channel_id=1, source_target_pairs={{0,1},{2,0},{4,2},{6,4},{7,6},{5,7},{3,5},{1,3},{8,9},{10,8},{12,1... | collective-permute-start | bytes 2555912 | tf_op jit(solution)/shard_map/ppermute | solution.py:59
  107.9 11.8 %copy-start.8 = (bf16[208,2048]{1,0:T(8,128)(2,1)}, bf16[208,2048]{1,0:T(8,128)(2,1)S(1)}, u32[]{:S(2)}) copy-start(bf16[208,2048]{1,0:T(8,128)(2,1)S(1)} %collective-permute-done.11) | copy-start | bytes 2555908
  107.9 54.3 %collective-permute-start.25 = (bf16[208,2048]{1,0:T(8,128)(2,1)S(1)}, bf16[208,2048]{1,0:T(8,128)(2,1)S(1)}, u32[]{:S(2)}, u32[]{:S(2)}) collective-permute-start(bf16[208,2048]{1,0:T(8,128)(2,1)S(1)} %collective-permute-done.10), channel_id=1, source_target_pairs={{0,2},{2,4},{4,6},{6,7},{7,5},{5,3},{3,1},{1,0},{8,10},{10,12},{12... | collective-permute-start | bytes 2555912 | tf_op jit(solution)/shard_map/ppermute | solution.py:58
  109.5 54.6 %collective-permute-start.26 = (bf16[208,2048]{1,0:T(8,128)(2,1)S(1)}, bf16[208,2048]{1,0:T(8,128)(2,1)}, u32[]{:S(2)}, u32[]{:S(2)}) collective-permute-start(bf16[208,2048]{1,0:T(8,128)(2,1)S(1)} %collective-permute-done.11), channel_id=1, source_target_pairs={{0,1},{2,0},{4,2},{6,4},{7,6},{5,7},{3,5},{1,3},{8,9},{10,8},{12,1... | collective-permute-start | bytes 2555912 | tf_op jit(solution)/shard_map/ppermute | solution.py:59
  115.6 39.6 %collective-permute-start.7 = (bf16[208,1248]{1,0:T(8,128)(2,1)S(1)}, bf16[208,1248]{1,0:T(8,128)(2,1)S(1)}, u32[]{:S(2)}, u32[]{:S(2)}) collective-permute-start(bf16[208,1248]{1,0:T(8,128)(2,1)S(1)} %collective-permute-done.5), channel_id=1, source_target_pairs={{0,1},{2,0},{4,2},{6,4},{7,6},{5,7},{3,5},{1,3},{8,9},{10,8},{12,1... | collective-permute-start | bytes 1557512 | tf_op jit(solution)/shard_map/ppermute | solution.py:59
  155.2 8.9 %collective-permute-start.8 = (bf16[208,624]{1,0:T(8,128)(2,1)S(1)}, bf16[208,624]{1,0:T(8,128)(2,1)}, u32[]{:S(2)}, u32[]{:S(2)}) collective-permute-start(bf16[208,624]{1,0:T(8,128)(2,1)S(1)} %slice.118), channel_id=1, source_target_pairs={{0,2},{2,4},{4,6},{6,7},{7,5},{5,3},{3,1},{1,0},{8,10},{10,12},{12... | collective-permute-start | bytes 778760 | tf_op jit(solution)/shard_map/ppermute | solution.py:65
  157.7 6.5 %copy-start.37 = (bf16[208,2048]{1,0:T(8,128)(2,1)}, bf16[208,2048]{1,0:T(8,128)(2,1)S(1)}, u32[]{:S(2)}) copy-start(bf16[208,2048]{1,0:T(8,128)(2,1)S(1)} %collective-permute-done.27) | copy-start | bytes 2555908
  157.7 7.9 %collective-permute-start.9 = (bf16[208,624]{1,0:T(8,128)(2,1)}, bf16[208,624]{1,0:T(8,128)(2,1)}, u32[]{:S(2)}, u32[]{:S(2)}) collective-permute-start(bf16[208,624]{1,0:T(8,128)(2,1)} %slice.119), channel_id=1, source_target_pairs={{0,1},{2,0},{4,2},{6,4},{7,6},{5,7},{3,5},{1,3},{8,9},{10,8},{12,1... | collective-permute-start | bytes 778760 | tf_op jit(solution)/shard_map/ppermute | solution.py:66
  160.7 22.9 %collective-permute-start.20 = (bf16[208,208]{0,1:T(8,128)(2,1)S(1)}, bf16[208,208]{0,1:T(8,128)(2,1)}, u32[]{:S(2)}, u32[]{:S(2)}) collective-permute-start(bf16[208,208]{0,1:T(8,128)(2,1)S(1)} %slice.123), channel_id=1, source_target_pairs={{0,2},{2,4},{4,6},{6,7},{7,5},{5,3},{3,1},{1,0},{8,10},{10,12},{12... | collective-permute-start | bytes 259592 | tf_op jit(solution)/shard_map/ppermute | solution.py:65
  163.2 20.4 %collective-permute-start.21 = (bf16[208,208]{0,1:T(8,128)(2,1)}, bf16[208,208]{0,1:T(8,128)(2,1)}, u32[]{:S(2)}, u32[]{:S(2)}) collective-permute-start(bf16[208,208]{0,1:T(8,128)(2,1)} %slice.124), channel_id=1, source_target_pairs={{0,1},{2,0},{4,2},{6,4},{7,6},{5,7},{3,5},{1,3},{8,9},{10,8},{12,1... | collective-permute-start | bytes 259592 | tf_op jit(solution)/shard_map/ppermute | solution.py:66
  174.1 5.7 %copy-start.26 = (bf16[208,416]{0,1:T(8,128)(2,1)S(1)}, bf16[208,416]{0,1:T(8,128)(2,1)}, u32[]{:S(2)}) copy-start(bf16[208,416]{0,1:T(8,128)(2,1)} %copy-done.25) | copy-start | bytes 519172
  174.1 6.6 %copy-start.28 = (bf16[208,416]{0,1:T(8,128)(2,1)S(1)}, bf16[208,416]{0,1:T(8,128)(2,1)}, u32[]{:S(2)}) copy-start(bf16[208,416]{0,1:T(8,128)(2,1)} %copy-done.27) | copy-start | bytes 519172
  175.1 6.6 %copy-start.15 = (bf16[208,416]{0,1:T(8,128)(2,1)S(1)}, bf16[208,416]{0,1:T(8,128)(2,1)}, u32[]{:S(2)}) copy-start(bf16[208,416]{0,1:T(8,128)(2,1)} %copy-done.14) | copy-start | bytes 519172
  175.1 7.6 %copy-start.17 = (bf16[208,416]{0,1:T(8,128)(2,1)S(1)}, bf16[208,416]{0,1:T(8,128)(2,1)}, u32[]{:S(2)}) copy-start(bf16[208,416]{0,1:T(8,128)(2,1)} %copy-done.16) | copy-start | bytes 519172
  187.7 3.9 collective-permute-start.22
  188.4 6.3 %copy-start.3 = (bf16[2,2,512,416]{2,3,1,0:T(8,128)(2,1)S(1)}, bf16[2,2,512,416]{2,3,1,0:T(8,128)(2,1)}, u32[]{:S(2)}) copy-start(bf16[2,2,512,416]{2,3,1,0:T(8,128)(2,1)} %get-tuple-element.47) | copy-start | bytes 5111812
  193.2 21.1 %collective-permute-start.23 = (bf16[256,1664]{1,0:T(8,128)(2,1)S(1)}, bf16[256,1664]{1,0:T(8,128)(2,1)S(1)}, u32[]{:S(2)}, u32[]{:S(2)}) collective-permute-start(bf16[256,1664]{1,0:T(8,128)(2,1)S(1)} %add_convert_fusion.3), channel_id=1, source_target_pairs={{0,16},{8,24},{16,0},{24,8},{1,17},{9,25},{17,1},{25,9},{2,18},{10... | collective-permute-start | bytes 2555912 | tf_op jit(solution)/shard_map/ppermute | solution.py:143
  195.5 39.4 %collective-permute-start.29 = (bf16[208,2048]{1,0:T(8,128)(2,1)}, bf16[208,2048]{1,0:T(8,128)(2,1)S(1)}, u32[]{:S(2)}, u32[]{:S(2)}) collective-permute-start(bf16[208,2048]{1,0:T(8,128)(2,1)} %copy-done.10), channel_id=1, source_target_pairs={{0,2},{2,4},{4,6},{6,7},{7,5},{5,3},{3,1},{1,0},{8,10},{10,12},{12... | collective-permute-start | bytes 2555912 | tf_op jit(solution)/shard_map/ppermute | solution.py:58
  197.1 52.0 %collective-permute-start.30 = (bf16[208,2048]{1,0:T(8,128)(2,1)}, bf16[208,2048]{1,0:T(8,128)(2,1)S(1)}, u32[]{:S(2)}, u32[]{:S(2)}) collective-permute-start(bf16[208,2048]{1,0:T(8,128)(2,1)} %collective-permute-done.26), channel_id=1, source_target_pairs={{0,1},{2,0},{4,2},{6,4},{7,6},{5,7},{3,5},{1,3},{8,9},{10,8},{12,1... | collective-permute-start | bytes 2555912 | tf_op jit(solution)/shard_map/ppermute | solution.py:59
  197.6 68.1 %collective-permute-start.33 = (bf16[208,2048]{1,0:T(8,128)(2,1)}, bf16[208,2048]{1,0:T(8,128)(2,1)S(1)}, u32[]{:S(2)}, u32[]{:S(2)}) collective-permute-start(bf16[208,2048]{1,0:T(8,128)(2,1)} %copy-done.37), channel_id=1, source_target_pairs={{0,2},{2,4},{4,6},{6,7},{7,5},{5,3},{3,1},{1,0},{8,10},{10,12},{12... | collective-permute-start | bytes 2555912 | tf_op jit(solution)/shard_map/ppermute | solution.py:58
  199.1 69.8 %collective-permute-start.34 = (bf16[208,2048]{1,0:T(8,128)(2,1)}, bf16[208,2048]{1,0:T(8,128)(2,1)S(1)}, u32[]{:S(2)}, u32[]{:S(2)}) collective-permute-start(bf16[208,2048]{1,0:T(8,128)(2,1)} %copy-done.39), channel_id=1, source_target_pairs={{0,1},{2,0},{4,2},{6,4},{7,6},{5,7},{3,5},{1,3},{8,9},{10,8},{12,1... | collective-permute-start | bytes 2555912 | tf_op jit(solution)/shard_map/ppermute | solution.py:59
  214.6 56.2 %collective-permute-start.24 = (bf16[256,1664]{1,0:T(8,128)(2,1)S(1)}, bf16[256,1664]{1,0:T(8,128)(2,1)S(1)}, u32[]{:S(2)}, u32[]{:S(2)}) collective-permute-start(bf16[256,1664]{1,0:T(8,128)(2,1)S(1)} %add_convert_fusion.2), channel_id=1, source_target_pairs={{0,8},{8,0},{16,24},{24,16},{1,9},{9,1},{17,25},{25,17},{2,10},{10... | collective-permute-start | bytes 2555912 | tf_op jit(solution)/shard_map/ppermute | solution.py:146
  234.9 36.1 %copy-start.4 = (bf16[208,2048]{1,0:T(8,128)(2,1)}, bf16[208,2048]{1,0:T(8,128)(2,1)S(1)}, u32[]{:S(2)}) copy-start(bf16[208,2048]{1,0:T(8,128)(2,1)S(1)} %collective-permute-done.29) | copy-start | bytes 2555908
  235.8 40.6 %collective-permute-start.31 = (bf16[208,1024]{1,0:T(8,128)(2,1)}, bf16[208,1024]{1,0:T(8,128)(2,1)}, u32[]{:S(2)}, u32[]{:S(2)}) collective-permute-start(bf16[208,1024]{1,0:T(8,128)(2,1)} %slice.125), channel_id=1, source_target_pairs={{0,2},{2,4},{4,6},{6,7},{7,5},{5,3},{3,1},{1,0},{8,10},{10,12},{12... | collective-permute-start | bytes 1277960 | tf_op jit(solution)/shard_map/ppermute | solution.py:65
  249.1 21.7 %copy-start.23 = (bf16[208,2048]{1,0:T(8,128)(2,1)}, bf16[208,2048]{1,0:T(8,128)(2,1)S(1)}, u32[]{:S(2)}) copy-start(bf16[208,2048]{1,0:T(8,128)(2,1)S(1)} %collective-permute-done.30) | copy-start | bytes 2555908
  250.0 28.6 %collective-permute-start.32 = (bf16[208,1024]{1,0:T(8,128)(2,1)}, bf16[208,1024]{1,0:T(8,128)(2,1)}, u32[]{:S(2)}, u32[]{:S(2)}) collective-permute-start(bf16[208,1024]{1,0:T(8,128)(2,1)} %slice.126), channel_id=1, source_target_pairs={{0,1},{2,0},{4,2},{6,4},{7,6},{5,7},{3,5},{1,3},{8,9},{10,8},{12,1... | collective-permute-start | bytes 1277960 | tf_op jit(solution)/shard_map/ppermute | solution.py:66
  265.7 5.1 %copy-start.19 = (bf16[208,2048]{1,0:T(8,128)(2,1)}, bf16[208,2048]{1,0:T(8,128)(2,1)S(1)}, u32[]{:S(2)}) copy-start(bf16[208,2048]{1,0:T(8,128)(2,1)S(1)} %collective-permute-done.33) | copy-start | bytes 2555908
  266.5 60.4 %collective-permute-start.35 = (bf16[208,1024]{1,0:T(8,128)(2,1)}, bf16[208,1024]{1,0:T(8,128)(2,1)}, u32[]{:S(2)}, u32[]{:S(2)}) collective-permute-start(bf16[208,1024]{1,0:T(8,128)(2,1)} %slice.127), channel_id=1, source_target_pairs={{0,2},{2,4},{4,6},{6,7},{7,5},{5,3},{3,1},{1,0},{8,10},{10,12},{12... | collective-permute-start | bytes 1277960 | tf_op jit(solution)/shard_map/ppermute | solution.py:65
  269.8 57.2 %collective-permute-start.36 = (bf16[208,1024]{1,0:T(8,128)(2,1)}, bf16[208,1024]{1,0:T(8,128)(2,1)}, u32[]{:S(2)}, u32[]{:S(2)}) collective-permute-start(bf16[208,1024]{1,0:T(8,128)(2,1)} %slice.128), channel_id=1, source_target_pairs={{0,1},{2,0},{4,2},{6,4},{7,6},{5,7},{3,5},{1,3},{8,9},{10,8},{12,1... | collective-permute-start | bytes 1277960 | tf_op jit(solution)/shard_map/ppermute | solution.py:66
  313.1 4.2 copy-start.34
  334.0 3.9 collective-permute-start.37
  335.6 25.9 %copy-start.31 = (s32[128,4]{0,1:T(4,128)S(1)}, s32[128,4]{0,1:T(4,128)}, u32[]{:S(2)}) copy-start(s32[128,4]{0,1:T(4,128)} %param.17) | copy-start | bytes 6148
  340.0 23.7 %copy-start.41 = (s32[32]{0:T(128)S(1)}, s32[32]{0:T(128)}, u32[]{:S(2)}) copy-start(s32[32]{0:T(128)} %param.16) | copy-start | bytes 388
  340.0 21.1 %collective-permute-start.38 = (bf16[256,1664]{1,0:T(8,128)(2,1)S(1)}, bf16[256,1664]{1,0:T(8,128)(2,1)S(1)}, u32[]{:S(2)}, u32[]{:S(2)}) collective-permute-start(bf16[256,1664]{1,0:T(8,128)(2,1)S(1)} %add_convert_fusion.1), channel_id=1, source_target_pairs={{0,16},{8,24},{16,0},{24,8},{1,17},{9,25},{17,1},{25,9},{2,18},{10... | collective-permute-start | bytes 2555912 | tf_op jit(solution)/shard_map/ppermute | solution.py:143
  361.4 2.4 collective-permute-start.39
  (20 other events, 43.9 us)
Sparse Core Ops, SparseCore 0:
  164.3 233.0 all-gather.1

commit v4 on v3

--- a/solution.py
+++ b/solution.py
@@ -50,23 +50,27 @@
     def origin(self, offset):
         return self.origins[offset % self.count]
 
-    def gather(self, shard, split_axis):
-        n = self.count
+    def steps(self, shard):
         found = [(self.origin(0), shard)]
         cw = ccw = shard
-        for step in range(1, (n - 1) // 2 + 1):
+        for step in range(1, (self.count - 1) // 2 + 1):
             cw = lax.ppermute(cw, "gy", self.right)
             ccw = lax.ppermute(ccw, "gy", self.left)
             found.append((self.origin(-step), cw))
             found.append((self.origin(step), ccw))
-        half = shard.shape[split_axis] // 2
+        return found
+
+    def last(self, cw, ccw, split_axis):
+        half = cw.shape[split_axis] // 2
         first = lax.slice_in_dim(cw, 0, half, axis=split_axis)
         second = lax.slice_in_dim(ccw, half, 2 * half, axis=split_axis)
         first = lax.ppermute(first, "gy", self.right)
         second = lax.ppermute(second, "gy", self.left)
-        far = lax.concatenate([first, second], split_axis)
-        found.append((self.origin(n // 2), far))
-        return found
+        return (self.origin(self.count // 2), lax.concatenate([first, second], split_axis))
+
+    def gather(self, shard, split_axis):
+        found = self.steps(shard)
+        return found + [self.last(found[-2][1], found[-1][1], split_axis)]
 
 
 def step_of(found, step):
@@ -256,23 +260,28 @@
     local_heads = head_share // HEAD
 
     qkv_found = ring.gather(qkv_weight.reshape(qkv_weight.shape[0], -1), 1)
-    out_found = ring.gather(out_weight.T, 1)
-    up_found = ring.gather(up_weight, 1)
+    up_found = ring.steps(up_weight)
     down_found = ring.gather(down_weight.T, 1)
     first_steps = step_of(up_found, 1) + step_of(down_found, 1)
     second_steps = step_of(up_found, 2) + step_of(down_found, 2)
-    merge_full = lax.all_gather(after(merge_weight, *second_steps), "gy", axis=0, tiled=True)
+    out_found = ring.gather(after(out_weight.T, *first_steps), 1)
+    merge_full = lax.all_gather(after(merge_weight, *first_steps), "gy", axis=0, tiled=True)
 
     stream_full = gather_features(patches, gx)
     normed = layer_norm(stream_full.astype(jnp.float32)).astype(jnp.bfloat16)
     projected = sum_chunks(chunked(normed, gy), qkv_found)
     projected = after(projected.astype(jnp.bfloat16), *first_steps).reshape(tok_rows, 3, local_heads, HEAD)
     mixed = attend(projected, segment_ids).reshape(tok_rows, head_share)
+    mixed = after(mixed, *second_steps)
     head_partial = place_columns(mixed, out_found, gy)
     stream_full = add_sum(head_partial, stream_full, gx)
-    stream_full = after(stream_full, *second_steps)
     normed_two = layer_norm(stream_full.astype(jnp.float32)).astype(jnp.bfloat16)
-    hidden = sum_chunks(chunked(normed_two, gy), up_found)
+    left = chunked(normed_two, gy)
+    hidden = sum_chunks(left, up_found[:-2])
+    cw, ccw, hidden = lax.optimization_barrier((up_found[-2][1], up_found[-1][1], hidden))
+    ends = [(up_found[-2][0], cw), (up_found[-1][0], ccw), ring.last(cw, ccw, 1)]
+    for index, shard in ends:
+        hidden = add_chunk(left, hidden, index, shard)
     hidden = jax.nn.gelu(hidden, approximate=False).astype(jnp.bfloat16)
     unit_partial = place_columns(hidden, down_found, gy)
     final_full = add_sum(unit_partial, stream_full, gx)

time: 435 us -> 494 us (1.14)
  starting transfers between devices: 54.4 us -> 87.2 us
  waiting for transfers between devices: 214 us -> 244 us
    ppermute x32, waiting for transfers between devices: 139 us -> 193 us  [the longest x12 79.4 us: steps(): ccw = lax.ppermute(ccw, 'gy', self.left)]
    ppermute x32, starting transfers between devices: 47.9 us -> 81.9 us  [the longest x12 50.3 us: steps(): ccw = lax.ppermute(ccw, 'gy', self.left)]
    all_gather x1, waiting for transfers between devices: 26.1 us -> 0.01 us  [per_device(): lax.all_gather(after(merge_weight, *first_steps), 'gy', axis=0, tiled=True)]
    dot_general x16, matrix products: 48.7 us -> 39.5 us  [add_chunk(): term = jnp.dot(pick(left, index), shard, preferred_element_type=jnp.float32)]
    unnamed x93 -> x33, local copies, waits for them, and re-layouts: 13.3 us -> 12.6 us
  transfers between devices with their start and end apart: 41 -> 41, of which waited for: 20 -> 21; matrix products, arithmetic and copies ran while one was open for 28% -> 23% of each run, Pallas kernels for 0% -> 0%
where the time goes in v4:
time: 494 us; the launch traced here: 485 us
  waiting for transfers between devices  244 us (49%)
  starting transfers between devices  87.2 us (18%)
  matrix products  79.3 us (16%)
  local copies, waits for them, and re-layouts  35 us (7%)
  between operations  15.2 us (3%)
  other arithmetic  12.2 us (2%)
  Pallas kernels  11.6 us (2%)
    ppermute x12, waiting for transfers between devices, steps(): ccw = lax.ppermute(ccw, 'gy', self.left)  79.4 us
    ppermute x12, waiting for transfers between devices, steps(): cw = lax.ppermute(cw, 'gy', self.right)  76.9 us
    ppermute x12, starting transfers between devices, steps(): ccw = lax.ppermute(ccw, 'gy', self.left)  50.3 us
    dot_general x16, matrix products, add_chunk(): term = jnp.dot(pick(left, index), shard, preferred_element_type=jnp.float32)  39.5 us
    ppermute x2, waiting for transfers between devices, add_sum(): total = total + lax.ppermute(sent, 'gx', x_shift(gx, k)).astype(jnp.float32)  37.8 us
    ppermute x4, waiting for transfers between devices, last(): first = lax.ppermute(first, 'gy', self.right)  37 us
    dot_general x16, matrix products, place_columns(): lax.dot_general(left, shard, (((1,), (1,)), ((), ())), preferred_element_...  30.2 us
    ppermute x12, starting transfers between devices, steps(): cw = lax.ppermute(cw, 'gy', self.right)  16 us
  transfers between devices with their start and end apart: 41, of which 21 were waited for; matrix products, arithmetic and copies ran while one was open for 23% of the time, Pallas kernels for 0%

profile of v4, /device:TPU:0, one launch (start us, length us, event | category | flops | bytes accessed | tf_op | source)
XLA Modules:
  0.0 484.7 jit_solution(3106829053688538692)
XLA Ops:
  8.9 3.1 collective-permute-start.2
  13.4 1.6 collective-permute-start.12
  15.9 7.6 %collective-permute-done = bf16[512,416]{0,1:T(8,128)(2,1)} collective-permute-done((bf16[512,416]{0,1:T(8,128)(2,1)}, bf16[512,416]{0,1:T(8,128)(2,1)}, u32[]{:S(2)}, u32[]{:S(2)}) %collective-permute-start) | collective-permute-done | bytes 426016 | tf_op jit(solution)/shard_map/ppermute | solution.py:129
  23.5 1.6 collective-permute-start.10
  25.9 1.8 collective-permute-start.11
  29.8 18.8 %collective-permute-done.3 = bf16[208,1248]{1,0:T(8,128)(2,1)} collective-permute-done((bf16[208,1248]{1,0:T(8,128)(2,1)S(1)}, bf16[208,1248]{1,0:T(8,128)(2,1)}, u32[]{:S(2)}, u32[]{:S(2)}) %collective-permute-start.3) | collective-permute-done | bytes 519200 | tf_op jit(solution)/shard_map/ppermute | solution.py:58
  49.1 1.6 collective-permute-start.4
  50.7 10.7 %collective-permute-done.10 = bf16[208,2048]{1,0:T(8,128)(2,1)S(1)} collective-permute-done((bf16[208,2048]{1,0:T(8,128)(2,1)}, bf16[208,2048]{1,0:T(8,128)(2,1)S(1)}, u32[]{:S(2)}, u32[]{:S(2)}) %collective-permute-start.10) | collective-permute-done | bytes 852000 | tf_op jit(solution)/shard_map/ppermute | solution.py:57
  61.3 5.6 %collective-permute-done.11 = bf16[208,2048]{1,0:T(8,128)(2,1)} collective-permute-done((bf16[208,2048]{1,0:T(8,128)(2,1)}, bf16[208,2048]{1,0:T(8,128)(2,1)}, u32[]{:S(2)}, u32[]{:S(2)}) %collective-permute-start.11) | collective-permute-done | bytes 852000 | tf_op jit(solution)/shard_map/ppermute | solution.py:58
  66.9 1.6 collective-permute-start.18
  70.3 6.3 %collective-permute-done.18 = bf16[208,416]{0,1:T(8,128)(2,1)} collective-permute-done((bf16[208,416]{0,1:T(8,128)(2,1)S(1)}, bf16[208,416]{0,1:T(8,128)(2,1)}, u32[]{:S(2)}, u32[]{:S(2)}) %collective-permute-start.18) | collective-permute-done | bytes 173088 | tf_op jit(solution)/shard_map/ppermute | solution.py:57
  76.6 1.8 collective-permute-start.20
  78.4 2.4 collective-permute-done.19
  81.5 1.6 collective-permute-start.16
  85.7 3.6 collective-permute-done.21
  96.4 2.2 convolution_add_fusion.2
  98.6 2.2 fusion.82
  100.8 2.4 fusion.12
  103.2 40.8 %collective-permute-done.22 = bf16[208,416]{0,1:T(8,128)(2,1)S(1)} collective-permute-done((bf16[208,416]{0,1:T(8,128)(2,1)}, bf16[208,416]{0,1:T(8,128)(2,1)S(1)}, u32[]{:S(2)}, u32[]{:S(2)}) %collective-permute-start.22) | collective-permute-done | bytes 173088 | tf_op jit(solution)/shard_map/ppermute | solution.py:57
  144.0 27.6 %collective-permute-start.17 = (bf16[208,2048]{1,0:T(8,128)(2,1)}, bf16[208,2048]{1,0:T(8,128)(2,1)}, u32[]{:S(2)}, u32[]{:S(2)}) collective-permute-start(bf16[208,2048]{1,0:T(8,128)(2,1)} %collective-permute-done.13), channel_id=1, source_target_pairs={{0,1},{2,0},{4,2},{6,4},{7,6},{5,7},{3,5},{1,3},{8,9},{10,8},{12,1... | collective-permute-start | bytes 2555912 | tf_op jit(solution)/shard_map/ppermute | solution.py:58
  171.8 4.2 collective-permute-start.8
  177.4 34.7 %collective-permute-done.8 = bf16[208,624]{1,0:T(8,128)(2,1)S(1)} collective-permute-done((bf16[208,624]{1,0:T(8,128)(2,1)S(1)}, bf16[208,624]{1,0:T(8,128)(2,1)S(1)}, u32[]{:S(2)}, u32[]{:S(2)}) %collective-permute-start.8) | collective-permute-done | bytes 259616 | tf_op jit(solution)/shard_map/ppermute | solution.py:67
  212.1 13.8 %collective-permute-start.15 = (bf16[208,2048]{1,0:T(8,128)(2,1)}, bf16[208,2048]{1,0:T(8,128)(2,1)}, u32[]{:S(2)}, u32[]{:S(2)}) collective-permute-start(bf16[208,2048]{1,0:T(8,128)(2,1)} %collective-permute-done.11), channel_id=1, source_target_pairs={{0,1},{2,0},{4,2},{6,4},{7,6},{5,7},{3,5},{1,3},{8,9},{10,8},{12,1... | collective-permute-start | bytes 2555912 | tf_op jit(solution)/shard_map/ppermute | solution.py:58
  225.9 6.9 %collective-permute-start.24 = (bf16[208,208]{0,1:T(8,128)(2,1)S(1)}, bf16[208,208]{0,1:T(8,128)(2,1)S(1)}, u32[]{:S(2)}, u32[]{:S(2)}) collective-permute-start(bf16[208,208]{0,1:T(8,128)(2,1)S(1)} %slice.123), channel_id=1, source_target_pairs={{0,2},{2,4},{4,6},{6,7},{7,5},{5,3},{3,1},{1,0},{8,10},{10,12},{12... | collective-permute-start | bytes 259592 | tf_op jit(solution)/shard_map/ppermute | solution.py:67
  236.2 2.1 fusion.130
  239.1 48.9 %collective-permute-done.15 = bf16[208,2048]{1,0:T(8,128)(2,1)} collective-permute-done((bf16[208,2048]{1,0:T(8,128)(2,1)}, bf16[208,2048]{1,0:T(8,128)(2,1)}, u32[]{:S(2)}, u32[]{:S(2)}) %collective-permute-start.15) | collective-permute-done | bytes 852000 | tf_op jit(solution)/shard_map/ppermute | solution.py:58
  289.4 1.9 fusion.31
  291.3 1.9 fusion.30
  293.2 1.9 fusion.29
  295.1 1.9 fusion.28
  300.4 1.7 copy.74
  302.8 3.2 collective-permute-done.26
  306.0 1.6 add_convert_fusion.3
  307.6 1.8 collective-permute-start.27
  310.2 18.5 %collective-permute-done.27 = bf16[256,1664]{1,0:T(8,128)(2,1)S(1)} collective-permute-done((bf16[256,1664]{1,0:T(8,128)(2,1)S(1)}, bf16[256,1664]{1,0:T(8,128)(2,1)S(1)}, u32[]{:S(2)}, u32[]{:S(2)}) %collective-permute-start.27) | collective-permute-done | bytes 852000 | tf_op jit(solution)/shard_map/ppermute | solution.py:147
  329.1 2.0 collective-permute-start.30
  331.2 1.9 collective-permute-start.34
  337.1 2.6 fusion.72
  341.1 2.6 fusion.70
  343.7 3.0 add_add_fusion.1
  346.7 4.5 collective-permute-done.29
  353.4 2.1 collective-permute-start.32
  355.5 13.9 %collective-permute-done.33 = bf16[208,2048]{1,0:T(8,128)(2,1)} collective-permute-done((bf16[208,2048]{1,0:T(8,128)(2,1)}, bf16[208,2048]{1,0:T(8,128)(2,1)}, u32[]{:S(2)}, u32[]{:S(2)}) %collective-permute-start.33) | collective-permute-done | bytes 852000 | tf_op jit(solution)/shard_map/ppermute | solution.py:57
  371.6 2.0 collective-permute-start.36
  373.6 2.5 fusion.64
  376.2 2.3 collective-permute-done.31
  379.9 11.7 %fusion.3 = bf16[512,2048]{1,0:T(8,128)(2,1)S(1)} fusion(f32[512,2048]{1,0:T(8,128)S(1)} %fusion.42, f32[512,2048]{1,0:T(8,128)S(1)} %add_add_fusion.1, f32[512,2048]{1,0:T(8,128)S(1)} %fusion.64, bf16[208,2048]{1,0:T(8,128)(2,1)} %collective-permute-done.30, bf16[512,8,208]{0,2,1:T(8,128)(2,1)S(1)} %multiply_convert_fusion, u32[]{:T(128)} %bitcast.20), kind=kOutput, calls=%fused_computation.7 | convolution fusion | flops 507510784 | bytes 15745028 | tf_op jit(solution)/shard_map/dot_general | solution.py:93
  394.3 2.6 fusion.39
  396.9 2.6 fusion.38
  399.5 2.7 fusion.37
  402.2 2.6 fusion.36
  404.8 2.6 fusion.35
  407.5 2.6 fusion.34
  411.7 1.6 constant_dynamic-slice_fusion.1
  413.3 2.7 copy.76
  416.0 1.9 copy.75
  417.9 2.0 collective-permute-done.37
  419.9 2.1 add_convert_fusion.1
  422.0 1.8 collective-permute-start.38
  423.8 19.3 %collective-permute-done.38 = bf16[256,1664]{1,0:T(8,128)(2,1)S(1)} collective-permute-done((bf16[256,1664]{1,0:T(8,128)(2,1)S(1)}, bf16[256,1664]{1,0:T(8,128)(2,1)S(1)}, u32[]{:S(2)}, u32[]{:S(2)}) %collective-permute-start.38) | collective-permute-done | bytes 852000 | tf_op jit(solution)/shard_map/ppermute | solution.py:147
  446.7 3.1 gather_fusion
  449.9 3.0 gather.7
  453.6 8.4 %fusion.128 = (f32[]{:T(128)}, bf16[128,1024]{1,0:T(8,128)(2,1)}) fusion(bf16[6656,1024]{1,0:T(8,128)(2,1)} %all-gather.2.cloned.1.call-done, pred[128,6656]{1,0:T(8,128)(4,1)} %bitcast.237, bf16[128,6656]{1,0:T(8,128)(2,1)S(1)} %gather.7), kind=kOutput, calls=%fused_computation.209 | convolution fusion | flops 1745944576 | bytes 16449540 | tf_op jit(solution)/shard_map/dot_general | solution.py:301
  463.4 11.6 %scalar_sums.1 = f32[8,128]{1,0:T(8,128)} custom-call(f32[8,128]{1,0:T(8,128)} %copy-done.9), custom_call_target="tpu_custom_call" | custom-call | tf_op jit(solution)/shard_map/scalar_sums/pallas_call | solution.py:212
  (145 shorter events, 55.3 us)
Async XLA Ops:
  7.2 59.7 %copy-start.6 = (bf16[416,208]{1,0:T(8,128)(2,1)S(1)}, bf16[416,208]{1,0:T(8,128)(2,1)}, u32[]{:S(2)}) copy-start(bf16[416,208]{1,0:T(8,128)(2,1)} %param.19) | copy-start | bytes 519172
  7.2 74.1 %copy-start.8 = (s32[512]{0:T(512)S(1)}, s32[512]{0:T(512)}, u32[]{:S(2)}) copy-start(s32[512]{0:T(512)} %param.15) | copy-start | bytes 6148
  7.2 446.4 %all-gather.2.cloned.1.call-start = ((), (), s32[]{:S(2)}) async-start(), calls=%async_computation | async-start | bytes 15335424 | tf_op jit(solution)/shard_map/all_gather | solution.py:268
  8.9 16.2 %collective-permute-start.2 = (bf16[208,1248]{1,0:T(8,128)(2,1)S(1)}, bf16[208,1248]{1,0:T(8,128)(2,1)S(1)}, u32[]{:S(2)}, u32[]{:S(2)}) collective-permute-start(bf16[208,1248]{1,0:T(8,128)(2,1)S(1)} %copy.61), channel_id=1, source_target_pairs={{0,2},{2,4},{4,6},{6,7},{7,5},{5,3},{3,1},{1,0},{8,10},{10,12},{12... | collective-permute-start | bytes 1557512 | tf_op jit(solution)/shard_map/ppermute | solution.py:57
  11.9 11.6 %collective-permute-start = (bf16[512,416]{0,1:T(8,128)(2,1)}, bf16[512,416]{0,1:T(8,128)(2,1)}, u32[]{:S(2)}, u32[]{:S(2)}) collective-permute-start(bf16[512,416]{0,1:T(8,128)(2,1)} %param.14), channel_id=1, source_target_pairs={{0,16},{8,24},{16,0},{24,8},{1,17},{9,25},{17,1},{25,9},{2,18},{10... | collective-permute-start | bytes 1277960 | tf_op jit(solution)/shard_map/ppermute | solution.py:129
  13.4 35.2 %collective-permute-start.12 = (bf16[208,2048]{1,0:T(8,128)(2,1)}, bf16[208,2048]{1,0:T(8,128)(2,1)}, u32[]{:S(2)}, u32[]{:S(2)}) collective-permute-start(bf16[208,2048]{1,0:T(8,128)(2,1)} %bitcast.243), channel_id=1, source_target_pairs={{0,2},{2,4},{4,6},{6,7},{7,5},{5,3},{3,1},{1,0},{8,10},{10,12},{12... | collective-permute-start | bytes 2555912 | tf_op jit(solution)/shard_map/ppermute | solution.py:57
  15.0 34.1 %collective-permute-start.13 = (bf16[208,2048]{1,0:T(8,128)(2,1)}, bf16[208,2048]{1,0:T(8,128)(2,1)}, u32[]{:S(2)}, u32[]{:S(2)}) collective-permute-start(bf16[208,2048]{1,0:T(8,128)(2,1)} %bitcast.244), channel_id=1, source_target_pairs={{0,1},{2,0},{4,2},{6,4},{7,6},{5,7},{3,5},{1,3},{8,9},{10,8},{12,1... | collective-permute-start | bytes 2555912 | tf_op jit(solution)/shard_map/ppermute | solution.py:58
  15.5 33.2 %collective-permute-start.3 = (bf16[208,1248]{1,0:T(8,128)(2,1)S(1)}, bf16[208,1248]{1,0:T(8,128)(2,1)}, u32[]{:S(2)}, u32[]{:S(2)}) collective-permute-start(bf16[208,1248]{1,0:T(8,128)(2,1)S(1)} %copy.61), channel_id=1, source_target_pairs={{0,1},{2,0},{4,2},{6,4},{7,6},{5,7},{3,5},{1,3},{8,9},{10,8},{12,1... | collective-permute-start | bytes 1557512 | tf_op jit(solution)/shard_map/ppermute | solution.py:58
  23.5 37.8 %collective-permute-start.10 = (bf16[208,2048]{1,0:T(8,128)(2,1)}, bf16[208,2048]{1,0:T(8,128)(2,1)S(1)}, u32[]{:S(2)}, u32[]{:S(2)}) collective-permute-start(bf16[208,2048]{1,0:T(8,128)(2,1)} %param.20), channel_id=1, source_target_pairs={{0,2},{2,4},{4,6},{6,7},{7,5},{5,3},{3,1},{1,0},{8,10},{10,12},{12... | collective-permute-start | bytes 2555912 | tf_op jit(solution)/shard_map/ppermute | solution.py:57
  25.1 0.8 copy-start.4
  25.9 41.0 %collective-permute-start.11 = (bf16[208,2048]{1,0:T(8,128)(2,1)}, bf16[208,2048]{1,0:T(8,128)(2,1)}, u32[]{:S(2)}, u32[]{:S(2)}) collective-permute-start(bf16[208,2048]{1,0:T(8,128)(2,1)} %param.20), channel_id=1, source_target_pairs={{0,1},{2,0},{4,2},{6,4},{7,6},{5,7},{3,5},{1,3},{8,9},{10,8},{12,1... | collective-permute-start | bytes 2555912 | tf_op jit(solution)/shard_map/ppermute | solution.py:58
  48.6 42.3 %collective-permute-start.1 = (bf16[2,512,416]{1,2,0:T(8,128)(2,1)S(1)}, bf16[2,512,416]{1,2,0:T(8,128)(2,1)S(1)}, u32[]{:S(2)}, u32[]{:S(2)}) collective-permute-start(bf16[2,512,416]{1,2,0:T(8,128)(2,1)S(1)} %bitcast_dynamic-update-slice_fusion), channel_id=1, source_target_pairs={{0,8},{8,0},{16,24},{24,16},{1,9},{9,1},{17,25},{25,17},{2,10},{10... | collective-permute-start | bytes 2555912 | tf_op jit(solution)/shard_map/ppermute | solution.py:131
  48.6 32.9 %collective-permute-start.5 = (bf16[208,1248]{1,0:T(8,128)(2,1)}, bf16[208,1248]{1,0:T(8,128)(2,1)}, u32[]{:S(2)}, u32[]{:S(2)}) collective-permute-start(bf16[208,1248]{1,0:T(8,128)(2,1)} %collective-permute-done.3), channel_id=1, source_target_pairs={{0,1},{2,0},{4,2},{6,4},{7,6},{5,7},{3,5},{1,3},{8,9},{10,8},{12,1... | collective-permute-start | bytes 1557512 | tf_op jit(solution)/shard_map/ppermute | solution.py:58
  49.1 34.1 %collective-permute-start.4 = (bf16[208,1248]{1,0:T(8,128)(2,1)}, bf16[208,1248]{1,0:T(8,128)(2,1)}, u32[]{:S(2)}, u32[]{:S(2)}) collective-permute-start(bf16[208,1248]{1,0:T(8,128)(2,1)} %copy-done.4), channel_id=1, source_target_pairs={{0,2},{2,4},{4,6},{6,7},{7,5},{5,3},{3,1},{1,0},{8,10},{10,12},{12... | collective-permute-start | bytes 1557512 | tf_op jit(solution)/shard_map/ppermute | solution.py:57
  61.3 110.3 %copy-start.2 = (bf16[208,2048]{1,0:T(8,128)(2,1)}, bf16[208,2048]{1,0:T(8,128)(2,1)S(1)}, u32[]{:S(2)}) copy-start(bf16[208,2048]{1,0:T(8,128)(2,1)S(1)} %collective-permute-done.10) | copy-start | bytes 2555908
  66.9 9.7 %collective-permute-start.18 = (bf16[208,416]{0,1:T(8,128)(2,1)S(1)}, bf16[208,416]{0,1:T(8,128)(2,1)}, u32[]{:S(2)}, u32[]{:S(2)}) collective-permute-start(bf16[208,416]{0,1:T(8,128)(2,1)S(1)} %bitcast.238), channel_id=1, source_target_pairs={{0,2},{2,4},{4,6},{6,7},{7,5},{5,3},{3,1},{1,0},{8,10},{10,12},{12... | collective-permute-start | bytes 519176 | tf_op jit(solution)/shard_map/ppermute | solution.py:57
  68.5 12.4 %collective-permute-start.19 = (bf16[208,416]{0,1:T(8,128)(2,1)S(1)}, bf16[208,416]{0,1:T(8,128)(2,1)}, u32[]{:S(2)}, u32[]{:S(2)}) collective-permute-start(bf16[208,416]{0,1:T(8,128)(2,1)S(1)} %bitcast.239), channel_id=1, source_target_pairs={{0,1},{2,0},{4,2},{6,4},{7,6},{5,7},{3,5},{1,3},{8,9},{10,8},{12,1... | collective-permute-start | bytes 519176 | tf_op jit(solution)/shard_map/ppermute | solution.py:58
  76.6 7.7 %collective-permute-start.20 = (bf16[208,416]{0,1:T(8,128)(2,1)}, bf16[208,416]{0,1:T(8,128)(2,1)}, u32[]{:S(2)}, u32[]{:S(2)}) collective-permute-start(bf16[208,416]{0,1:T(8,128)(2,1)} %collective-permute-done.18), channel_id=1, source_target_pairs={{0,2},{2,4},{4,6},{6,7},{7,5},{5,3},{3,1},{1,0},{8,10},{10,12},{12... | collective-permute-start | bytes 519176 | tf_op jit(solution)/shard_map/ppermute | solution.py:57
  80.8 8.5 %collective-permute-start.21 = (bf16[208,416]{0,1:T(8,128)(2,1)}, bf16[208,416]{0,1:T(8,128)(2,1)}, u32[]{:S(2)}, u32[]{:S(2)}) collective-permute-start(bf16[208,416]{0,1:T(8,128)(2,1)} %collective-permute-done.19), channel_id=1, source_target_pairs={{0,1},{2,0},{4,2},{6,4},{7,6},{5,7},{3,5},{1,3},{8,9},{10,8},{12,1... | collective-permute-start | bytes 519176 | tf_op jit(solution)/shard_map/ppermute | solution.py:58
  81.5 157.3 %collective-permute-start.16 = (bf16[208,2048]{1,0:T(8,128)(2,1)}, bf16[208,2048]{1,0:T(8,128)(2,1)}, u32[]{:S(2)}, u32[]{:S(2)}) collective-permute-start(bf16[208,2048]{1,0:T(8,128)(2,1)} %collective-permute-done.12), channel_id=1, source_target_pairs={{0,2},{2,4},{4,6},{6,7},{7,5},{5,3},{3,1},{1,0},{8,10},{10,12},{12... | collective-permute-start | bytes 2555912 | tf_op jit(solution)/shard_map/ppermute | solution.py:57
  83.2 92.8 %collective-permute-start.7 = (bf16[208,1248]{1,0:T(8,128)(2,1)}, bf16[208,1248]{1,0:T(8,128)(2,1)S(1)}, u32[]{:S(2)}, u32[]{:S(2)}) collective-permute-start(bf16[208,1248]{1,0:T(8,128)(2,1)} %collective-permute-done.5), channel_id=1, source_target_pairs={{0,1},{2,0},{4,2},{6,4},{7,6},{5,7},{3,5},{1,3},{8,9},{10,8},{12,1... | collective-permute-start | bytes 1557512 | tf_op jit(solution)/shard_map/ppermute | solution.py:58
  84.3 87.4 %collective-permute-start.6 = (bf16[208,1248]{1,0:T(8,128)(2,1)}, bf16[208,1248]{1,0:T(8,128)(2,1)S(1)}, u32[]{:S(2)}, u32[]{:S(2)}) collective-permute-start(bf16[208,1248]{1,0:T(8,128)(2,1)} %collective-permute-done.4), channel_id=1, source_target_pairs={{0,2},{2,4},{4,6},{6,7},{7,5},{5,3},{3,1},{1,0},{8,10},{10,12},{12... | collective-permute-start | bytes 1557512 | tf_op jit(solution)/shard_map/ppermute | solution.py:57
  89.3 54.7 %collective-permute-start.22 = (bf16[208,416]{0,1:T(8,128)(2,1)}, bf16[208,416]{0,1:T(8,128)(2,1)S(1)}, u32[]{:S(2)}, u32[]{:S(2)}) collective-permute-start(bf16[208,416]{0,1:T(8,128)(2,1)} %collective-permute-done.20), channel_id=1, source_target_pairs={{0,2},{2,4},{4,6},{6,7},{7,5},{5,3},{3,1},{1,0},{8,10},{10,12},{12... | collective-permute-start | bytes 519176 | tf_op jit(solution)/shard_map/ppermute | solution.py:57
  90.9 80.7 %collective-permute-start.23 = (bf16[208,416]{0,1:T(8,128)(2,1)}, bf16[208,416]{0,1:T(8,128)(2,1)S(1)}, u32[]{:S(2)}, u32[]{:S(2)}) collective-permute-start(bf16[208,416]{0,1:T(8,128)(2,1)} %collective-permute-done.21), channel_id=1, source_target_pairs={{0,1},{2,0},{4,2},{6,4},{7,6},{5,7},{3,5},{1,3},{8,9},{10,8},{12,1... | collective-permute-start | bytes 519176 | tf_op jit(solution)/shard_map/ppermute | solution.py:58
  93.5 1.6 copy-start.5
  144.0 95.1 %collective-permute-start.17 = (bf16[208,2048]{1,0:T(8,128)(2,1)}, bf16[208,2048]{1,0:T(8,128)(2,1)}, u32[]{:S(2)}, u32[]{:S(2)}) collective-permute-start(bf16[208,2048]{1,0:T(8,128)(2,1)} %collective-permute-done.13), channel_id=1, source_target_pairs={{0,1},{2,0},{4,2},{6,4},{7,6},{5,7},{3,5},{1,3},{8,9},{10,8},{12,1... | collective-permute-start | bytes 2555912 | tf_op jit(solution)/shard_map/ppermute | solution.py:58
  171.6 67.5 %collective-permute-start.14 = (bf16[208,2048]{1,0:T(8,128)(2,1)S(1)}, bf16[208,2048]{1,0:T(8,128)(2,1)}, u32[]{:S(2)}, u32[]{:S(2)}) collective-permute-start(bf16[208,2048]{1,0:T(8,128)(2,1)S(1)} %collective-permute-done.10), channel_id=1, source_target_pairs={{0,2},{2,4},{4,6},{6,7},{7,5},{5,3},{3,1},{1,0},{8,10},{10,12},{12... | collective-permute-start | bytes 2555912 | tf_op jit(solution)/shard_map/ppermute | solution.py:57
  171.8 40.3 %collective-permute-start.8 = (bf16[208,624]{1,0:T(8,128)(2,1)S(1)}, bf16[208,624]{1,0:T(8,128)(2,1)S(1)}, u32[]{:S(2)}, u32[]{:S(2)}) collective-permute-start(bf16[208,624]{1,0:T(8,128)(2,1)S(1)} %slice.118), channel_id=1, source_target_pairs={{0,2},{2,4},{4,6},{6,7},{7,5},{5,3},{3,1},{1,0},{8,10},{10,12},{12... | collective-permute-start | bytes 778760 | tf_op jit(solution)/shard_map/ppermute | solution.py:67
  176.1 49.8 %collective-permute-start.9 = (bf16[208,624]{1,0:T(8,128)(2,1)S(1)}, bf16[208,624]{1,0:T(8,128)(2,1)S(1)}, u32[]{:S(2)}, u32[]{:S(2)}) collective-permute-start(bf16[208,624]{1,0:T(8,128)(2,1)S(1)} %slice.119), channel_id=1, source_target_pairs={{0,1},{2,0},{4,2},{6,4},{7,6},{5,7},{3,5},{1,3},{8,9},{10,8},{12,1... | collective-permute-start | bytes 778760 | tf_op jit(solution)/shard_map/ppermute | solution.py:68
  212.1 75.9 %collective-permute-start.15 = (bf16[208,2048]{1,0:T(8,128)(2,1)}, bf16[208,2048]{1,0:T(8,128)(2,1)}, u32[]{:S(2)}, u32[]{:S(2)}) collective-permute-start(bf16[208,2048]{1,0:T(8,128)(2,1)} %collective-permute-done.11), channel_id=1, source_target_pairs={{0,1},{2,0},{4,2},{6,4},{7,6},{5,7},{3,5},{1,3},{8,9},{10,8},{12,1... | collective-permute-start | bytes 2555912 | tf_op jit(solution)/shard_map/ppermute | solution.py:58
  225.9 73.0 %collective-permute-start.24 = (bf16[208,208]{0,1:T(8,128)(2,1)S(1)}, bf16[208,208]{0,1:T(8,128)(2,1)S(1)}, u32[]{:S(2)}, u32[]{:S(2)}) collective-permute-start(bf16[208,208]{0,1:T(8,128)(2,1)S(1)} %slice.123), channel_id=1, source_target_pairs={{0,2},{2,4},{4,6},{6,7},{7,5},{5,3},{3,1},{1,0},{8,10},{10,12},{12... | collective-permute-start | bytes 259592 | tf_op jit(solution)/shard_map/ppermute | solution.py:67
  238.8 49.6 %copy-start.7 = (bf16[416,208]{1,0:T(8,128)(2,1)S(1)}, bf16[416,208]{1,0:T(8,128)(2,1)}, u32[]{:S(2)}) copy-start(bf16[416,208]{1,0:T(8,128)(2,1)} %param.19) | copy-start | bytes 519172
  238.8 60.1 %collective-permute-start.25 = (bf16[208,208]{0,1:T(8,128)(2,1)S(1)}, bf16[208,208]{0,1:T(8,128)(2,1)S(1)}, u32[]{:S(2)}, u32[]{:S(2)}) collective-permute-start(bf16[208,208]{0,1:T(8,128)(2,1)S(1)} %slice.124), channel_id=1, source_target_pairs={{0,1},{2,0},{4,2},{6,4},{7,6},{5,7},{3,5},{1,3},{8,9},{10,8},{12,1... | collective-permute-start | bytes 259592 | tf_op jit(solution)/shard_map/ppermute | solution.py:68
  302.0 3.9 collective-permute-start.26
  302.8 6.6 %copy-start = (bf16[2,2,512,416]{2,3,1,0:T(8,128)(2,1)S(1)}, bf16[2,2,512,416]{2,3,1,0:T(8,128)(2,1)}, u32[]{:S(2)}) copy-start(bf16[2,2,512,416]{2,3,1,0:T(8,128)(2,1)} %get-tuple-element.55) | copy-start | bytes 5111812
  307.6 21.1 %collective-permute-start.27 = (bf16[256,1664]{1,0:T(8,128)(2,1)S(1)}, bf16[256,1664]{1,0:T(8,128)(2,1)S(1)}, u32[]{:S(2)}, u32[]{:S(2)}) collective-permute-start(bf16[256,1664]{1,0:T(8,128)(2,1)S(1)} %add_convert_fusion.3), channel_id=1, source_target_pairs={{0,16},{8,24},{16,0},{24,8},{1,17},{9,25},{17,1},{25,9},{2,18},{10... | collective-permute-start | bytes 2555912 | tf_op jit(solution)/shard_map/ppermute | solution.py:147
  329.0 4.2 collective-permute-start.28
  329.1 22.1 %collective-permute-start.29 = (bf16[208,2048]{1,0:T(8,128)(2,1)}, bf16[208,2048]{1,0:T(8,128)(2,1)}, u32[]{:S(2)}, u32[]{:S(2)}) collective-permute-start(bf16[208,2048]{1,0:T(8,128)(2,1)} %collective-permute-done.14), channel_id=1, source_target_pairs={{0,2},{2,4},{4,6},{6,7},{7,5},{5,3},{3,1},{1,0},{8,10},{10,12},{12... | collective-permute-start | bytes 2555912 | tf_op jit(solution)/shard_map/ppermute | solution.py:57
  329.1 22.1 %collective-permute-start.30 = (bf16[208,2048]{1,0:T(8,128)(2,1)}, bf16[208,2048]{1,0:T(8,128)(2,1)}, u32[]{:S(2)}, u32[]{:S(2)}) collective-permute-start(bf16[208,2048]{1,0:T(8,128)(2,1)} %collective-permute-done.15), channel_id=1, source_target_pairs={{0,1},{2,0},{4,2},{6,4},{7,6},{5,7},{3,5},{1,3},{8,9},{10,8},{12,1... | collective-permute-start | bytes 2555912 | tf_op jit(solution)/shard_map/ppermute | solution.py:58
  331.1 38.3 %collective-permute-start.33 = (bf16[208,2048]{1,0:T(8,128)(2,1)}, bf16[208,2048]{1,0:T(8,128)(2,1)}, u32[]{:S(2)}, u32[]{:S(2)}) collective-permute-start(bf16[208,2048]{1,0:T(8,128)(2,1)} %collective-permute-done.16), channel_id=1, source_target_pairs={{0,2},{2,4},{4,6},{6,7},{7,5},{5,3},{3,1},{1,0},{8,10},{10,12},{12... | collective-permute-start | bytes 2555912 | tf_op jit(solution)/shard_map/ppermute | solution.py:57
  331.2 39.4 %collective-permute-start.34 = (bf16[208,2048]{1,0:T(8,128)(2,1)}, bf16[208,2048]{1,0:T(8,128)(2,1)}, u32[]{:S(2)}, u32[]{:S(2)}) collective-permute-start(bf16[208,2048]{1,0:T(8,128)(2,1)} %collective-permute-done.17), channel_id=1, source_target_pairs={{0,1},{2,0},{4,2},{6,4},{7,6},{5,7},{3,5},{1,3},{8,9},{10,8},{12,1... | collective-permute-start | bytes 2555912 | tf_op jit(solution)/shard_map/ppermute | solution.py:58
  334.5 1.2 copy-start.1
  337.1 2.6 copy-start.3
  352.3 26.1 %collective-permute-start.31 = (bf16[208,1024]{1,0:T(8,128)(2,1)S(1)}, bf16[208,1024]{1,0:T(8,128)(2,1)S(1)}, u32[]{:S(2)}, u32[]{:S(2)}) collective-permute-start(bf16[208,1024]{1,0:T(8,128)(2,1)S(1)} %slice.110), channel_id=1, source_target_pairs={{0,2},{2,4},{4,6},{6,7},{7,5},{5,3},{3,1},{1,0},{8,10},{10,12},{12... | collective-permute-start | bytes 1277960 | tf_op jit(solution)/shard_map/ppermute | solution.py:67
  353.4 25.1 %collective-permute-start.32 = (bf16[208,1024]{1,0:T(8,128)(2,1)S(1)}, bf16[208,1024]{1,0:T(8,128)(2,1)S(1)}, u32[]{:S(2)}, u32[]{:S(2)}) collective-permute-start(bf16[208,1024]{1,0:T(8,128)(2,1)S(1)} %slice.111), channel_id=1, source_target_pairs={{0,1},{2,0},{4,2},{6,4},{7,6},{5,7},{3,5},{1,3},{8,9},{10,8},{12,1... | collective-permute-start | bytes 1277960 | tf_op jit(solution)/shard_map/ppermute | solution.py:68
  370.5 39.7 %collective-permute-start.35 = (bf16[208,1024]{1,0:T(8,128)(2,1)S(1)}, bf16[208,1024]{1,0:T(8,128)(2,1)S(1)}, u32[]{:S(2)}, u32[]{:S(2)}) collective-permute-start(bf16[208,1024]{1,0:T(8,128)(2,1)S(1)} %slice.125), channel_id=1, source_target_pairs={{0,2},{2,4},{4,6},{6,7},{7,5},{5,3},{3,1},{1,0},{8,10},{10,12},{12... | collective-permute-start | bytes 1277960 | tf_op jit(solution)/shard_map/ppermute | solution.py:67
  371.6 38.5 %collective-permute-start.36 = (bf16[208,1024]{1,0:T(8,128)(2,1)S(1)}, bf16[208,1024]{1,0:T(8,128)(2,1)S(1)}, u32[]{:S(2)}, u32[]{:S(2)}) collective-permute-start(bf16[208,1024]{1,0:T(8,128)(2,1)S(1)} %slice.126), channel_id=1, source_target_pairs={{0,1},{2,0},{4,2},{6,4},{7,6},{5,7},{3,5},{1,3},{8,9},{10,8},{12,1... | collective-permute-start | bytes 1277960 | tf_op jit(solution)/shard_map/ppermute | solution.py:68
  391.6 1.2 copy-start.11
  416.0 3.9 collective-permute-start.37
  417.9 26.2 %copy-start.10 = (s32[128,4]{0,1:T(4,128)S(1)}, s32[128,4]{0,1:T(4,128)}, u32[]{:S(2)}) copy-start(s32[128,4]{0,1:T(4,128)} %param.17) | copy-start | bytes 6148
  422.0 24.3 %copy-start.12 = (s32[32]{0:T(128)S(1)}, s32[32]{0:T(128)}, u32[]{:S(2)}) copy-start(s32[32]{0:T(128)} %param.16) | copy-start | bytes 388
  422.0 21.1 %collective-permute-start.38 = (bf16[256,1664]{1,0:T(8,128)(2,1)S(1)}, bf16[256,1664]{1,0:T(8,128)(2,1)S(1)}, u32[]{:S(2)}, u32[]{:S(2)}) collective-permute-start(bf16[256,1664]{1,0:T(8,128)(2,1)S(1)} %add_convert_fusion.1), channel_id=1, source_target_pairs={{0,16},{8,24},{16,0},{24,8},{1,17},{9,25},{17,1},{25,9},{2,18},{10... | collective-permute-start | bytes 2555912 | tf_op jit(solution)/shard_map/ppermute | solution.py:147
  444.0 2.4 collective-permute-start.39
  462.8 0.6 copy-start.9
Sparse Core Ops, SparseCore 0:
  81.7 234.0 all-gather.1
